TPU v7x, 512 devices: a whole 4x4x16 slice. The times are simulated.
512 devices in a mesh: dp: 8 (over x, core), expert: 64 (over y, z).
Axes of the slice: x: 4, y: 4, z: 16, core: 2. Of those that a mesh axis runs over, the one named last changes fastest.
Arguments:
- tokens: bfloat16 [65536, 2048], P(('dp', 'expert')), may hold values from -6 to 6
- out_grad: bfloat16 [65536, 2048], P(('dp', 'expert')), may hold values from -3 to 3
- expert_ids: int32 [65536, 1], P(('dp', 'expert')), may hold values from 0 to 63, as said below
- gates: float32 [65536, 1], P(('dp', 'expert')), may hold values from 0.1 to 1
- w_gate: bfloat16 [64, 2048, 384], P('expert', 'dp'), may hold values from -0.125 to 0.125
- w_up: bfloat16 [64, 2048, 384], P('expert', 'dp'), may hold values from -0.125 to 0.125
- w_down: bfloat16 [64, 384, 2048], P('expert', None, 'dp'), may hold values from -0.3125 to 0.3125
Outputs:
- input_grad: bfloat16 [65536, 2048], P(('dp', 'expert'))
- gate_grad: bfloat16 [64, 2048, 384], P('expert', 'dp')
- up_grad: bfloat16 [64, 2048, 384], P('expert', 'dp')
- down_grad: bfloat16 [64, 384, 2048], P('expert')
Inputs may be any that keep to these rules, and one draw needn't show every extreme that they name: `expert_ids`: among the rows of one device no expert is named more than 6 times; 4 experts, the same ones for every device, are named exactly 6 times by every device.
All inputs are finite; a program needn't handle non-finite values.
Results may differ from a plain program's by a relative error of at most 0.013.
Values may be sent and summed in bfloat16 or wider, within the bound.
A program may use at most 64 MiB of HBM per device.

v0:
```python
import jax
import jax.numpy as jnp
from jax import lax
from jax.sharding import PartitionSpec as P


def on_device(tokens, out_grad, expert_ids, gates, w_gate, w_up, w_down):
    expert_count = lax.axis_size("expert")
    tok_rows = tokens.shape[0]
    model_width = tokens.shape[1]
    per_token = expert_ids.shape[1]
    hidden = w_gate.shape[2]
    entries = tok_rows * per_token
    slot_depth = 3 * entries // expert_count
    slot_count = expert_count * slot_depth
    flat_ids = expert_ids.reshape(entries)
    onehot = (flat_ids[:, None] == jnp.arange(expert_count, dtype=jnp.int32)[None, :]).astype(
        jnp.int32
    )
    before = jnp.cumsum(onehot, axis=0) - onehot
    ranking = jnp.sum(before * onehot, axis=1)
    slot_of_entry = flat_ids * slot_depth + ranking
    source = (
        jnp.full((slot_count,), entries, jnp.int32)
        .at[slot_of_entry]
        .set(jnp.arange(entries, dtype=jnp.int32))
    )
    entry_scaled = (
        (gates[:, :, None] * out_grad.astype(jnp.float32)[:, None, :])
        .astype(jnp.bfloat16)
        .reshape(entries, model_width)
    )
    grad_table = jnp.concatenate([entry_scaled, jnp.zeros((1, model_width), jnp.bfloat16)], axis=0)
    input_table = jnp.concatenate([tokens, jnp.zeros((1, model_width), tokens.dtype)], axis=0)
    send_grads = grad_table[source].reshape(expert_count, slot_depth, model_width)
    send_inputs = input_table[source // per_token].reshape(expert_count, slot_depth, model_width)
    recv_inputs, recv_grads = (
        lax.all_to_all(send_inputs, "expert", split_axis=0, concat_axis=0, tiled=True),
        lax.all_to_all(send_grads, "expert", split_axis=0, concat_axis=0, tiled=True),
    )
    rows_in = recv_inputs.reshape(slot_count, model_width)
    grads_in = recv_grads.reshape(slot_count, model_width)
    local_joined = jnp.concatenate([w_gate[0], w_up[0]], axis=1)
    full_joined, full_down = (
        lax.all_gather(local_joined, "dp", axis=0, tiled=True),
        lax.all_gather(w_down[0], "dp", axis=1, tiled=True),
    )
    preact = jnp.dot(rows_in, full_joined, preferred_element_type=jnp.float32)
    hidden_grad = lax.dot_general(
        grads_in, full_down, (((1,), (1,)), ((), ())), preferred_element_type=jnp.float32
    )
    gate_pre = preact[:, :hidden]
    up_pre = preact[:, hidden:]
    sigmoid = jax.nn.sigmoid(gate_pre)
    silu_value = gate_pre * sigmoid
    activated = (silu_value * up_pre).astype(jnp.bfloat16)
    gate_side = (hidden_grad * up_pre * sigmoid * (1.0 + gate_pre * (1.0 - sigmoid))).astype(
        jnp.bfloat16
    )
    up_side = (hidden_grad * silu_value).astype(jnp.bfloat16)
    both_sides = jnp.concatenate([gate_side, up_side], axis=1)
    slot_grad = lax.dot_general(
        both_sides, full_joined, (((1,), (1,)), ((), ())), preferred_element_type=jnp.float32
    )
    slot_grad = slot_grad.astype(jnp.bfloat16).reshape(expert_count, slot_depth, model_width)
    returned = lax.all_to_all(slot_grad, "expert", split_axis=0, concat_axis=0, tiled=True).reshape(
        slot_count, model_width
    )
    picked = returned[slot_of_entry].astype(jnp.float32).reshape(tok_rows, per_token, model_width)
    input_grad = jnp.sum(picked, axis=1).astype(jnp.bfloat16)
    down_part = lax.dot_general(
        activated, grads_in, (((0,), (0,)), ((), ())), preferred_element_type=jnp.float32
    )
    down_grad = lax.psum(down_part.astype(jnp.bfloat16), "dp")[None]
    joined_grad = lax.psum_scatter(
        lax.dot_general(
            rows_in, both_sides, (((0,), (0,)), ((), ())), preferred_element_type=jnp.float32
        ).astype(jnp.bfloat16),
        "dp",
        scatter_dimension=0,
        tiled=True,
    )
    gate_grad = joined_grad[:, :hidden][None]
    up_grad = joined_grad[:, hidden:][None]
    return (input_grad, gate_grad, up_grad, down_grad)


def solution(mesh):
    in_specs = (
        P(("dp", "expert"), None),
        P(("dp", "expert"), None),
        P(("dp", "expert"), None),
        P(("dp", "expert"), None),
        P("expert", "dp", None),
        P("expert", "dp", None),
        P("expert", None, "dp"),
    )
    out_specs = (
        P(("dp", "expert"), None),
        P("expert", "dp", None),
        P("expert", "dp", None),
        P("expert", None, None),
    )
    return jax.shard_map(
        on_device, mesh=mesh, in_specs=in_specs, out_specs=out_specs, check_vma=False
    )
```

profile of v0, /device:TPU:1, one launch (start us, length us, event | category | flops | bytes accessed | tf_op | source)
XLA Modules:
  0.0 381.8 jit_solution(3051048810982180025)
XLA Ops:
  7.2 0.7 fusion.5
  7.9 0.2 reduce_window_sum.11
  8.1 0.8 select_reduce_fusion
  8.9 0.7 fusion.8
  9.6 1.0 scatter_custom_fusion
  10.6 1.1 concatenate.13
  11.7 2.5 gather_fusion.1
  14.1 1.6 reshape.40
  15.8 19.4 %all-to-all-start.1 = ((bf16[64,6,2048]{2,1,0:T(8,128)(2,1)}), bf16[64,6,2048]{2,1,0:T(8,128)(2,1)S(1)}, u32[]{:S(2)}, u32[]{:S(2)}) async-start(bf16[64,6,2048]{2,1,0:T(8,128)(2,1)} %reshape.40), calls=%async_computation.1 | async-start | bytes 4194304 | tf_op jit(solution)/shard_map/all_to_all | solution.py:38
  35.2 0.0 all-gather.4.cloned.1.call-start
  35.3 0.0 copy-done.2
  35.3 0.0 copy-done.3
  35.3 0.8 pad_maximum_fusion.1
  36.1 0.0 all-gather.4.cloned.1.call-update
  36.1 0.0 copy-done.1
  36.1 0.0 copy-done.4
  36.1 0.2 multiply_convert_fusion
  36.3 3.1 gather_fusion
  39.4 3.7 reshape.38
  43.1 86.9 %all-to-all-done.1 = bf16[64,6,2048]{2,1,0:T(8,128)(2,1)S(1)} async-done(((bf16[64,6,2048]{2,1,0:T(8,128)(2,1)}), bf16[64,6,2048]{2,1,0:T(8,128)(2,1)S(1)}, u32[]{:S(2)}, u32[]{:S(2)}) %all-to-all-start.1) | async-done | bytes 1572896 | tf_op jit(solution)/shard_map/all_to_all | solution.py:38
  130.0 11.1 %all-to-all-start = ((bf16[64,6,2048]{2,1,0:T(8,128)(2,1)}), bf16[64,6,2048]{2,1,0:T(8,128)(2,1)}, u32[]{:S(2)}, u32[]{:S(2)}) async-start(bf16[64,6,2048]{2,1,0:T(8,128)(2,1)} %reshape.38), calls=%async_computation | async-start | bytes 4194304 | tf_op jit(solution)/shard_map/all_to_all | solution.py:39
  141.2 0.0 all-gather.6.cloned.1.call-start
  141.2 0.7 all-gather.6.cloned.1.call-update
  141.9 0.2 reduce-scatter.2.cloned.1.call-start
  142.1 1.4 reshape.41
  143.6 92.5 %all-to-all-done = bf16[64,6,2048]{2,1,0:T(8,128)(2,1)} async-done(((bf16[64,6,2048]{2,1,0:T(8,128)(2,1)}), bf16[64,6,2048]{2,1,0:T(8,128)(2,1)}, u32[]{:S(2)}, u32[]{:S(2)}) %all-to-all-start) | async-done | bytes 1572896 | tf_op jit(solution)/shard_map/all_to_all | solution.py:39
  236.1 2.6 reshape.39
  238.7 0.0 all-gather.4.cloned.1.call-done
  238.7 0.0 copy-done
  238.7 4.7 %fusion.12 = f32[384,768]{0,1:T(8,128)} fusion(bf16[384,2048]{1,0:T(8,128)(2,1)S(1)} %copy-done, bf16[2048,768]{1,0:T(8,128)(2,1)} %all-gather.4.cloned.1.call-done), kind=kOutput, calls=%fused_computation.34 | convolution fusion | flops 1207959552 | bytes 5898240 | tf_op jit(solution)/shard_map/dot_general | solution.py:48
  243.5 2.8 multiply_convert_fusion.3
  246.3 0.0 copy-start.6
  246.3 0.7 copy-done.6
  247.0 3.5 convolution_convert_fusion
  250.5 0.0 reduce-scatter.2.cloned.1.call-update
  250.5 3.4 convolution_convert_fusion.2
  254.0 1.6 reshape.42
  255.6 11.0 %all-to-all-start.2 = ((bf16[64,6,2048]{2,1,0:T(8,128)(2,1)}), bf16[64,6,2048]{2,1,0:T(8,128)(2,1)}, u32[]{:S(2)}, u32[]{:S(2)}) async-start(bf16[64,6,2048]{2,1,0:T(8,128)(2,1)} %reshape.42), calls=%async_computation.2 | async-start | bytes 4194304 | tf_op jit(solution)/shard_map/all_to_all | solution.py:66
  266.6 0.0 all-reduce.4.cloned.1.call-start
  266.7 0.0 copy-done.5
  266.7 2.1 fusion
  268.8 0.0 all-reduce.4.cloned.1.call-update
  268.9 92.7 %all-to-all-done.2 = bf16[64,6,2048]{2,1,0:T(8,128)(2,1)} async-done(((bf16[64,6,2048]{2,1,0:T(8,128)(2,1)}), bf16[64,6,2048]{2,1,0:T(8,128)(2,1)}, u32[]{:S(2)}, u32[]{:S(2)}) %all-to-all-start.2) | async-done | bytes 1572896 | tf_op jit(solution)/shard_map/all_to_all | solution.py:66
  361.6 2.6 reshape.43
  364.2 1.7 gather_fusion.2
  365.9 1.8 slice_bitcast_fusion
  367.7 4.8 %all-reduce.4.cloned.1.call-done = bf16[1,384,2048]{2,1,0:T(8,128)(2,1)} async-done(((bf16[1,384,2048]{2,1,0:T(8,128)(2,1)}), bf16[1,384,2048]{2,1,0:T(8,128)(2,1)}) %all-reduce.4.cloned.1.call-update) | async-done | bytes 1572880 | tf_op jit(solution)/shard_map/psum | solution.py:74
  372.5 2.7 copy.17
  (13 shorter events, 0.1 us)
Async XLA Ops:
  15.8 19.5 %copy-start.2 = (bf16[1,256,384]{2,1,0:T(8,128)(2,1)S(1)}, bf16[1,256,384]{2,1,0:T(8,128)(2,1)}, u32[]{:S(2)}) copy-start(bf16[1,256,384]{2,1,0:T(8,128)(2,1)} %param.12) | copy-start | bytes 589828
  15.8 19.5 %copy-start.3 = (bf16[1,256,384]{2,1,0:T(8,128)(2,1)S(1)}, bf16[1,256,384]{2,1,0:T(8,128)(2,1)}, u32[]{:S(2)}) copy-start(bf16[1,256,384]{2,1,0:T(8,128)(2,1)} %param.11) | copy-start | bytes 589828
  15.8 20.3 %copy-start.1 = (bf16[128,2048]{1,0:T(8,128)(2,1)S(1)}, bf16[128,2048]{1,0:T(8,128)(2,1)}, u32[]{:S(2)}) copy-start(bf16[128,2048]{1,0:T(8,128)(2,1)} %param.8) | copy-start | bytes 1572868
  15.8 20.3 %copy-start.4 = (f32[128,1]{0,1:T(1,128)S(1)}, f32[128,1]{0,1:T(1,128)}, u32[]{:S(2)}) copy-start(f32[128,1]{0,1:T(1,128)} %param.10) | copy-start | bytes 1540
  15.8 114.2 %all-to-all-start.1 = ((bf16[64,6,2048]{2,1,0:T(8,128)(2,1)}), bf16[64,6,2048]{2,1,0:T(8,128)(2,1)S(1)}, u32[]{:S(2)}, u32[]{:S(2)}) async-start(bf16[64,6,2048]{2,1,0:T(8,128)(2,1)} %reshape.40), calls=%async_computation.1 | async-start | bytes 4194304 | tf_op jit(solution)/shard_map/all_to_all | solution.py:38
  35.2 203.5 %all-gather.4.cloned.1.call-start = ((), (), s32[]{:S(2)}) async-start(), calls=%async_computation.4 | async-start | bytes 3538944 | tf_op jit(solution)/shard_map/all_gather | solution.py:45
  130.0 106.1 %all-to-all-start = ((bf16[64,6,2048]{2,1,0:T(8,128)(2,1)}), bf16[64,6,2048]{2,1,0:T(8,128)(2,1)}, u32[]{:S(2)}, u32[]{:S(2)}) async-start(bf16[64,6,2048]{2,1,0:T(8,128)(2,1)} %reshape.38), calls=%async_computation | async-start | bytes 4194304 | tf_op jit(solution)/shard_map/all_to_all | solution.py:39
  141.2 102.3 %all-gather.6.cloned.1.call-start = ((), (), s32[]{:S(2)}) async-start(), calls=%async_computation.7 | async-start | bytes 1769472 | tf_op jit(solution)/shard_map/all_gather | solution.py:46
  141.9 224.0 %reduce-scatter.2.cloned.1.call-start = ((), (), s32[]{:S(2)}) async-start(), calls=%async_computation.5 | async-start | bytes 3538944 | tf_op jit(solution)/shard_map/reduce_scatter | solution.py:75
  143.6 95.2 %copy-start = (bf16[384,2048]{1,0:T(8,128)(2,1)S(1)}, bf16[384,2048]{1,0:T(8,128)(2,1)}, u32[]{:S(2)}) copy-start(bf16[384,2048]{1,0:T(8,128)(2,1)} %reshape.41) | copy-start | bytes 4718596
  246.3 0.7 copy-start.6
  255.6 11.0 %copy-start.5 = (f32[384,768]{0,1:T(8,128)S(1)}, f32[384,768]{0,1:T(8,128)}, u32[]{:S(2)}) copy-start(f32[384,768]{0,1:T(8,128)} %fusion.12) | copy-start | bytes 3538948
  255.6 105.9 %all-to-all-start.2 = ((bf16[64,6,2048]{2,1,0:T(8,128)(2,1)}), bf16[64,6,2048]{2,1,0:T(8,128)(2,1)}, u32[]{:S(2)}, u32[]{:S(2)}) async-start(bf16[64,6,2048]{2,1,0:T(8,128)(2,1)} %reshape.42), calls=%async_computation.2 | async-start | bytes 4194304 | tf_op jit(solution)/shard_map/all_to_all | solution.py:66
  266.6 105.9 %all-reduce.4.cloned.1.call-start = ((), (), s32[]{:S(2)}) async-start(), calls=%async_computation.6 | async-start | bytes 3145728 | tf_op jit(solution)/shard_map/psum | solution.py:74
Sparse Core Ops, SparseCore 0:
  38.8 36.9 all-gather.3
  144.1 34.2 all-gather.5
  250.7 38.2 reduce-scatter.1
  291.8 80.7 all-reduce.3
where the time goes:
time: 383 us; the launch traced here: 382 us
  waiting for transfers between devices  278 us (73%)
  starting transfers between devices  41.9 us (11%)
  local copies, waits for them, and re-layouts  28.2 us (7%)
  matrix products  16.7 us (4%)
  between operations  14 us (4%)
    all_to_all x1, waiting for transfers between devices, on_device(): lax.all_to_all(slot_grad, 'expert', split_axis=0, concat_axis=0, tiled=True)  92.7 us
    all_to_all x1, waiting for transfers between devices, on_device(): lax.all_to_all(send_grads, 'expert', split_axis=0, concat_axis=0, tiled=T...  92.5 us
    all_to_all x1, waiting for transfers between devices, on_device(): lax.all_to_all(send_inputs, 'expert', split_axis=0, concat_axis=0, tiled=...  86.9 us
    all_to_all x1, starting transfers between devices, on_device(): lax.all_to_all(send_inputs, 'expert', split_axis=0, concat_axis=0, tiled=...  19.4 us
    all_to_all x1, starting transfers between devices, on_device(): lax.all_to_all(send_grads, 'expert', split_axis=0, concat_axis=0, tiled=T...  11.1 us
    all_to_all x1, starting transfers between devices, on_device(): lax.all_to_all(slot_grad, 'expert', split_axis=0, concat_axis=0, tiled=True)  11 us
  transfers between devices with their start and end apart: 7, of which 4 were waited for; matrix products, arithmetic and copies ran while one was open for 8% of the time, Pallas kernels for 0%

commit v1 on v0

--- a/solution.py
+++ b/solution.py
@@ -34,12 +34,15 @@
     input_table = jnp.concatenate([tokens, jnp.zeros((1, model_width), tokens.dtype)], axis=0)
     send_grads = grad_table[source].reshape(expert_count, slot_depth, model_width)
     send_inputs = input_table[source // per_token].reshape(expert_count, slot_depth, model_width)
-    recv_inputs, recv_grads = (
-        lax.all_to_all(send_inputs, "expert", split_axis=0, concat_axis=0, tiled=True),
-        lax.all_to_all(send_grads, "expert", split_axis=0, concat_axis=0, tiled=True),
-    )
-    rows_in = recv_inputs.reshape(slot_count, model_width)
-    grads_in = recv_grads.reshape(slot_count, model_width)
+    recv_both = lax.all_to_all(
+        jnp.concatenate([send_inputs, send_grads], axis=2),
+        "expert",
+        split_axis=0,
+        concat_axis=0,
+        tiled=True,
+    ).reshape(slot_count, 2 * model_width)
+    rows_in = recv_both[:, :model_width]
+    grads_in = recv_both[:, model_width:]
     local_joined = jnp.concatenate([w_gate[0], w_up[0]], axis=1)
     full_joined, full_down = (
         lax.all_gather(local_joined, "dp", axis=0, tiled=True),

time: 383 us -> 382 us (level)
  starting transfers between devices: 41.9 us -> 33 us
  other arithmetic: 3.35 us -> 9.1 us
    all_to_all x2 -> x1, starting transfers between devices: 30.6 us -> 19.7 us  [on_device(): lax.all_to_all(jnp.concatenate([send_inputs, send_grads], axis=2), 'exper...]
    concatenate x0 -> x1, other arithmetic: none -> 4.7 us  [on_device(): jnp.concatenate([send_inputs, send_grads], axis=2)]
    all_to_all x1, waiting for transfers between devices: 92.7 us -> 88.2 us  [on_device(): lax.all_to_all(slot_grad, 'expert', split_axis=0, concat_axis=0, tiled=True)]
    all_to_all x2 -> x1, waiting for transfers between devices: 179 us -> 180 us  [on_device(): lax.all_to_all(jnp.concatenate([send_inputs, send_grads], axis=2), 'exper...]
  transfers between devices with their start and end apart: 7 -> 6, of which waited for: 4 -> 3; matrix products, arithmetic and copies ran while one was open for 8% -> 7% of each run, Pallas kernels for 0% -> 0%
where the time goes in v1:
time: 382 us; the launch traced here: 381 us
  waiting for transfers between devices  275 us (72%)
  starting transfers between devices  33 us (9%)
  local copies, waits for them, and re-layouts  30.9 us (8%)
  matrix products  19.1 us (5%)
  between operations  13.9 us (4%)
  other arithmetic  9.1 us (2%)
    all_to_all x1, waiting for transfers between devices, on_device(): lax.all_to_all(jnp.concatenate([send_inputs, send_grads], axis=2), 'exper...  180 us
    all_to_all x1, waiting for transfers between devices, on_device(): lax.all_to_all(slot_grad, 'expert', split_axis=0, concat_axis=0, tiled=True)  88.2 us
    all_to_all x1, starting transfers between devices, on_device(): lax.all_to_all(jnp.concatenate([send_inputs, send_grads], axis=2), 'exper...  19.7 us
    all_to_all x1, starting transfers between devices, on_device(): lax.all_to_all(slot_grad, 'expert', split_axis=0, concat_axis=0, tiled=True)  13 us
  transfers between devices with their start and end apart: 6, of which 3 were waited for; matrix products, arithmetic and copies ran while one was open for 7% of the time, Pallas kernels for 0%

profile of v1, /device:TPU:1, one launch (start us, length us, event | category | flops | bytes accessed | tf_op | source)
XLA Modules:
  0.0 381.1 jit_solution(12540610922786385212)
XLA Ops:
  7.2 0.7 fusion.10
  7.9 0.2 reduce_window_sum.11
  8.1 0.8 select_reduce_fusion
  8.9 0.7 fusion.13
  9.6 1.0 scatter_custom_fusion
  10.6 1.2 multiply_convert_fusion
  11.8 3.1 gather_fusion.1
  15.0 0.0 copy-start
  15.0 2.5 reshape.36
  17.5 0.0 copy-done
  17.6 3.1 gather_fusion
  20.7 3.7 reshape.35
  24.4 4.7 %pad_maximum_fusion = bf16[64,6,4096]{2,1,0:T(8,128)(2,1)} fusion(bf16[64,6,2048]{2,1,0:T(8,128)(2,1)S(1)} %reshape.36, bf16[64,6,2048]{2,1,0:T(8,128)(2,1)} %reshape.35), kind=kLoop, calls=%fused_computation.4 | loop fusion | flops 6291456 | bytes 6291456 | tf_op jit(solution)/shard_map/concatenate | solution.py:38
  29.1 0.0 copy-start.1
  29.1 0.0 copy-start.2
  29.1 19.7 %all-to-all-start = ((bf16[64,6,4096]{2,1,0:T(8,128)(2,1)}), bf16[64,6,4096]{2,1,0:T(8,128)(2,1)}, u32[]{:S(2)}, u32[]{:S(2)}) async-start(bf16[64,6,4096]{2,1,0:T(8,128)(2,1)} %pad_maximum_fusion), calls=%async_computation | async-start | bytes 8388608 | tf_op jit(solution)/shard_map/all_to_all | solution.py:37
  48.7 0.0 all-gather.4.cloned.1.call-start
  48.8 0.0 copy-done.1
  48.8 0.0 copy-done.2
  48.8 0.8 pad_maximum_fusion.2
  49.6 0.0 all-gather.4.cloned.1.call-update
  49.6 0.0 all-gather.6.cloned.1.call-start
  49.7 0.7 all-gather.6.cloned.1.call-update
  50.4 0.2 reduce-scatter.2.cloned.1.call-start
  50.6 180.4 %all-to-all-done = bf16[64,6,4096]{2,1,0:T(8,128)(2,1)} async-done(((bf16[64,6,4096]{2,1,0:T(8,128)(2,1)}), bf16[64,6,4096]{2,1,0:T(8,128)(2,1)}, u32[]{:S(2)}, u32[]{:S(2)}) %all-to-all-start) | async-done | bytes 3145760 | tf_op jit(solution)/shard_map/all_to_all | solution.py:37
  231.0 4.2 %reshape.37 = bf16[384,4096]{1,0:T(8,128)(2,1)S(1)} reshape(bf16[64,6,4096]{2,1,0:T(8,128)(2,1)} %all-to-all-done) | data formatting | bytes 6291456 | tf_op jit(solution)/shard_map/reshape | solution.py:43
  235.2 0.0 all-gather.4.cloned.1.call-done
  235.2 4.7 %fusion.4 = f32[384,768]{0,1:T(8,128)} fusion(bf16[2048,768]{1,0:T(8,128)(2,1)} %all-gather.4.cloned.1.call-done, bf16[384,4096]{1,0:T(8,128)(2,1)S(1)} %reshape.37), kind=kOutput, calls=%fused_computation.12 | convolution fusion | flops 1207959552 | bytes 5898240 | tf_op jit(solution)/shard_map/dot_general | solution.py:51
  240.0 0.0 all-gather.6.cloned.1.call-done
  240.0 2.8 multiply_convert_fusion.3
  242.8 0.0 copy-start.3
  242.8 0.7 copy-done.3
  243.5 3.5 convolution_convert_fusion
  247.0 0.0 reduce-scatter.2.cloned.1.call-update
  247.0 4.6 %convolution_convert_fusion.2 = bf16[384,2048]{1,0:T(8,128)(2,1)} fusion(bf16[2048,768]{1,0:T(8,128)(2,1)} %all-gather.4.cloned.1.call-done, bf16[384,384]{0,1:T(8,128)(2,1)} %copy-done.3, bf16[384,384]{0,1:T(8,128)(2,1)S(1)} %get-tuple-element.4), kind=kOutput, calls=%fused_computation.7 | convolution fusion | flops 1209925632 | bytes 5308416 | tf_op jit(solution)/shard_map/dot_general | solution.py:65
  251.6 3.7 reshape.38
  255.3 13.0 %all-to-all-start.1 = ((bf16[64,6,2048]{2,1,0:T(8,128)(2,1)}), bf16[64,6,2048]{2,1,0:T(8,128)(2,1)}, u32[]{:S(2)}, u32[]{:S(2)}) async-start(bf16[64,6,2048]{2,1,0:T(8,128)(2,1)} %reshape.38), calls=%async_computation.1 | async-start | bytes 4194304 | tf_op jit(solution)/shard_map/all_to_all | solution.py:69
  268.3 0.0 all-reduce.4.cloned.1.call-start
  268.3 3.4 fusion
  271.7 0.0 all-reduce.4.cloned.1.call-update
  271.8 88.2 %all-to-all-done.1 = bf16[64,6,2048]{2,1,0:T(8,128)(2,1)} async-done(((bf16[64,6,2048]{2,1,0:T(8,128)(2,1)}), bf16[64,6,2048]{2,1,0:T(8,128)(2,1)}, u32[]{:S(2)}, u32[]{:S(2)}) %all-to-all-start.1) | async-done | bytes 1572896 | tf_op jit(solution)/shard_map/all_to_all | solution.py:69
  359.9 2.6 reshape.39
  362.6 1.7 gather_fusion.2
  364.3 0.0 reduce-scatter.2.cloned.1.call-done
  364.3 1.8 slice_bitcast_fusion
  366.1 5.7 %all-reduce.4.cloned.1.call-done = bf16[1,384,2048]{2,1,0:T(8,128)(2,1)} async-done(((bf16[1,384,2048]{2,1,0:T(8,128)(2,1)}), bf16[1,384,2048]{2,1,0:T(8,128)(2,1)}) %all-reduce.4.cloned.1.call-update) | async-done | bytes 1572880 | tf_op jit(solution)/shard_map/psum | solution.py:77
  371.8 2.7 copy.17
  (6 shorter events, 0.1 us)
Async XLA Ops:
  15.0 2.6 copy-start
  29.1 19.7 %copy-start.1 = (bf16[1,256,384]{2,1,0:T(8,128)(2,1)S(1)}, bf16[1,256,384]{2,1,0:T(8,128)(2,1)}, u32[]{:S(2)}) copy-start(bf16[1,256,384]{2,1,0:T(8,128)(2,1)} %param.12) | copy-start | bytes 589828
  29.1 19.7 %copy-start.2 = (bf16[1,256,384]{2,1,0:T(8,128)(2,1)S(1)}, bf16[1,256,384]{2,1,0:T(8,128)(2,1)}, u32[]{:S(2)}) copy-start(bf16[1,256,384]{2,1,0:T(8,128)(2,1)} %param.11) | copy-start | bytes 589828
  29.1 202.0 %all-to-all-start = ((bf16[64,6,4096]{2,1,0:T(8,128)(2,1)}), bf16[64,6,4096]{2,1,0:T(8,128)(2,1)}, u32[]{:S(2)}, u32[]{:S(2)}) async-start(bf16[64,6,4096]{2,1,0:T(8,128)(2,1)} %pad_maximum_fusion), calls=%async_computation | async-start | bytes 8388608 | tf_op jit(solution)/shard_map/all_to_all | solution.py:37
  48.7 186.5 %all-gather.4.cloned.1.call-start = ((), (), s32[]{:S(2)}) async-start(), calls=%async_computation.3 | async-start | bytes 3538944 | tf_op jit(solution)/shard_map/all_gather | solution.py:48
  49.6 190.3 %all-gather.6.cloned.1.call-start = ((), (), s32[]{:S(2)}) async-start(), calls=%async_computation.6 | async-start | bytes 1769472 | tf_op jit(solution)/shard_map/all_gather | solution.py:49
  50.4 313.9 %reduce-scatter.2.cloned.1.call-start = ((), (), s32[]{:S(2)}) async-start(), calls=%async_computation.4 | async-start | bytes 3538944 | tf_op jit(solution)/shard_map/reduce_scatter | solution.py:78
  242.8 0.7 copy-start.3
  255.3 104.6 %all-to-all-start.1 = ((bf16[64,6,2048]{2,1,0:T(8,128)(2,1)}), bf16[64,6,2048]{2,1,0:T(8,128)(2,1)}, u32[]{:S(2)}, u32[]{:S(2)}) async-start(bf16[64,6,2048]{2,1,0:T(8,128)(2,1)} %reshape.38), calls=%async_computation.1 | async-start | bytes 4194304 | tf_op jit(solution)/shard_map/all_to_all | solution.py:69
  268.3 103.6 %all-reduce.4.cloned.1.call-start = ((), (), s32[]{:S(2)}) async-start(), calls=%async_computation.5 | async-start | bytes 3145728 | tf_op jit(solution)/shard_map/psum | solution.py:77
Sparse Core Ops, SparseCore 0:
  52.3 36.8 all-gather.3
  91.3 32.9 all-gather.5
  247.1 41.1 reduce-scatter.1
  291.1 80.6 all-reduce.3

commit v2 on v0

--- a/solution.py
+++ b/solution.py
@@ -1,7 +1,84 @@
+import functools
 import jax
 import jax.numpy as jnp
 from jax import lax
+from jax.experimental import pallas as pl
+from jax.experimental.pallas import tpu as pltpu
 from jax.sharding import PartitionSpec as P
+
+MESH = pl.DeviceIdType.MESH
+
+
+def exchange_kernel(n, count, *refs):
+    sources = refs[:count]
+    targets = refs[count : 2 * count]
+    send_sem, recv_sem, local_sem = refs[2 * count :]
+    me = lax.axis_index("expert")
+    row = lax.axis_index("dp")
+    barrier = pltpu.get_barrier_semaphore()
+
+    def greet(i, carry):
+        peer = lax.rem(me + i, n)
+        pl.semaphore_signal(barrier, inc=1, device_id=(row, peer), device_id_type=MESH)
+        return carry
+
+    lax.fori_loop(1, n, greet, 0)
+    pl.semaphore_wait(barrier, n - 1)
+    local = [
+        pltpu.make_async_copy(sources[a].at[me], targets[a].at[me], local_sem.at[a])
+        for a in range(count)
+    ]
+    for copy in local:
+        copy.start()
+
+    def remote(a, peer, slot):
+        return pltpu.make_async_remote_copy(
+            src_ref=sources[a].at[peer],
+            dst_ref=targets[a].at[slot],
+            send_sem=send_sem.at[a, peer],
+            recv_sem=recv_sem.at[a, slot],
+            device_id=(row, peer),
+            device_id_type=MESH,
+        )
+
+    def start(i, carry):
+        peer = lax.rem(me + i, n)
+        for a in range(count):
+            remote(a, peer, me).start()
+        return carry
+
+    lax.fori_loop(1, n, start, 0)
+
+    def finish(i, carry):
+        peer = lax.rem(me + i, n)
+        source = lax.rem(me + n - i, n)
+        for a in range(count):
+            remote(a, peer, me).wait_send()
+            remote(a, source, source).wait_recv()
+        return carry
+
+    lax.fori_loop(1, n, finish, 0)
+    for copy in local:
+        copy.wait()
+
+
+def expert_exchange(arrays, collective_id):
+    n = arrays[0].shape[0]
+    count = len(arrays)
+    return pl.pallas_call(
+        functools.partial(exchange_kernel, n, count),
+        out_shape=[jax.ShapeDtypeStruct(a.shape, a.dtype) for a in arrays],
+        in_specs=[pl.BlockSpec(memory_space=pl.ANY)] * count,
+        out_specs=[pl.BlockSpec(memory_space=pl.ANY)] * count,
+        scratch_shapes=[
+            pltpu.SemaphoreType.DMA((count, n)),
+            pltpu.SemaphoreType.DMA((count, n)),
+            pltpu.SemaphoreType.DMA((count,)),
+        ],
+        compiler_params=pltpu.CompilerParams(
+            collective_id=collective_id, has_side_effects=True
+        ),
+    )(*arrays)
 
 
 def on_device(tokens, out_grad, expert_ids, gates, w_gate, w_up, w_down):
@@ -34,10 +111,7 @@
     input_table = jnp.concatenate([tokens, jnp.zeros((1, model_width), tokens.dtype)], axis=0)
     send_grads = grad_table[source].reshape(expert_count, slot_depth, model_width)
     send_inputs = input_table[source // per_token].reshape(expert_count, slot_depth, model_width)
-    recv_inputs, recv_grads = (
-        lax.all_to_all(send_inputs, "expert", split_axis=0, concat_axis=0, tiled=True),
-        lax.all_to_all(send_grads, "expert", split_axis=0, concat_axis=0, tiled=True),
-    )
+    recv_inputs, recv_grads = expert_exchange([send_inputs, send_grads], 0)
     rows_in = recv_inputs.reshape(slot_count, model_width)
     grads_in = recv_grads.reshape(slot_count, model_width)
     local_joined = jnp.concatenate([w_gate[0], w_up[0]], axis=1)
@@ -63,9 +137,7 @@
         both_sides, full_joined, (((1,), (1,)), ((), ())), preferred_element_type=jnp.float32
     )
     slot_grad = slot_grad.astype(jnp.bfloat16).reshape(expert_count, slot_depth, model_width)
-    returned = lax.all_to_all(slot_grad, "expert", split_axis=0, concat_axis=0, tiled=True).reshape(
-        slot_count, model_width
-    )
+    returned = expert_exchange([slot_grad], 1)[0].reshape(slot_count, model_width)
     picked = returned[slot_of_entry].astype(jnp.float32).reshape(tok_rows, per_token, model_width)
     input_grad = jnp.sum(picked, axis=1).astype(jnp.bfloat16)
     down_part = lax.dot_general(

time: 383 us -> 372 us (0.971)
  Pallas kernels: 0 us -> 302 us
  waiting for transfers between devices: 278 us -> 6.83 us
  starting transfers between devices: 41.9 us -> 0.34 us
    pallas_call x0 -> x2, Pallas kernels: none -> 302 us  [expert_exchange(): pl.pallas_call(functools.partial(exchange_kernel, n, count), out_shape=[j...]
    all_to_all x3 -> x0, waiting for transfers between devices: 272 us -> none  [the longest x1 92.7 us: on_device(): lax.all_to_all(slot_grad, 'expert', split_axis=0, concat_axis=0, tiled=True)]
    all_to_all x3 -> x0, starting transfers between devices: 41.5 us -> none  [the longest x1 19.4 us: on_device(): lax.all_to_all(send_inputs, 'expert', split_axis=0, concat_axis=0, tiled=...]
  transfers between devices with their start and end apart: 7 -> 4, of which waited for: 4 -> 1; matrix products, arithmetic and copies ran while one was open for 8% -> 9% of each run, Pallas kernels for 0% -> 81%
where the time goes in v2:
time: 372 us; the launch traced here: 371 us
  Pallas kernels  302 us (81%)
  local copies, waits for them, and re-layouts  27.6 us (7%)
  matrix products  17.3 us (5%)
  between operations  14 us (4%)
  waiting for transfers between devices  6.83 us (2%)
    pallas_call x2, Pallas kernels, expert_exchange(): pl.pallas_call(functools.partial(exchange_kernel, n, count), out_shape=[j...  302 us
  transfers between devices with their start and end apart: 4, of which 1 were waited for; matrix products, arithmetic and copies ran while one was open for 9% of the time, Pallas kernels for 81%

profile of v2, /device:TPU:1, one launch (start us, length us, event | category | flops | bytes accessed | tf_op | source)
XLA Modules:
  0.0 371.2 jit_solution(16103058180699073481)
XLA Ops:
  7.2 0.0 copy-start.6
  7.2 0.0 copy-start.3
  7.2 0.0 all-gather.4.cloned.1.call-start
  7.2 1.9 pad_maximum_fusion.1
  9.1 0.0 all-gather.4.cloned.1.call-update
  9.1 0.0 all-gather.6.cloned.1.call-start
  9.2 0.7 all-gather.6.cloned.1.call-update
  9.9 0.0 reduce-scatter.2.cloned.1.call-start
  9.9 0.7 fusion.5
  10.7 0.2 reduce_window_sum.11
  10.8 0.0 copy-done.6
  10.8 0.0 copy-done.3
  10.8 0.2 multiply_convert_fusion
  11.0 0.0 copy-done.5
  11.1 0.2 select_reduce_fusion
  11.3 1.0 scatter_custom_fusion
  12.3 2.5 gather_fusion.1
  14.7 0.0 copy-start.4
  14.7 1.6 reshape.39.refs_1_
  16.4 0.0 copy-done.4
  16.4 2.5 gather_fusion
  18.9 1.6 reshape.38.refs_0_
  20.5 202.1 %shard_map.102 = (bf16[64,6,2048]{2,1,0:T(8,128)(2,1)}, bf16[64,6,2048]{2,1,0:T(8,128)(2,1)}) custom-call(bf16[64,6,2048]{2,1,0:T(8,128)(2,1)} %reshape.38.refs_0_, bf16[64,6,2048]{2,1,0:T(8,128)(2,1)} %reshape.39.refs_1_), custom_call_target="tpu_custom_call" | custom-call | tf_op jit(solution)/shard_map/pallas_call | solution.py:68
  222.6 0.0 copy-start
  222.6 3.8 %reshape.41 = bf16[384,2048]{1,0:T(8,128)(2,1)} reshape(bf16[64,6,2048]{2,1,0:T(8,128)(2,1)} %get-tuple-element.7) | data formatting | bytes 3145728 | tf_op jit(solution)/shard_map/reshape | solution.py:115
  226.4 0.0 copy-done
  226.4 1.4 reshape.40
  227.9 5.4 %fusion.12 = f32[384,768]{0,1:T(8,128)} fusion(bf16[384,2048]{1,0:T(8,128)(2,1)} %reshape.41, bf16[2048,768]{1,0:T(8,128)(2,1)} %all-gather.4.cloned.1.call-done), kind=kOutput, calls=%fused_computation.34 | convolution fusion | flops 1207959552 | bytes 5898240 | tf_op jit(solution)/shard_map/dot_general | solution.py:122
  233.2 0.0 copy-done.1
  233.2 2.9 multiply_convert_fusion.3
  236.1 0.0 copy-start.8
  236.2 0.7 copy-done.8
  236.9 0.0 copy-done.2
  236.9 3.5 convolution_convert_fusion
  240.4 0.0 reduce-scatter.2.cloned.1.call-update
  240.4 0.2 all-reduce.4.cloned.1.call-start
  240.6 1.0 copy-done.7
  241.7 2.1 fusion
  243.8 0.0 all-reduce.4.cloned.1.call-update
  243.8 0.9 copy-done.9
  244.8 3.3 convolution_convert_fusion.2
  248.1 1.6 reshape.42.refs_0_
  249.7 99.9 %shard_map.103 = bf16[64,6,2048]{2,1,0:T(8,128)(2,1)} custom-call(bf16[64,6,2048]{2,1,0:T(8,128)(2,1)} %reshape.42.refs_0_), custom_call_target="tpu_custom_call" | custom-call | tf_op jit(solution)/shard_map/pallas_call | solution.py:68
  349.7 2.6 reshape.43
  352.3 1.7 gather_fusion.2
  354.0 1.8 slice_bitcast_fusion
  355.8 6.1 %all-reduce.4.cloned.1.call-done = bf16[1,384,2048]{2,1,0:T(8,128)(2,1)} async-done(((bf16[1,384,2048]{2,1,0:T(8,128)(2,1)}), bf16[1,384,2048]{2,1,0:T(8,128)(2,1)}) %all-reduce.4.cloned.1.call-update) | async-done | bytes 1572880 | tf_op jit(solution)/shard_map/psum | solution.py:146
  361.9 2.7 copy.17
  (15 shorter events, 0.1 us)
Async XLA Ops:
  7.2 3.7 copy-start.6
  7.2 3.7 copy-start.3
  7.2 220.7 %all-gather.4.cloned.1.call-start = ((), (), s32[]{:S(2)}) async-start(), calls=%async_computation.1 | async-start | bytes 3538944 | tf_op jit(solution)/shard_map/all_gather | solution.py:119
  9.1 2.0 copy-start.5
  9.1 224.1 %all-gather.6.cloned.1.call-start = ((), (), s32[]{:S(2)}) async-start(), calls=%async_computation.4 | async-start | bytes 1769472 | tf_op jit(solution)/shard_map/all_gather | solution.py:120
  9.9 344.2 %reduce-scatter.2.cloned.1.call-start = ((), (), s32[]{:S(2)}) async-start(), calls=%async_computation.2 | async-start | bytes 3538944 | tf_op jit(solution)/shard_map/reduce_scatter | solution.py:147
  14.7 1.6 copy-start.4
  222.6 3.9 %copy-start = (bf16[64,6,2048]{2,1,0:T(8,128)(2,1)S(1)}, bf16[64,6,2048]{2,1,0:T(8,128)(2,1)}, u32[]{:S(2)}) copy-start(bf16[64,6,2048]{2,1,0:T(8,128)(2,1)} %get-tuple-element.6) | copy-start | bytes 4718596
  227.9 5.4 %copy-start.1 = (bf16[384,2048]{1,0:T(8,128)(2,1)S(1)}, bf16[384,2048]{1,0:T(8,128)(2,1)}, u32[]{:S(2)}) copy-start(bf16[384,2048]{1,0:T(8,128)(2,1)} %reshape.40) | copy-start | bytes 4718596
  233.2 3.7 copy-start.2
  236.1 0.7 copy-start.8
  240.4 1.3 copy-start.7
  240.4 121.5 %all-reduce.4.cloned.1.call-start = ((), (), s32[]{:S(2)}) async-start(), calls=%async_computation.3 | async-start | bytes 3145728 | tf_op jit(solution)/shard_map/psum | solution.py:146
  243.8 1.0 copy-start.9
Sparse Core Ops, SparseCore 0:
  10.7 41.1 all-gather.3
  54.0 32.9 all-gather.5
  240.5 38.0 reduce-scatter.1
  281.4 80.4 all-reduce.3

commit v3 on v2

--- a/solution.py
+++ b/solution.py
@@ -109,22 +109,23 @@
     )
     grad_table = jnp.concatenate([entry_scaled, jnp.zeros((1, model_width), jnp.bfloat16)], axis=0)
     input_table = jnp.concatenate([tokens, jnp.zeros((1, model_width), tokens.dtype)], axis=0)
-    send_grads = grad_table[source].reshape(expert_count, slot_depth, model_width)
-    send_inputs = input_table[source // per_token].reshape(expert_count, slot_depth, model_width)
-    recv_inputs, recv_grads = expert_exchange([send_inputs, send_grads], 0)
-    rows_in = recv_inputs.reshape(slot_count, model_width)
-    grads_in = recv_grads.reshape(slot_count, model_width)
+    picks = source.reshape(expert_count, slot_depth)
+    send_grads = grad_table[picks]
+    send_inputs = input_table[picks // per_token]
+    rows_in, grads_in = expert_exchange([send_inputs, send_grads], 0)
     local_joined = jnp.concatenate([w_gate[0], w_up[0]], axis=1)
     full_joined, full_down = (
         lax.all_gather(local_joined, "dp", axis=0, tiled=True),
         lax.all_gather(w_down[0], "dp", axis=1, tiled=True),
     )
-    preact = jnp.dot(rows_in, full_joined, preferred_element_type=jnp.float32)
+    preact = lax.dot_general(
+        rows_in, full_joined, (((2,), (0,)), ((), ())), preferred_element_type=jnp.float32
+    )
     hidden_grad = lax.dot_general(
-        grads_in, full_down, (((1,), (1,)), ((), ())), preferred_element_type=jnp.float32
+        grads_in, full_down, (((2,), (1,)), ((), ())), preferred_element_type=jnp.float32
     )
-    gate_pre = preact[:, :hidden]
-    up_pre = preact[:, hidden:]
+    gate_pre = preact[:, :, :hidden]
+    up_pre = preact[:, :, hidden:]
     sigmoid = jax.nn.sigmoid(gate_pre)
     silu_value = gate_pre * sigmoid
     activated = (silu_value * up_pre).astype(jnp.bfloat16)
@@ -132,21 +133,20 @@
         jnp.bfloat16
     )
     up_side = (hidden_grad * silu_value).astype(jnp.bfloat16)
-    both_sides = jnp.concatenate([gate_side, up_side], axis=1)
+    both_sides = jnp.concatenate([gate_side, up_side], axis=2)
     slot_grad = lax.dot_general(
-        both_sides, full_joined, (((1,), (1,)), ((), ())), preferred_element_type=jnp.float32
-    )
-    slot_grad = slot_grad.astype(jnp.bfloat16).reshape(expert_count, slot_depth, model_width)
-    returned = expert_exchange([slot_grad], 1)[0].reshape(slot_count, model_width)
-    picked = returned[slot_of_entry].astype(jnp.float32).reshape(tok_rows, per_token, model_width)
+        both_sides, full_joined, (((2,), (1,)), ((), ())), preferred_element_type=jnp.float32
+    ).astype(jnp.bfloat16)
+    returned = expert_exchange([slot_grad], 1)[0]
+    picked = returned[flat_ids, ranking].astype(jnp.float32).reshape(tok_rows, per_token, model_width)
     input_grad = jnp.sum(picked, axis=1).astype(jnp.bfloat16)
     down_part = lax.dot_general(
-        activated, grads_in, (((0,), (0,)), ((), ())), preferred_element_type=jnp.float32
+        activated, grads_in, (((0, 1), (0, 1)), ((), ())), preferred_element_type=jnp.float32
     )
     down_grad = lax.psum(down_part.astype(jnp.bfloat16), "dp")[None]
     joined_grad = lax.psum_scatter(
         lax.dot_general(
-            rows_in, both_sides, (((0,), (0,)), ((), ())), preferred_element_type=jnp.float32
+            rows_in, both_sides, (((0, 1), (0, 1)), ((), ())), preferred_element_type=jnp.float32
         ).astype(jnp.bfloat16),
         "dp",
         scatter_dimension=0,

time: 372 us -> 368 us (0.989)
  local copies, waits for them, and re-layouts: 27.6 us -> 23.7 us
    reshape x6 -> x1, local copies, waits for them, and re-layouts: 12.7 us -> 0.13 us  [on_device(): picks = source.reshape(expert_count, slot_depth)]
    gather x3 -> x5, local copies, waits for them, and re-layouts: 6.63 us -> 11.4 us  [the longest x2 4.09 us: on_device(): send_inputs = input_table[picks // per_token]]
  transfers between devices with their start and end apart: 4 -> 4, of which waited for: 1 -> 1; matrix products, arithmetic and copies ran while one was open for 9% -> 9% of each run, Pallas kernels for 81% -> 82%
where the time goes in v3:
time: 368 us
  Pallas kernels  302 us (82%)
  local copies, waits for them, and re-layouts  23.7 us (6%)
  matrix products  20.6 us (6%)
  between operations  14 us (4%)
  waiting for transfers between devices  3.79 us (1%)
    pallas_call x2, Pallas kernels, expert_exchange(): pl.pallas_call(functools.partial(exchange_kernel, n, count), out_shape=[j...  302 us
  transfers between devices with their start and end apart: 4, of which 1 were waited for; matrix products, arithmetic and copies ran while one was open for 9% of the time, Pallas kernels for 82%

profile of v3, /device:TPU:1, one launch (start us, length us, event | category | flops | bytes accessed | tf_op | source)
XLA Modules:
  0.0 367.6 jit_solution(15978541024977403981)
XLA Ops:
  7.2 0.0 copy-start.2
  7.2 0.0 copy-start
  7.2 0.0 all-gather.4.cloned.1.call-start
  7.2 1.9 pad_maximum_fusion.1
  9.1 0.0 all-gather.4.cloned.1.call-update
  9.1 0.0 all-gather.6.cloned.1.call-start
  9.2 0.7 all-gather.6.cloned.1.call-update
  9.9 0.0 reduce-scatter.2.cloned.1.call-start
  9.9 0.7 fusion.16
  10.7 0.2 reduce_window_sum.11
  10.8 0.0 copy-done.2
  10.8 0.2 select_reduce_fusion
  11.0 1.0 scatter_custom_fusion
  12.0 0.1 reshape.74
  12.2 0.1 reshape.77
  12.3 0.0 copy-done
  12.4 2.5 gather_fusion
  14.8 0.0 copy-start.1
  14.9 0.0 copy-start.3
  14.9 1.6 reshape.76.refs_0_
  16.5 0.0 copy-done.1
  16.5 0.0 copy-done.3
  16.5 0.2 multiply_convert_fusion
  16.7 2.5 gather_fusion.1
  19.2 1.6 reshape.84.refs_1_
  20.8 202.1 %shard_map.102 = (bf16[64,6,2048]{2,1,0:T(8,128)(2,1)}, bf16[64,6,2048]{2,1,0:T(8,128)(2,1)}) custom-call(bf16[64,6,2048]{2,1,0:T(8,128)(2,1)} %reshape.76.refs_0_, bf16[64,6,2048]{2,1,0:T(8,128)(2,1)} %reshape.84.refs_1_), custom_call_target="tpu_custom_call" | custom-call | tf_op jit(solution)/shard_map/pallas_call | solution.py:68
  222.9 0.0 all-gather.4.cloned.1.call-done
  222.9 0.0 copy-start.5
  222.9 5.5 %fusion.2 = f32[64,6,768]{2,0,1:T(8,128)S(1)} fusion(bf16[2048,768]{1,0:T(8,128)(2,1)} %all-gather.4.cloned.1.call-done, bf16[64,6,2048]{2,1,0:T(8,128)(2,1)} %get-tuple-element.7), kind=kOutput, calls=%fused_computation.8 | convolution fusion | flops 1207959552 | bytes 5898240 | tf_op jit(solution)/shard_map/dot_general | solution.py:121
  228.4 0.0 all-gather.6.cloned.1.call-done
  228.5 3.3 multiply_convert_fusion.3
  231.8 0.0 copy-start.10
  231.8 0.7 copy-done.8
  232.5 0.1 copy-done.10
  232.6 4.0 %bitcast_convert_fusion = bf16[2048,768]{1,0:T(8,128)(2,1)} fusion(bf16[64,6,2048]{2,1,0:T(8,128)(2,1)S(1)} %copy-done.6, bf16[64,6,384]{2,0,1:T(8,128)(2,1)S(1)} %get-tuple-element.9, bf16[64,6,384]{2,0,1:T(8,128)(2,1)S(1)} %get-tuple-element.8), kind=kOutput, calls=%fused_computation.4 | convolution fusion | flops 1210712064 | bytes 5308416 | tf_op jit(solution)/shard_map/dot_general | solution.py:148
  236.6 0.0 reduce-scatter.2.cloned.1.call-update
  236.6 0.2 all-reduce.4.cloned.1.call-start
  236.8 5.5 %fusion.7 = bf16[1,384,2048]{2,1,0:T(8,128)(2,1)} fusion(bf16[64,6,2048]{2,1,0:T(8,128)(2,1)} %get-tuple-element.6, f32[64,6,768]{2,0,1:T(8,128)} %copy-done.7), kind=kOutput, calls=%fused_computation.11 | convolution fusion | flops 605650944 | bytes 4325376 | tf_op jit(solution)/shard_map/dot_general | solution.py:143
  242.3 0.0 all-reduce.4.cloned.1.call-update
  242.4 0.9 copy-done.9
  243.3 2.4 fusion.4
  245.7 2.2 copy.25.refs_0_
  247.9 99.9 %shard_map.103 = bf16[64,6,2048]{2,1,0:T(8,128)(2,1)} custom-call(bf16[64,6,2048]{2,1,0:T(8,128)(2,1)} %copy.25.refs_0_), custom_call_target="tpu_custom_call" | custom-call | tf_op jit(solution)/shard_map/pallas_call | solution.py:68
  347.8 2.5 copy.26
  350.3 3.2 gather_fusion.2
  353.5 1.8 slice_bitcast_fusion
  355.3 3.0 all-reduce.4.cloned.1.call-done
  358.3 2.7 copy.40
  (16 shorter events, 0.1 us)
Async XLA Ops:
  7.2 3.7 copy-start.2
  7.2 5.1 %copy-start = (bf16[128,2048]{1,0:T(8,128)(2,1)S(1)}, bf16[128,2048]{1,0:T(8,128)(2,1)}, u32[]{:S(2)}) copy-start(bf16[128,2048]{1,0:T(8,128)(2,1)} %param.7) | copy-start | bytes 1572868
  7.2 215.7 %all-gather.4.cloned.1.call-start = ((), (), s32[]{:S(2)}) async-start(), calls=%async_computation.1 | async-start | bytes 3538944 | tf_op jit(solution)/shard_map/all_gather | solution.py:118
  9.1 219.4 %all-gather.6.cloned.1.call-start = ((), (), s32[]{:S(2)}) async-start(), calls=%async_computation.4 | async-start | bytes 1769472 | tf_op jit(solution)/shard_map/all_gather | solution.py:119
  9.9 343.7 %reduce-scatter.2.cloned.1.call-start = ((), (), s32[]{:S(2)}) async-start(), calls=%async_computation.2 | async-start | bytes 3538944 | tf_op jit(solution)/shard_map/reduce_scatter | solution.py:147
  14.8 1.7 copy-start.1
  14.9 1.7 copy-start.3
  222.9 5.6 %copy-start.5 = (bf16[64,6,2048]{2,1,0:T(8,128)(2,1)S(1)}, bf16[64,6,2048]{2,1,0:T(8,128)(2,1)}, u32[]{:S(2)}) copy-start(bf16[64,6,2048]{2,1,0:T(8,128)(2,1)} %get-tuple-element.6) | copy-start | bytes 4718596
  228.4 3.4 copy-start.7
  228.5 4.1 %copy-start.6 = (bf16[64,6,2048]{2,1,0:T(8,128)(2,1)S(1)}, bf16[64,6,2048]{2,1,0:T(8,128)(2,1)}, u32[]{:S(2)}) copy-start(bf16[64,6,2048]{2,1,0:T(8,128)(2,1)} %get-tuple-element.7) | copy-start | bytes 4718596
  231.8 0.7 copy-start.8
  231.8 0.8 copy-start.10
  236.6 121.7 %all-reduce.4.cloned.1.call-start = ((), (), s32[]{:S(2)}) async-start(), calls=%async_computation.3 | async-start | bytes 3145728 | tf_op jit(solution)/shard_map/psum | solution.py:146
  236.8 5.6 %copy-start.4 = (bf16[2048,768]{1,0:T(8,128)(2,1)S(1)}, bf16[2048,768]{1,0:T(8,128)(2,1)}, u32[]{:S(2)}) copy-start(bf16[2048,768]{1,0:T(8,128)(2,1)} %all-gather.4.cloned.1.call-done) | copy-start | bytes 9437188
  242.3 1.0 copy-start.9
Sparse Core Ops, SparseCore 0:
  10.7 41.1 all-gather.3
  54.0 32.9 all-gather.5
  236.7 37.8 reduce-scatter.1
  277.4 80.9 all-reduce.3

commit v4 on v3

--- a/solution.py
+++ b/solution.py
@@ -81,6 +81,148 @@
     )(*arrays)
 
 
+def return_kernel(n, groups, slot_ref, part_ref, out_ref, down_ref, send_sem, recv_sem,
+                  local_sem, rs_send, rs_recv, ag_send, ag_recv, own_sem, parts, reduced):
+    me = lax.axis_index("expert")
+    row = lax.axis_index("dp")
+    rows = reduced.shape[0]
+    barrier = pltpu.get_barrier_semaphore()
+
+    def greet(i, carry):
+        peer = lax.rem(me + i, n)
+        pl.semaphore_signal(barrier, inc=1, device_id=(row, peer), device_id_type=MESH)
+        return carry
+
+    def greet_group(i, carry):
+        other = lax.rem(row + i, groups)
+        pl.semaphore_signal(barrier, inc=1, device_id=(other, me), device_id_type=MESH)
+        return carry
+
+    lax.fori_loop(1, n, greet, 0)
+    lax.fori_loop(1, groups, greet_group, 0)
+    pl.semaphore_wait(barrier, n - 1 + groups - 1)
+    local = pltpu.make_async_copy(slot_ref.at[me], out_ref.at[me], local_sem)
+    local.start()
+
+    def remote(peer, slot):
+        return pltpu.make_async_remote_copy(
+            src_ref=slot_ref.at[peer],
+            dst_ref=out_ref.at[slot],
+            send_sem=send_sem.at[peer],
+            recv_sem=recv_sem.at[slot],
+            device_id=(row, peer),
+            device_id_type=MESH,
+        )
+
+    def start(i, carry):
+        remote(lax.rem(me + i, n), me).start()
+        return carry
+
+    lax.fori_loop(1, n, start, 0)
+
+    def scatter_copy(other, slot):
+        return pltpu.make_async_remote_copy(
+            src_ref=part_ref.at[pl.ds(pl.multiple_of(other * rows, rows), rows)],
+            dst_ref=parts.at[slot],
+            send_sem=rs_send.at[other],
+            recv_sem=rs_recv.at[slot],
+            device_id=(other, me),
+            device_id_type=MESH,
+        )
+
+    own = pltpu.make_async_copy(
+        part_ref.at[pl.ds(pl.multiple_of(row * rows, rows), rows)], parts.at[row], own_sem.at[0]
+    )
+    own.start()
+
+    def scatter_start(i, carry):
+        scatter_copy(lax.rem(row + i, groups), row).start()
+        return carry
+
+    lax.fori_loop(1, groups, scatter_start, 0)
+
+    def scatter_finish(i, carry):
+        scatter_copy(lax.rem(row + i, groups), row).wait_send()
+        source = lax.rem(row + groups - i, groups)
+        scatter_copy(source, source).wait_recv()
+        return carry
+
+    lax.fori_loop(1, groups, scatter_finish, 0)
+    own.wait()
+    total = parts[0].astype(jnp.float32)
+    for slot in range(1, groups):
+        total = total + parts[slot].astype(jnp.float32)
+    reduced[...] = total.astype(reduced.dtype)
+
+    def gather_copy(other, slot):
+        return pltpu.make_async_remote_copy(
+            src_ref=reduced,
+            dst_ref=down_ref.at[pl.ds(pl.multiple_of(slot * rows, rows), rows)],
+            send_sem=ag_send.at[other],
+            recv_sem=ag_recv.at[slot],
+            device_id=(other, me),
+            device_id_type=MESH,
+        )
+
+    keep = pltpu.make_async_copy(
+        reduced, down_ref.at[pl.ds(pl.multiple_of(row * rows, rows), rows)], own_sem.at[1]
+    )
+    keep.start()
+
+    def gather_start(i, carry):
+        gather_copy(lax.rem(row + i, groups), row).start()
+        return carry
+
+    lax.fori_loop(1, groups, gather_start, 0)
+
+    def gather_finish(i, carry):
+        gather_copy(lax.rem(row + i, groups), row).wait_send()
+        source = lax.rem(row + groups - i, groups)
+        gather_copy(source, source).wait_recv()
+        return carry
+
+    lax.fori_loop(1, groups, gather_finish, 0)
+    keep.wait()
+
+    def finish(i, carry):
+        remote(lax.rem(me + i, n), me).wait_send()
+        source = lax.rem(me + n - i, n)
+        remote(source, source).wait_recv()
+        return carry
+
+    lax.fori_loop(1, n, finish, 0)
+    local.wait()
+
+
+def return_and_reduce(slot_grad, down_part, groups, collective_id):
+    n = slot_grad.shape[0]
+    rows = down_part.shape[0] // groups
+    return pl.pallas_call(
+        functools.partial(return_kernel, n, groups),
+        out_shape=[
+            jax.ShapeDtypeStruct(slot_grad.shape, slot_grad.dtype),
+            jax.ShapeDtypeStruct(down_part.shape, down_part.dtype),
+        ],
+        in_specs=[pl.BlockSpec(memory_space=pl.ANY)] * 2,
+        out_specs=[pl.BlockSpec(memory_space=pl.ANY)] * 2,
+        scratch_shapes=[
+            pltpu.SemaphoreType.DMA((n,)),
+            pltpu.SemaphoreType.DMA((n,)),
+            pltpu.SemaphoreType.DMA(()),
+            pltpu.SemaphoreType.DMA((groups,)),
+            pltpu.SemaphoreType.DMA((groups,)),
+            pltpu.SemaphoreType.DMA((groups,)),
+            pltpu.SemaphoreType.DMA((groups,)),
+            pltpu.SemaphoreType.DMA((2,)),
+            pltpu.VMEM((groups, rows, down_part.shape[1]), down_part.dtype),
+            pltpu.VMEM((rows, down_part.shape[1]), down_part.dtype),
+        ],
+        compiler_params=pltpu.CompilerParams(
+            collective_id=collective_id, has_side_effects=True
+        ),
+    )(slot_grad, down_part)
+
+
 def on_device(tokens, out_grad, expert_ids, gates, w_gate, w_up, w_down):
     expert_count = lax.axis_size("expert")
     tok_rows = tokens.shape[0]
@@ -137,13 +279,13 @@
     slot_grad = lax.dot_general(
         both_sides, full_joined, (((2,), (1,)), ((), ())), preferred_element_type=jnp.float32
     ).astype(jnp.bfloat16)
-    returned = expert_exchange([slot_grad], 1)[0]
+    down_part = lax.dot_general(
+        activated, grads_in, (((0, 1), (0, 1)), ((), ())), preferred_element_type=jnp.float32
+    ).astype(jnp.bfloat16)
+    returned, down_grad = return_and_reduce(slot_grad, down_part, lax.axis_size("dp"), 1)
+    down_grad = down_grad[None]
     picked = returned[flat_ids, ranking].astype(jnp.float32).reshape(tok_rows, per_token, model_width)
     input_grad = jnp.sum(picked, axis=1).astype(jnp.bfloat16)
-    down_part = lax.dot_general(
-        activated, grads_in, (((0, 1), (0, 1)), ((), ())), preferred_element_type=jnp.float32
-    )
-    down_grad = lax.psum(down_part.astype(jnp.bfloat16), "dp")[None]
     joined_grad = lax.psum_scatter(
         lax.dot_general(
             rows_in, both_sides, (((0, 1), (0, 1)), ((), ())), preferred_element_type=jnp.float32

time: 368 us -> 363 us (0.986)
    pallas_call x0 -> x1, Pallas kernels: none -> 100 us  [return_and_reduce(): pl.pallas_call(functools.partial(return_kernel, n, groups), out_shape=[ja...]
    pallas_call x2 -> x1, Pallas kernels: 302 us -> 202 us  [expert_exchange(): pl.pallas_call(functools.partial(exchange_kernel, n, count), out_shape=[j...]
  transfers between devices with their start and end apart: 4 -> 3, of which waited for: 1 -> 0; matrix products, arithmetic and copies ran while one was open for 9% -> 8% of each run, Pallas kernels for 82% -> 83%
where the time goes in v4:
time: 363 us; the launch traced here: 362 us
  Pallas kernels  302 us (83%)
  local copies, waits for them, and re-layouts  23.1 us (6%)
  matrix products  18.7 us (5%)
  between operations  14 us (4%)
    pallas_call x1, Pallas kernels, expert_exchange(): pl.pallas_call(functools.partial(exchange_kernel, n, count), out_shape=[j...  202 us
    pallas_call x1, Pallas kernels, return_and_reduce(): pl.pallas_call(functools.partial(return_kernel, n, groups), out_shape=[ja...  100 us
  transfers between devices with their start and end apart: 3, of which 0 were waited for; matrix products, arithmetic and copies ran while one was open for 8% of the time, Pallas kernels for 83%

profile of v4, /device:TPU:1, one launch (start us, length us, event | category | flops | bytes accessed | tf_op | source)
XLA Modules:
  0.0 362.4 jit_solution(8490414411427894560)
XLA Ops:
  7.2 0.0 copy-start.3
  7.2 0.0 copy-start.4
  7.2 0.0 copy-start.1
  7.2 0.0 all-gather.4.cloned.1.call-start
  7.2 1.9 pad_maximum_fusion.1
  9.1 0.0 all-gather.4.cloned.1.call-update
  9.1 0.0 all-gather.6.cloned.1.call-start
  9.2 0.7 all-gather.6.cloned.1.call-update
  9.9 0.0 reduce-scatter.2.cloned.1.call-start
  9.9 0.7 fusion.15
  10.7 0.2 reduce_window_sum.11
  10.8 0.0 copy-done.3
  10.8 0.2 select_reduce_fusion
  11.0 1.0 scatter_custom_fusion
  12.0 0.1 reshape.74
  12.2 0.1 reshape.77
  12.3 0.0 copy-done.4
  12.3 0.2 multiply_convert_fusion
  12.6 2.5 gather_fusion.1
  15.0 0.0 copy-start.2
  15.0 1.7 reshape.84.refs_1_
  16.7 0.0 copy-done.2
  16.8 2.5 gather_fusion
  19.2 1.6 reshape.76.refs_0_
  20.8 202.1 %shard_map.102 = (bf16[64,6,2048]{2,1,0:T(8,128)(2,1)}, bf16[64,6,2048]{2,1,0:T(8,128)(2,1)}) custom-call(bf16[64,6,2048]{2,1,0:T(8,128)(2,1)} %reshape.76.refs_0_, bf16[64,6,2048]{2,1,0:T(8,128)(2,1)} %reshape.84.refs_1_), custom_call_target="tpu_custom_call" | custom-call | tf_op jit(solution)/shard_map/pallas_call | solution.py:68
  222.9 0.0 all-gather.4.cloned.1.call-done
  222.9 0.0 copy-start.6
  223.0 5.5 %fusion.2 = f32[64,6,768]{2,0,1:T(8,128)S(1)} fusion(bf16[2048,768]{1,0:T(8,128)(2,1)} %all-gather.4.cloned.1.call-done, bf16[64,6,2048]{2,1,0:T(8,128)(2,1)} %get-tuple-element.9), kind=kOutput, calls=%fused_computation.8 | convolution fusion | flops 1207959552 | bytes 5898240 | tf_op jit(solution)/shard_map/dot_general | solution.py:263
  228.5 0.0 copy-start.9
  228.5 0.0 all-gather.6.cloned.1.call-done
  228.5 3.3 multiply_convert_fusion.3
  231.8 0.0 copy-start.12
  231.9 0.7 copy-done.11
  232.6 0.1 copy-done.12
  232.7 4.0 %bitcast_convert_fusion = bf16[2048,768]{1,0:T(8,128)(2,1)} fusion(bf16[64,6,2048]{2,1,0:T(8,128)(2,1)S(1)} %copy-done.8, bf16[64,6,384]{2,0,1:T(8,128)(2,1)S(1)} %get-tuple-element.13, bf16[64,6,384]{2,0,1:T(8,128)(2,1)S(1)} %get-tuple-element.12), kind=kOutput, calls=%fused_computation.4 | convolution fusion | flops 1210712064 | bytes 5308416 | tf_op jit(solution)/shard_map/dot_general | solution.py:290
  236.6 0.0 reduce-scatter.2.cloned.1.call-update
  236.6 1.9 copy-done.5
  238.5 2.5 fusion.4
  241.0 0.0 copy-start.10
  241.0 2.3 copy.26.slot_ref
  243.3 0.0 copy-done.7
  243.3 3.5 bitcast_convert_fusion.1.part_ref
  246.8 100.4 %shard_map.103 = (bf16[64,6,2048]{2,1,0:T(8,128)(2,1)}, bf16[384,2048]{1,0:T(8,128)(2,1)}) custom-call(bf16[64,6,2048]{2,1,0:T(8,128)(2,1)} %copy.26.slot_ref, bf16[384,2048]{1,0:T(8,128)(2,1)} %bitcast_convert_fusion.1.part_ref), custom_call_target="tpu_custom_call" | custom-call | tf_op jit(solution)/shard_map/pallas_call | solution.py:200
  347.2 2.5 copy.27
  349.7 0.0 copy-start
  349.7 3.2 gather_fusion.2
  352.9 1.8 slice_bitcast_fusion
  354.7 1.1 copy.40
  (17 shorter events, 0.1 us)
Async XLA Ops:
  7.2 3.7 %copy-start.3 = (s32[128,1]{0,1:T(1,128)S(1)}, s32[128,1]{0,1:T(1,128)}, u32[]{:S(2)}) copy-start(s32[128,1]{0,1:T(1,128)} %param.9) | copy-start | bytes 1540
  7.2 5.1 %copy-start.4 = (f32[128,1]{0,1:T(1,128)S(1)}, f32[128,1]{0,1:T(1,128)}, u32[]{:S(2)}) copy-start(f32[128,1]{0,1:T(1,128)} %param.10) | copy-start | bytes 1540
  7.2 5.1 %copy-start.1 = (bf16[128,2048]{1,0:T(8,128)(2,1)S(1)}, bf16[128,2048]{1,0:T(8,128)(2,1)}, u32[]{:S(2)}) copy-start(bf16[128,2048]{1,0:T(8,128)(2,1)} %param.8) | copy-start | bytes 1572868
  7.2 215.7 %all-gather.4.cloned.1.call-start = ((), (), s32[]{:S(2)}) async-start(), calls=%async_computation.1 | async-start | bytes 3538944 | tf_op jit(solution)/shard_map/all_gather | solution.py:260
  9.1 219.4 %all-gather.6.cloned.1.call-start = ((), (), s32[]{:S(2)}) async-start(), calls=%async_computation.3 | async-start | bytes 1769472 | tf_op jit(solution)/shard_map/all_gather | solution.py:261
  9.9 343.0 %reduce-scatter.2.cloned.1.call-start = ((), (), s32[]{:S(2)}) async-start(), calls=%async_computation.2 | async-start | bytes 3538944 | tf_op jit(solution)/shard_map/reduce_scatter | solution.py:289
  15.0 1.7 copy-start.2
  222.9 5.6 %copy-start.6 = (bf16[64,6,2048]{2,1,0:T(8,128)(2,1)S(1)}, bf16[64,6,2048]{2,1,0:T(8,128)(2,1)}, u32[]{:S(2)}) copy-start(bf16[64,6,2048]{2,1,0:T(8,128)(2,1)} %get-tuple-element.8) | copy-start | bytes 4718596
  228.5 3.4 copy-start.9
  228.5 4.1 %copy-start.8 = (bf16[64,6,2048]{2,1,0:T(8,128)(2,1)S(1)}, bf16[64,6,2048]{2,1,0:T(8,128)(2,1)}, u32[]{:S(2)}) copy-start(bf16[64,6,2048]{2,1,0:T(8,128)(2,1)} %get-tuple-element.9) | copy-start | bytes 4718596
  231.8 0.7 copy-start.11
  231.8 0.8 copy-start.12
  236.6 1.9 copy-start.5
  241.0 2.3 copy-start.7
  241.0 2.3 copy-start.10
  349.7 5.0 %copy-start = (bf16[384,2048]{1,0:T(8,128)(2,1)S(1)}, bf16[384,2048]{1,0:T(8,128)(2,1)}, u32[]{:S(2)}) copy-start(bf16[384,2048]{1,0:T(8,128)(2,1)} %get-tuple-element.11) | copy-start | bytes 4718596
Sparse Core Ops, SparseCore 0:
  10.7 41.1 all-gather.3
  54.0 32.9 all-gather.5
  236.8 63.0 reduce-scatter.1

commit v5 on v4

--- a/solution.py
+++ b/solution.py
@@ -9,12 +9,14 @@
 MESH = pl.DeviceIdType.MESH
 
 
-def exchange_kernel(n, count, *refs):
-    sources = refs[:count]
-    targets = refs[count : 2 * count]
-    send_sem, recv_sem, local_sem = refs[2 * count :]
+def forward_kernel(n, groups, inputs_ref, grads_ref, wg_ref, wu_ref, wd_ref, inputs_out,
+                   grads_out, joined_out, down_out, send_sem, recv_sem, local_sem, ag_send,
+                   ag_recv, own_sem):
     me = lax.axis_index("expert")
     row = lax.axis_index("dp")
+    width = wg_ref.shape[1]
+    piece = wg_ref.shape[0]
+    columns = wd_ref.shape[1]
     barrier = pltpu.get_barrier_semaphore()
 
     def greet(i, carry):
@@ -22,11 +24,19 @@
         pl.semaphore_signal(barrier, inc=1, device_id=(row, peer), device_id_type=MESH)
         return carry
 
+    def greet_group(i, carry):
+        other = lax.rem(row + i, groups)
+        pl.semaphore_signal(barrier, inc=1, device_id=(other, me), device_id_type=MESH)
+        return carry
+
     lax.fori_loop(1, n, greet, 0)
-    pl.semaphore_wait(barrier, n - 1)
+    lax.fori_loop(1, groups, greet_group, 0)
+    pl.semaphore_wait(barrier, n - 1 + groups - 1)
+    sources = (inputs_ref, grads_ref)
+    targets = (inputs_out, grads_out)
     local = [
         pltpu.make_async_copy(sources[a].at[me], targets[a].at[me], local_sem.at[a])
-        for a in range(count)
+        for a in range(2)
     ]
     for copy in local:
         copy.start()
@@ -43,16 +53,63 @@
 
     def start(i, carry):
         peer = lax.rem(me + i, n)
-        for a in range(count):
+        for a in range(2):
             remote(a, peer, me).start()
         return carry
 
     lax.fori_loop(1, n, start, 0)
+
+    def places(slot):
+        rows = pl.ds(pl.multiple_of(slot * piece, piece), piece)
+        cols = pl.ds(pl.multiple_of(slot * columns, columns), columns)
+        return (
+            (wg_ref, joined_out.at[rows, pl.ds(0, width)]),
+            (wu_ref, joined_out.at[rows, pl.ds(width, width)]),
+            (wd_ref, down_out.at[:, cols]),
+        )
+
+    def gather_copy(k, other, slot):
+        src, dst = places(slot)[k]
+        return pltpu.make_async_remote_copy(
+            src_ref=src,
+            dst_ref=dst,
+            send_sem=ag_send.at[k, other],
+            recv_sem=ag_recv.at[k, slot],
+            device_id=(other, me),
+            device_id_type=MESH,
+        )
+
+    own = [
+        pltpu.make_async_copy(src, dst, own_sem.at[k])
+        for k, (src, dst) in enumerate(places(row))
+    ]
+    for copy in own:
+        copy.start()
+
+    def gather_start(i, carry):
+        other = lax.rem(row + i, groups)
+        for k in range(3):
+            gather_copy(k, other, row).start()
+        return carry
+
+    lax.fori_loop(1, groups, gather_start, 0)
+
+    def gather_finish(i, carry):
+        other = lax.rem(row + i, groups)
+        source = lax.rem(row + groups - i, groups)
+        for k in range(3):
+            gather_copy(k, other, row).wait_send()
+            gather_copy(k, source, source).wait_recv()
+        return carry
+
+    lax.fori_loop(1, groups, gather_finish, 0)
+    for copy in own:
+        copy.wait()
 
     def finish(i, carry):
         peer = lax.rem(me + i, n)
         source = lax.rem(me + n - i, n)
-        for a in range(count):
+        for a in range(2):
             remote(a, peer, me).wait_send()
             remote(a, source, source).wait_recv()
         return carry
@@ -62,30 +119,41 @@
         copy.wait()
 
 
-def expert_exchange(arrays, collective_id):
-    n = arrays[0].shape[0]
-    count = len(arrays)
+def forward_exchange(send_inputs, send_grads, wg, wu, wd, groups, collective_id):
+    n = send_inputs.shape[0]
+    any_spec = pl.BlockSpec(memory_space=pl.ANY)
     return pl.pallas_call(
-        functools.partial(exchange_kernel, n, count),
-        out_shape=[jax.ShapeDtypeStruct(a.shape, a.dtype) for a in arrays],
-        in_specs=[pl.BlockSpec(memory_space=pl.ANY)] * count,
-        out_specs=[pl.BlockSpec(memory_space=pl.ANY)] * count,
+        functools.partial(forward_kernel, n, groups),
+        out_shape=[
+            jax.ShapeDtypeStruct(send_inputs.shape, send_inputs.dtype),
+            jax.ShapeDtypeStruct(send_grads.shape, send_grads.dtype),
+            jax.ShapeDtypeStruct((groups * wg.shape[0], 2 * wg.shape[1]), wg.dtype),
+            jax.ShapeDtypeStruct((wd.shape[0], groups * wd.shape[1]), wd.dtype),
+        ],
+        in_specs=[any_spec] * 5,
+        out_specs=[any_spec] * 4,
         scratch_shapes=[
-            pltpu.SemaphoreType.DMA((count, n)),
-            pltpu.SemaphoreType.DMA((count, n)),
-            pltpu.SemaphoreType.DMA((count,)),
+            pltpu.SemaphoreType.DMA((2, n)),
+            pltpu.SemaphoreType.DMA((2, n)),
+            pltpu.SemaphoreType.DMA((2,)),
+            pltpu.SemaphoreType.DMA((3, groups)),
+            pltpu.SemaphoreType.DMA((3, groups)),
+            pltpu.SemaphoreType.DMA((3,)),
         ],
         compiler_params=pltpu.CompilerParams(
             collective_id=collective_id, has_side_effects=True
         ),
-    )(*arrays)
-
-
-def return_kernel(n, groups, slot_ref, part_ref, out_ref, down_ref, send_sem, recv_sem,
-                  local_sem, rs_send, rs_recv, ag_send, ag_recv, own_sem, parts, reduced):
+    )(send_inputs, send_grads, wg, wu, wd)
+
+
+def return_kernel(n, groups, slot_ref, part_ref, joined_ref, out_ref, down_ref, gate_ref, up_ref,
+                  send_sem, recv_sem, local_sem, rs_send, rs_recv, ag_send, ag_recv, js_send,
+                  js_recv, own_sem, parts, reduced, joined_parts, joined_sum):
     me = lax.axis_index("expert")
     row = lax.axis_index("dp")
     rows = reduced.shape[0]
+    joined_rows = joined_sum.shape[0]
+    width = gate_ref.shape[1]
     barrier = pltpu.get_barrier_semaphore()
 
     def greet(i, carry):
@@ -130,13 +198,31 @@
             device_id_type=MESH,
         )
 
+    def joined_copy(other, slot):
+        return pltpu.make_async_remote_copy(
+            src_ref=joined_ref.at[pl.ds(pl.multiple_of(other * joined_rows, joined_rows), joined_rows)],
+            dst_ref=joined_parts.at[slot],
+            send_sem=js_send.at[other],
+            recv_sem=js_recv.at[slot],
+            device_id=(other, me),
+            device_id_type=MESH,
+        )
+
     own = pltpu.make_async_copy(
         part_ref.at[pl.ds(pl.multiple_of(row * rows, rows), rows)], parts.at[row], own_sem.at[0]
     )
     own.start()
+    own_joined = pltpu.make_async_copy(
+        joined_ref.at[pl.ds(pl.multiple_of(row * joined_rows, joined_rows), joined_rows)],
+        joined_parts.at[row],
+        own_sem.at[2],
+    )
+    own_joined.start()
 
     def scatter_start(i, carry):
-        scatter_copy(lax.rem(row + i, groups), row).start()
+        other = lax.rem(row + i, groups)
+        scatter_copy(other, row).start()
+        joined_copy(other, row).start()
         return carry
 
     lax.fori_loop(1, groups, scatter_start, 0)
@@ -175,6 +261,25 @@
 
     lax.fori_loop(1, groups, gather_start, 0)
 
+    def joined_finish(i, carry):
+        joined_copy(lax.rem(row + i, groups), row).wait_send()
+        source = lax.rem(row + groups - i, groups)
+        joined_copy(source, source).wait_recv()
+        return carry
+
+    lax.fori_loop(1, groups, joined_finish, 0)
+    own_joined.wait()
+    joined_total = joined_parts[0].astype(jnp.float32)
+    for slot in range(1, groups):
+        joined_total = joined_total + joined_parts[slot].astype(jnp.float32)
+    joined_sum[...] = joined_total.astype(joined_sum.dtype)
+    halves = [
+        pltpu.make_async_copy(joined_sum.at[:, pl.ds(0, width)], gate_ref, own_sem.at[3]),
+        pltpu.make_async_copy(joined_sum.at[:, pl.ds(width, width)], up_ref, own_sem.at[4]),
+    ]
+    for copy in halves:
+        copy.start()
+
     def gather_finish(i, carry):
         gather_copy(lax.rem(row + i, groups), row).wait_send()
         source = lax.rem(row + groups - i, groups)
@@ -183,6 +288,8 @@
 
     lax.fori_loop(1, groups, gather_finish, 0)
     keep.wait()
+    for copy in halves:
+        copy.wait()
 
     def finish(i, carry):
         remote(lax.rem(me + i, n), me).wait_send()
@@ -194,17 +301,22 @@
     local.wait()
 
 
-def return_and_reduce(slot_grad, down_part, groups, collective_id):
+def return_and_reduce(slot_grad, down_part, joined_part, groups, collective_id):
     n = slot_grad.shape[0]
     rows = down_part.shape[0] // groups
+    joined_rows = joined_part.shape[0] // groups
+    width = joined_part.shape[1] // 2
+    any_spec = pl.BlockSpec(memory_space=pl.ANY)
     return pl.pallas_call(
         functools.partial(return_kernel, n, groups),
         out_shape=[
             jax.ShapeDtypeStruct(slot_grad.shape, slot_grad.dtype),
             jax.ShapeDtypeStruct(down_part.shape, down_part.dtype),
+            jax.ShapeDtypeStruct((joined_rows, width), joined_part.dtype),
+            jax.ShapeDtypeStruct((joined_rows, width), joined_part.dtype),
         ],
-        in_specs=[pl.BlockSpec(memory_space=pl.ANY)] * 2,
-        out_specs=[pl.BlockSpec(memory_space=pl.ANY)] * 2,
+        in_specs=[any_spec] * 3,
+        out_specs=[any_spec] * 4,
         scratch_shapes=[
             pltpu.SemaphoreType.DMA((n,)),
             pltpu.SemaphoreType.DMA((n,)),
@@ -213,14 +325,18 @@
             pltpu.SemaphoreType.DMA((groups,)),
             pltpu.SemaphoreType.DMA((groups,)),
             pltpu.SemaphoreType.DMA((groups,)),
-            pltpu.SemaphoreType.DMA((2,)),
+            pltpu.SemaphoreType.DMA((groups,)),
+            pltpu.SemaphoreType.DMA((groups,)),
+            pltpu.SemaphoreType.DMA((5,)),
             pltpu.VMEM((groups, rows, down_part.shape[1]), down_part.dtype),
             pltpu.VMEM((rows, down_part.shape[1]), down_part.dtype),
+            pltpu.VMEM((groups, joined_rows, joined_part.shape[1]), joined_part.dtype),
+            pltpu.VMEM((joined_rows, joined_part.shape[1]), joined_part.dtype),
         ],
         compiler_params=pltpu.CompilerParams(
             collective_id=collective_id, has_side_effects=True
         ),
-    )(slot_grad, down_part)
+    )(slot_grad, down_part, joined_part)
 
 
 def on_device(tokens, out_grad, expert_ids, gates, w_gate, w_up, w_down):
@@ -254,11 +370,9 @@
     picks = source.reshape(expert_count, slot_depth)
     send_grads = grad_table[picks]
     send_inputs = input_table[picks // per_token]
-    rows_in, grads_in = expert_exchange([send_inputs, send_grads], 0)
-    local_joined = jnp.concatenate([w_gate[0], w_up[0]], axis=1)
-    full_joined, full_down = (
-        lax.all_gather(local_joined, "dp", axis=0, tiled=True),
-        lax.all_gather(w_down[0], "dp", axis=1, tiled=True),
+    groups = lax.axis_size("dp")
+    rows_in, grads_in, full_joined, full_down = forward_exchange(
+        send_inputs, send_grads, w_gate[0], w_up[0], w_down[0], groups, 0
     )
     preact = lax.dot_general(
         rows_in, full_joined, (((2,), (0,)), ((), ())), preferred_element_type=jnp.float32
@@ -282,20 +396,17 @@
     down_part = lax.dot_general(
         activated, grads_in, (((0, 1), (0, 1)), ((), ())), preferred_element_type=jnp.float32
     ).astype(jnp.bfloat16)
-    returned, down_grad = return_and_reduce(slot_grad, down_part, lax.axis_size("dp"), 1)
-    down_grad = down_grad[None]
+    joined_part = lax.dot_general(
+        rows_in, both_sides, (((0, 1), (0, 1)), ((), ())), preferred_element_type=jnp.float32
+    ).astype(jnp.bfloat16)
+    returned, down_grad, gate_grad, up_grad = return_and_reduce(
+        slot_grad, down_part, joined_part, groups, 1
+    )
     picked = returned[flat_ids, ranking].astype(jnp.float32).reshape(tok_rows, per_token, model_width)
     input_grad = jnp.sum(picked, axis=1).astype(jnp.bfloat16)
-    joined_grad = lax.psum_scatter(
-        lax.dot_general(
-            rows_in, both_sides, (((0, 1), (0, 1)), ((), ())), preferred_element_type=jnp.float32
-        ).astype(jnp.bfloat16),
-        "dp",
-        scatter_dimension=0,
-        tiled=True,
-    )
-    gate_grad = joined_grad[:, :hidden][None]
-    up_grad = joined_grad[:, hidden:][None]
+    down_grad = down_grad[None]
+    gate_grad = gate_grad[None]
+    up_grad = up_grad[None]
     return (input_grad, gate_grad, up_grad, down_grad)
 
 

time: 363 us -> 344 us (0.948)
  between operations: 14 us -> 0.84 us
  transfers between devices with their start and end apart: 3 -> 0, of which waited for: 0 -> 0; matrix products, arithmetic and copies ran while one was open for 8% -> 0% of each run, Pallas kernels for 83% -> 0%
where the time goes in v5:
time: 344 us; the launch traced here: 343 us
  Pallas kernels  303 us (88%)
  local copies, waits for them, and re-layouts  20.1 us (6%)
  matrix products  15.7 us (5%)
  other arithmetic  3.67 us (1%)
    pallas_call x1, Pallas kernels, forward_exchange(): pl.pallas_call(functools.partial(forward_kernel, n, groups), out_shape=[j...  203 us
    pallas_call x1, Pallas kernels, return_and_reduce(): pl.pallas_call(functools.partial(return_kernel, n, groups), out_shape=[ja...  100 us

profile of v5, /device:TPU:1, one launch (start us, length us, event | category | flops | bytes accessed | tf_op | source)
XLA Modules:
  0.0 343.1 jit_solution(5783481919523385734)
XLA Ops:
  0.6 0.0 copy-start.1
  0.6 0.8 fusion.15
  1.4 0.2 reduce_window_sum.11
  1.6 0.8 select_reduce_fusion
  2.5 0.7 fusion.24
  3.1 1.0 scatter_custom_fusion
  4.1 0.1 reshape.74
  4.3 0.1 reshape.77
  4.4 1.2 multiply_convert_fusion
  5.7 0.0 copy-done.1
  5.7 2.5 gather_fusion
  8.2 1.6 reshape.76.inputs_ref
  9.8 2.4 gather_fusion.1
  12.3 1.6 reshape.84.grads_ref
  13.9 202.5 %shard_map.102 = (bf16[64,6,2048]{2,1,0:T(8,128)(2,1)}, bf16[64,6,2048]{2,1,0:T(8,128)(2,1)}, bf16[2048,768]{1,0:T(8,128)(2,1)}, bf16[384,2048]{1,0:T(8,128)(2,1)}) custom-call(bf16[64,6,2048]{2,1,0:T(8,128)(2,1)} %reshape.76.inputs_ref, bf16[64,6,2048]{2,1,0:T(8,128)(2,1)} %reshape.84.grads_ref, bf16[256,384]{1,0:T(8,128)(2,1)} %bitcast.39, ...), custom_call_target="tpu_custom_call" | custom-call | tf_op jit(solution)/shard_map/pallas_call | solution.py:125
  216.5 0.0 copy-start.6
  216.5 0.0 copy-start.7
  216.5 5.5 %fusion.2 = f32[64,6,768]{2,0,1:T(8,128)S(1)} fusion(bf16[2048,768]{1,0:T(8,128)(2,1)} %get-tuple-element.15, bf16[64,6,2048]{2,1,0:T(8,128)(2,1)} %get-tuple-element.14), kind=kOutput, calls=%fused_computation.8 | convolution fusion | flops 1207959552 | bytes 5898240 | tf_op jit(solution)/shard_map/dot_general | solution.py:377
  222.0 0.0 copy-done.6
  222.0 0.0 copy-done.7
  222.0 1.4 multiply_convert_fusion.3
  223.4 0.0 copy-start.4
  223.4 3.5 %bitcast_convert_fusion.1.part_ref = bf16[384,2048]{1,0:T(8,128)(2,1)} fusion(bf16[64,6,2048]{2,1,0:T(8,128)(2,1)S(1)} %copy-done.6, f32[64,6,768]{2,0,1:T(8,128)S(1)} %fusion.2), kind=kOutput, calls=%fused_computation.5 | convolution fusion | flops 605650944 | bytes 4325376 | tf_op jit(solution)/shard_map/dot_general | solution.py:396
  226.9 0.0 copy-done.4
  226.9 0.0 copy-start.5
  226.9 1.4 fusion.4
  228.3 0.2 copy-done.5
  228.5 3.9 %bitcast_convert_fusion.joined_ref = bf16[2048,768]{1,0:T(8,128)(2,1)} fusion(bf16[64,6,2048]{2,1,0:T(8,128)(2,1)S(1)} %copy-done.5, bf16[64,6,384]{2,0,1:T(8,128)(2,1)S(1)} %get-tuple-element.21, bf16[64,6,384]{2,0,1:T(8,128)(2,1)S(1)} %get-tuple-element.20), kind=kOutput, calls=%fused_computation.4 | convolution fusion | flops 1210712064 | bytes 5308416 | tf_op jit(solution)/shard_map/dot_general | solution.py:399
  232.4 2.2 copy.27.slot_ref
  234.7 100.2 %shard_map.103 = (bf16[64,6,2048]{2,1,0:T(8,128)(2,1)}, bf16[384,2048]{1,0:T(8,128)(2,1)}, bf16[256,384]{1,0:T(8,128)(2,1)}, bf16[256,384]{1,0:T(8,128)(2,1)}) custom-call(bf16[64,6,2048]{2,1,0:T(8,128)(2,1)} %copy.27.slot_ref, bf16[384,2048]{1,0:T(8,128)(2,1)} %bitcast_convert_fusion.1.part_ref, bf16[2048,768]{1,0:T(8,128)(2,1)} %bitcast_convert_fusion.joined_ref), custom_call_target="tpu_custom_call" | custom-call | tf_op jit(solution)/shard_map/pallas_call | solution.py:310
  334.9 2.5 copy.28
  337.3 0.0 copy-start.3
  337.3 0.0 copy-start.2
  337.3 0.0 copy-start
  337.4 3.2 gather_fusion.2
  340.6 0.0 copy-done.3
  340.6 0.7 copy.42
  341.3 0.0 copy-done.2
  341.3 0.7 copy.43
  341.9 0.0 copy-done
  341.9 1.1 copy.44
  (5 shorter events, 0.1 us)
Async XLA Ops:
  0.6 5.0 %copy-start.1 = (bf16[128,2048]{1,0:T(8,128)(2,1)S(1)}, bf16[128,2048]{1,0:T(8,128)(2,1)}, u32[]{:S(2)}) copy-start(bf16[128,2048]{1,0:T(8,128)(2,1)} %param.7) | copy-start | bytes 1572868
  216.5 5.6 %copy-start.6 = (bf16[64,6,2048]{2,1,0:T(8,128)(2,1)S(1)}, bf16[64,6,2048]{2,1,0:T(8,128)(2,1)}, u32[]{:S(2)}) copy-start(bf16[64,6,2048]{2,1,0:T(8,128)(2,1)} %get-tuple-element.12) | copy-start | bytes 4718596
  216.5 5.6 %copy-start.7 = (bf16[384,2048]{1,0:T(8,128)(2,1)S(1)}, bf16[384,2048]{1,0:T(8,128)(2,1)}, u32[]{:S(2)}) copy-start(bf16[384,2048]{1,0:T(8,128)(2,1)} %get-tuple-element.13) | copy-start | bytes 4718596
  223.4 3.5 %copy-start.4 = (bf16[2048,768]{1,0:T(8,128)(2,1)S(1)}, bf16[2048,768]{1,0:T(8,128)(2,1)}, u32[]{:S(2)}) copy-start(bf16[2048,768]{1,0:T(8,128)(2,1)} %get-tuple-element.15) | copy-start | bytes 9437188
  226.9 1.6 copy-start.5
  337.3 3.2 copy-start.3
  337.3 3.9 %copy-start.2 = (bf16[256,384]{1,0:T(8,128)(2,1)S(1)}, bf16[256,384]{1,0:T(8,128)(2,1)}, u32[]{:S(2)}) copy-start(bf16[256,384]{1,0:T(8,128)(2,1)} %get-tuple-element.18) | copy-start | bytes 589828
  337.3 4.6 %copy-start = (bf16[384,2048]{1,0:T(8,128)(2,1)S(1)}, bf16[384,2048]{1,0:T(8,128)(2,1)}, u32[]{:S(2)}) copy-start(bf16[384,2048]{1,0:T(8,128)(2,1)} %get-tuple-element.19) | copy-start | bytes 4718596

commit v6 on v5

--- a/solution.py
+++ b/solution.py
@@ -402,8 +402,16 @@
     returned, down_grad, gate_grad, up_grad = return_and_reduce(
         slot_grad, down_part, joined_part, groups, 1
     )
-    picked = returned[flat_ids, ranking].astype(jnp.float32).reshape(tok_rows, per_token, model_width)
-    input_grad = jnp.sum(picked, axis=1).astype(jnp.bfloat16)
+    owner = (
+        (flat_ids[:, None, None] == jnp.arange(expert_count, dtype=jnp.int32)[None, :, None])
+        & (ranking[:, None, None] == jnp.arange(slot_depth, dtype=jnp.int32)[None, None, :])
+    ).astype(jnp.bfloat16)
+    input_grad = lax.dot_general(
+        owner.reshape(tok_rows, per_token, expert_count, slot_depth).sum(axis=1),
+        returned,
+        (((1, 2), (0, 1)), ((), ())),
+        preferred_element_type=jnp.float32,
+    ).astype(jnp.bfloat16)
     down_grad = down_grad[None]
     gate_grad = gate_grad[None]
     up_grad = up_grad[None]

time: 344 us -> 343 us (level)
  local copies, waits for them, and re-layouts: 20.1 us -> 14.5 us
  matrix products: 15.7 us -> 20.1 us
    dot_general x0 -> x1, matrix products: none -> 4.4 us  [on_device(): lax.dot_general(owner.reshape(tok_rows, per_token, expert_count, slot_dep...]
where the time goes in v6:
time: 343 us; the launch traced here: 342 us
  Pallas kernels  303 us (88%)
  matrix products  20.1 us (6%)
  local copies, waits for them, and re-layouts  14.5 us (4%)
  other arithmetic  3.68 us (1%)
    pallas_call x1, Pallas kernels, forward_exchange(): pl.pallas_call(functools.partial(forward_kernel, n, groups), out_shape=[j...  203 us
    pallas_call x1, Pallas kernels, return_and_reduce(): pl.pallas_call(functools.partial(return_kernel, n, groups), out_shape=[ja...  100 us

profile of v6, /device:TPU:1, one launch (start us, length us, event | category | flops | bytes accessed | tf_op | source)
XLA Modules:
  0.0 341.9 jit_solution(1356917508639987885)
XLA Ops:
  0.6 0.0 copy-start.1
  0.6 0.8 iota_compare_fusion
  1.5 0.1 copy.25
  1.6 0.2 reduce_window_sum.11
  1.7 0.8 select_reduce_fusion
  2.6 0.7 fusion.23
  3.2 1.0 scatter_custom_fusion
  4.2 0.1 reshape.109
  4.4 0.1 reshape.112
  4.5 1.2 multiply_convert_fusion
  5.8 0.0 copy-done.1
  5.8 0.1 concatenate.9
  5.8 2.5 gather_fusion
  8.3 1.6 reshape.111.inputs_ref
  9.9 2.4 gather_fusion.1
  12.4 1.6 reshape.119.grads_ref
  14.0 202.5 %shard_map.105 = (bf16[64,6,2048]{2,1,0:T(8,128)(2,1)}, bf16[64,6,2048]{2,1,0:T(8,128)(2,1)}, bf16[2048,768]{1,0:T(8,128)(2,1)}, bf16[384,2048]{1,0:T(8,128)(2,1)}) custom-call(bf16[64,6,2048]{2,1,0:T(8,128)(2,1)} %reshape.111.inputs_ref, bf16[64,6,2048]{2,1,0:T(8,128)(2,1)} %reshape.119.grads_ref, bf16[256,384]{1,0:T(8,128)(2,1)} %bitcast.38, ...), custom_call_target="tpu_custom_call" | custom-call | tf_op jit(solution)/shard_map/pallas_call | solution.py:125
  216.6 0.0 copy-start.6
  216.6 0.0 copy-start.7
  216.6 5.5 %fusion.2 = f32[64,6,768]{2,0,1:T(8,128)S(1)} fusion(bf16[2048,768]{1,0:T(8,128)(2,1)} %get-tuple-element.15, bf16[64,6,2048]{2,1,0:T(8,128)(2,1)} %get-tuple-element.14), kind=kOutput, calls=%fused_computation.7 | convolution fusion | flops 1207959552 | bytes 5898240 | tf_op jit(solution)/shard_map/dot_general | solution.py:377
  222.1 0.0 copy-done.6
  222.1 0.0 copy-done.7
  222.2 1.4 multiply_convert_fusion.3
  223.5 0.0 copy-start.4
  223.5 3.4 %bitcast_convert_fusion.1.part_ref = bf16[384,2048]{1,0:T(8,128)(2,1)} fusion(bf16[64,6,2048]{2,1,0:T(8,128)(2,1)S(1)} %copy-done.6, f32[64,6,768]{2,0,1:T(8,128)S(1)} %fusion.2), kind=kOutput, calls=%fused_computation.4 | convolution fusion | flops 605650944 | bytes 4325376 | tf_op jit(solution)/shard_map/dot_general | solution.py:396
  227.0 0.0 copy-done.4
  227.0 0.0 copy-start.5
  227.0 1.4 fusion.4
  228.4 0.2 copy-done.5
  228.6 3.9 %bitcast_convert_fusion.joined_ref = bf16[2048,768]{1,0:T(8,128)(2,1)} fusion(bf16[64,6,2048]{2,1,0:T(8,128)(2,1)S(1)} %copy-done.5, bf16[64,6,384]{2,0,1:T(8,128)(2,1)S(1)} %get-tuple-element.21, bf16[64,6,384]{2,0,1:T(8,128)(2,1)S(1)} %get-tuple-element.20), kind=kOutput, calls=%fused_computation.3 | convolution fusion | flops 1210712064 | bytes 5308416 | tf_op jit(solution)/shard_map/dot_general | solution.py:399
  232.5 2.2 copy.30.slot_ref
  234.7 100.2 %shard_map.106 = (bf16[64,6,2048]{2,1,0:T(8,128)(2,1)}, bf16[384,2048]{1,0:T(8,128)(2,1)}, bf16[256,384]{1,0:T(8,128)(2,1)}, bf16[256,384]{1,0:T(8,128)(2,1)}) custom-call(bf16[64,6,2048]{2,1,0:T(8,128)(2,1)} %copy.30.slot_ref, bf16[384,2048]{1,0:T(8,128)(2,1)} %bitcast_convert_fusion.1.part_ref, bf16[2048,768]{1,0:T(8,128)(2,1)} %bitcast_convert_fusion.joined_ref), custom_call_target="tpu_custom_call" | custom-call | tf_op jit(solution)/shard_map/pallas_call | solution.py:310
  335.0 0.0 copy-start.3
  335.0 0.0 copy-start.2
  335.0 0.0 copy-start
  335.0 4.4 %fusion.7 = bf16[128,2048]{1,0:T(8,128)(2,1)} fusion(bf16[64,6,2048]{2,1,0:T(8,128)(2,1)} %get-tuple-element.16, pred[128,6]{0,1:T(8,128)(4,1)S(1)} %iota_compare_fusion.1, pred[128,64]{0,1:T(8,128)(4,1)S(1)} %copy.25), kind=kOutput, calls=%fused_computation.11 | convolution fusion | flops 201637888 | bytes 2106112 | tf_op jit(solution)/shard_map/dot_general | solution.py:409
  339.4 0.0 copy-done.3
  339.4 0.7 copy.47
  340.1 0.0 copy-done.2
  340.1 0.7 copy.48
  340.8 0.0 copy-done
  340.8 1.1 copy.49
  (5 shorter events, 0.1 us)
Async XLA Ops:
  0.6 5.1 %copy-start.1 = (bf16[128,2048]{1,0:T(8,128)(2,1)S(1)}, bf16[128,2048]{1,0:T(8,128)(2,1)}, u32[]{:S(2)}) copy-start(bf16[128,2048]{1,0:T(8,128)(2,1)} %param.7) | copy-start | bytes 1572868
  216.6 5.6 %copy-start.6 = (bf16[64,6,2048]{2,1,0:T(8,128)(2,1)S(1)}, bf16[64,6,2048]{2,1,0:T(8,128)(2,1)}, u32[]{:S(2)}) copy-start(bf16[64,6,2048]{2,1,0:T(8,128)(2,1)} %get-tuple-element.12) | copy-start | bytes 4718596
  216.6 5.6 %copy-start.7 = (bf16[384,2048]{1,0:T(8,128)(2,1)S(1)}, bf16[384,2048]{1,0:T(8,128)(2,1)}, u32[]{:S(2)}) copy-start(bf16[384,2048]{1,0:T(8,128)(2,1)} %get-tuple-element.13) | copy-start | bytes 4718596
  223.5 3.4 %copy-start.4 = (bf16[2048,768]{1,0:T(8,128)(2,1)S(1)}, bf16[2048,768]{1,0:T(8,128)(2,1)}, u32[]{:S(2)}) copy-start(bf16[2048,768]{1,0:T(8,128)(2,1)} %get-tuple-element.15) | copy-start | bytes 9437188
  227.0 1.6 copy-start.5
  335.0 4.4 %copy-start.3 = (bf16[256,384]{1,0:T(8,128)(2,1)S(1)}, bf16[256,384]{1,0:T(8,128)(2,1)}, u32[]{:S(2)}) copy-start(bf16[256,384]{1,0:T(8,128)(2,1)} %get-tuple-element.17) | copy-start | bytes 589828
  335.0 5.1 %copy-start.2 = (bf16[256,384]{1,0:T(8,128)(2,1)S(1)}, bf16[256,384]{1,0:T(8,128)(2,1)}, u32[]{:S(2)}) copy-start(bf16[256,384]{1,0:T(8,128)(2,1)} %get-tuple-element.18) | copy-start | bytes 589828
  335.0 5.8 %copy-start = (bf16[384,2048]{1,0:T(8,128)(2,1)S(1)}, bf16[384,2048]{1,0:T(8,128)(2,1)}, u32[]{:S(2)}) copy-start(bf16[384,2048]{1,0:T(8,128)(2,1)} %get-tuple-element.19) | copy-start | bytes 4718596

commit v7 on v5

--- a/solution.py
+++ b/solution.py
@@ -9,7 +9,7 @@
 MESH = pl.DeviceIdType.MESH
 
 
-def forward_kernel(n, groups, inputs_ref, grads_ref, wg_ref, wu_ref, wd_ref, inputs_out,
+def forward_kernel(n, groups, depth, inputs_ref, grads_ref, wg_ref, wu_ref, wd_ref, inputs_out,
                    grads_out, joined_out, down_out, send_sem, recv_sem, local_sem, ag_send,
                    ag_recv, own_sem):
     me = lax.axis_index("expert")
@@ -35,7 +35,9 @@
     sources = (inputs_ref, grads_ref)
     targets = (inputs_out, grads_out)
     local = [
-        pltpu.make_async_copy(sources[a].at[me], targets[a].at[me], local_sem.at[a])
+        pltpu.make_async_copy(
+            sources[a].at[me, pl.ds(0, depth)], targets[a].at[me, pl.ds(0, depth)], local_sem.at[a]
+        )
         for a in range(2)
     ]
     for copy in local:
@@ -43,8 +45,8 @@
 
     def remote(a, peer, slot):
         return pltpu.make_async_remote_copy(
-            src_ref=sources[a].at[peer],
-            dst_ref=targets[a].at[slot],
+            src_ref=sources[a].at[peer, pl.ds(0, depth)],
+            dst_ref=targets[a].at[slot, pl.ds(0, depth)],
             send_sem=send_sem.at[a, peer],
             recv_sem=recv_sem.at[a, slot],
             device_id=(row, peer),
@@ -119,11 +121,11 @@
         copy.wait()
 
 
-def forward_exchange(send_inputs, send_grads, wg, wu, wd, groups, collective_id):
+def forward_exchange(send_inputs, send_grads, wg, wu, wd, groups, depth, collective_id):
     n = send_inputs.shape[0]
     any_spec = pl.BlockSpec(memory_space=pl.ANY)
     return pl.pallas_call(
-        functools.partial(forward_kernel, n, groups),
+        functools.partial(forward_kernel, n, groups, depth),
         out_shape=[
             jax.ShapeDtypeStruct(send_inputs.shape, send_inputs.dtype),
             jax.ShapeDtypeStruct(send_grads.shape, send_grads.dtype),
@@ -146,7 +148,7 @@
     )(send_inputs, send_grads, wg, wu, wd)
 
 
-def return_kernel(n, groups, slot_ref, part_ref, joined_ref, out_ref, down_ref, gate_ref, up_ref,
+def return_kernel(n, groups, depth, slot_ref, part_ref, joined_ref, out_ref, down_ref, gate_ref, up_ref,
                   send_sem, recv_sem, local_sem, rs_send, rs_recv, ag_send, ag_recv, js_send,
                   js_recv, own_sem, parts, reduced, joined_parts, joined_sum):
     me = lax.axis_index("expert")
@@ -169,13 +171,15 @@
     lax.fori_loop(1, n, greet, 0)
     lax.fori_loop(1, groups, greet_group, 0)
     pl.semaphore_wait(barrier, n - 1 + groups - 1)
-    local = pltpu.make_async_copy(slot_ref.at[me], out_ref.at[me], local_sem)
+    local = pltpu.make_async_copy(
+        slot_ref.at[me, pl.ds(0, depth)], out_ref.at[me, pl.ds(0, depth)], local_sem
+    )
     local.start()
 
     def remote(peer, slot):
         return pltpu.make_async_remote_copy(
-            src_ref=slot_ref.at[peer],
-            dst_ref=out_ref.at[slot],
+            src_ref=slot_ref.at[peer, pl.ds(0, depth)],
+            dst_ref=out_ref.at[slot, pl.ds(0, depth)],
             send_sem=send_sem.at[peer],
             recv_sem=recv_sem.at[slot],
             device_id=(row, peer),
@@ -301,14 +305,14 @@
     local.wait()
 
 
-def return_and_reduce(slot_grad, down_part, joined_part, groups, collective_id):
+def return_and_reduce(slot_grad, down_part, joined_part, groups, depth, collective_id):
     n = slot_grad.shape[0]
     rows = down_part.shape[0] // groups
     joined_rows = joined_part.shape[0] // groups
     width = joined_part.shape[1] // 2
     any_spec = pl.BlockSpec(memory_space=pl.ANY)
     return pl.pallas_call(
-        functools.partial(return_kernel, n, groups),
+        functools.partial(return_kernel, n, groups, depth),
         out_shape=[
             jax.ShapeDtypeStruct(slot_grad.shape, slot_grad.dtype),
             jax.ShapeDtypeStruct(down_part.shape, down_part.dtype),
@@ -341,20 +345,22 @@
 
 def on_device(tokens, out_grad, expert_ids, gates, w_gate, w_up, w_down):
     expert_count = lax.axis_size("expert")
+    groups = lax.axis_size("dp")
     tok_rows = tokens.shape[0]
     model_width = tokens.shape[1]
     per_token = expert_ids.shape[1]
     hidden = w_gate.shape[2]
     entries = tok_rows * per_token
     slot_depth = 3 * entries // expert_count
-    slot_count = expert_count * slot_depth
+    block = 8 * pl.cdiv(slot_depth, 8)
+    slot_count = expert_count * block
     flat_ids = expert_ids.reshape(entries)
     onehot = (flat_ids[:, None] == jnp.arange(expert_count, dtype=jnp.int32)[None, :]).astype(
         jnp.int32
     )
     before = jnp.cumsum(onehot, axis=0) - onehot
     ranking = jnp.sum(before * onehot, axis=1)
-    slot_of_entry = flat_ids * slot_depth + ranking
+    slot_of_entry = flat_ids * block + ranking
     source = (
         jnp.full((slot_count,), entries, jnp.int32)
         .at[slot_of_entry]
@@ -367,21 +373,22 @@
     )
     grad_table = jnp.concatenate([entry_scaled, jnp.zeros((1, model_width), jnp.bfloat16)], axis=0)
     input_table = jnp.concatenate([tokens, jnp.zeros((1, model_width), tokens.dtype)], axis=0)
-    picks = source.reshape(expert_count, slot_depth)
-    send_grads = grad_table[picks]
-    send_inputs = input_table[picks // per_token]
-    groups = lax.axis_size("dp")
+    send_grads = grad_table[source].reshape(expert_count, block, model_width)
+    send_inputs = input_table[source // per_token].reshape(expert_count, block, model_width)
     rows_in, grads_in, full_joined, full_down = forward_exchange(
-        send_inputs, send_grads, w_gate[0], w_up[0], w_down[0], groups, 0
-    )
-    preact = lax.dot_general(
-        rows_in, full_joined, (((2,), (0,)), ((), ())), preferred_element_type=jnp.float32
-    )
+        send_inputs, send_grads, w_gate[0], w_up[0], w_down[0], groups, slot_depth, 0
+    )
+    filled = (jnp.arange(slot_count, dtype=jnp.int32) % block < slot_depth)[:, None]
+    rows_in = jnp.where(filled, rows_in.reshape(slot_count, model_width), 0).astype(tokens.dtype)
+    grads_in = jnp.where(filled, grads_in.reshape(slot_count, model_width), 0).astype(
+        jnp.bfloat16
+    )
+    preact = jnp.dot(rows_in, full_joined, preferred_element_type=jnp.float32)
     hidden_grad = lax.dot_general(
-        grads_in, full_down, (((2,), (1,)), ((), ())), preferred_element_type=jnp.float32
-    )
-    gate_pre = preact[:, :, :hidden]
-    up_pre = preact[:, :, hidden:]
+        grads_in, full_down, (((1,), (1,)), ((), ())), preferred_element_type=jnp.float32
+    )
+    gate_pre = preact[:, :hidden]
+    up_pre = preact[:, hidden:]
     sigmoid = jax.nn.sigmoid(gate_pre)
     silu_value = gate_pre * sigmoid
     activated = (silu_value * up_pre).astype(jnp.bfloat16)
@@ -389,25 +396,28 @@
         jnp.bfloat16
     )
     up_side = (hidden_grad * silu_value).astype(jnp.bfloat16)
-    both_sides = jnp.concatenate([gate_side, up_side], axis=2)
+    both_sides = jnp.concatenate([gate_side, up_side], axis=1)
     slot_grad = lax.dot_general(
-        both_sides, full_joined, (((2,), (1,)), ((), ())), preferred_element_type=jnp.float32
+        both_sides, full_joined, (((1,), (1,)), ((), ())), preferred_element_type=jnp.float32
     ).astype(jnp.bfloat16)
     down_part = lax.dot_general(
-        activated, grads_in, (((0, 1), (0, 1)), ((), ())), preferred_element_type=jnp.float32
+        activated, grads_in, (((0,), (0,)), ((), ())), preferred_element_type=jnp.float32
     ).astype(jnp.bfloat16)
     joined_part = lax.dot_general(
-        rows_in, both_sides, (((0, 1), (0, 1)), ((), ())), preferred_element_type=jnp.float32
+        rows_in, both_sides, (((0,), (0,)), ((), ())), preferred_element_type=jnp.float32
     ).astype(jnp.bfloat16)
     returned, down_grad, gate_grad, up_grad = return_and_reduce(
-        slot_grad, down_part, joined_part, groups, 1
-    )
-    picked = returned[flat_ids, ranking].astype(jnp.float32).reshape(tok_rows, per_token, model_width)
+        slot_grad.reshape(expert_count, block, model_width),
+        down_part,
+        joined_part,
+        groups,
+        slot_depth,
+        1,
+    )
+    picked = returned.reshape(slot_count, model_width)[slot_of_entry]
+    picked = picked.astype(jnp.float32).reshape(tok_rows, per_token, model_width)
     input_grad = jnp.sum(picked, axis=1).astype(jnp.bfloat16)
-    down_grad = down_grad[None]
-    gate_grad = gate_grad[None]
-    up_grad = up_grad[None]
-    return (input_grad, gate_grad, up_grad, down_grad)
+    return (input_grad, gate_grad[None], up_grad[None], down_grad[None])
 
 
 def solution(mesh):

time: 344 us -> 274 us (0.80)
  Pallas kernels: 303 us -> 239 us
  local copies, waits for them, and re-layouts: 20.1 us -> 14.7 us
    pallas_call x2, Pallas kernels: 303 us -> 239 us  [the longest x1 157 us: forward_exchange(): pl.pallas_call(functools.partial(forward_kernel, n, groups, depth), out_s...]
    gather x5 -> x3, local copies, waits for them, and re-layouts: 11.4 us -> 10.8 us  [the longest x1 4.23 us: on_device(): picked = returned.reshape(slot_count, model_width)[slot_of_entry]]
where the time goes in v7:
time: 274 us; the launch traced here: 273 us
  Pallas kernels  239 us (87%)
  matrix products  15 us (5%)
  local copies, waits for them, and re-layouts  14.7 us (5%)
  other arithmetic  3.63 us (1%)
    pallas_call x1, Pallas kernels, forward_exchange(): pl.pallas_call(functools.partial(forward_kernel, n, groups, depth), out_s...  157 us
    pallas_call x1, Pallas kernels, return_and_reduce(): pl.pallas_call(functools.partial(return_kernel, n, groups, depth), out_sh...  81.8 us

profile of v7, /device:TPU:1, one launch (start us, length us, event | category | flops | bytes accessed | tf_op | source)
XLA Modules:
  0.0 273.4 jit_solution(13755151016319614297)
XLA Ops:
  0.6 0.7 fusion.5
  1.4 0.2 reduce_window_sum.11
  1.5 0.8 select_reduce_fusion
  2.4 0.7 fusion.12
  3.0 1.0 scatter_custom_fusion
  4.1 1.2 multiply_convert_fusion
  5.3 0.0 copy-start.1
  5.3 3.3 %gather_fusion.1 = bf16[512,2048]{1,0:T(8,128)(2,1)} fusion(bf16[129,2048]{1,0:T(8,128)(2,1)S(1)} %concatenate.10, s32[1024]{0:T(1024)S(1)} %pad_clamp_fusion.1), kind=kCustom, calls=%fused_computation.1 | custom fusion | bytes 4196352 | tf_op jit(solution)/shard_map/gather | solution.py:376
  8.6 0.0 copy-done.1
  8.7 3.3 %gather_fusion = bf16[512,2048]{1,0:T(8,128)(2,1)} fusion(bf16[129,2048]{1,0:T(8,128)(2,1)S(1)} %concatenate.9, s32[1024]{0:T(1024)S(1)} %pad_clamp_fusion.1), kind=kCustom, calls=%fused_computation | custom fusion | bytes 4196352 | tf_op jit(solution)/shard_map/gather | solution.py:377
  12.0 157.4 %shard_map.102 = (bf16[64,8,2048]{2,1,0:T(8,128)(2,1)}, bf16[64,8,2048]{2,1,0:T(8,128)(2,1)}, bf16[2048,768]{1,0:T(8,128)(2,1)}, bf16[384,2048]{1,0:T(8,128)(2,1)}) custom-call(bf16[64,8,2048]{2,1,0:T(8,128)(2,1)} %bitcast.33, bf16[64,8,2048]{2,1,0:T(8,128)(2,1)} %bitcast.32, bf16[256,384]{1,0:T(8,128)(2,1)} %bitcast.36, bf16[256,384]{1,0:T(8,128)(2,1)} %bitcast.37, ...), custom_call_target="tpu_custom_call" | custom-call | tf_op jit(solution)/shard_map/pallas_call | solution.py:127
  169.4 0.0 copy-start.5
  169.4 0.0 copy-start.7
  169.4 4.6 %fusion.2 = f32[512,768]{0,1:T(8,128)S(1)} fusion(bf16[2048,768]{1,0:T(8,128)(2,1)} %get-tuple-element.15, bf16[64,8,2048]{2,1,0:T(8,128)(2,1)} %get-tuple-element.14, pred[512]{0:T(512)(128)(4,1)S(1)} %fusion.6), kind=kOutput, calls=%fused_computation.12 | convolution fusion | flops 1611661312 | bytes 6816256 | tf_op jit(solution)/shard_map/dot_general | solution.py:386
  174.0 0.0 copy-done.5
  174.0 0.0 copy-done.7
  174.0 0.0 copy-start.6
  174.1 1.3 multiply_convert_fusion.3
  175.4 0.3 copy-done.6
  175.6 0.0 copy-start.4
  175.6 3.7 %convolution_convert_fusion.joined_ref = bf16[2048,768]{1,0:T(8,128)(2,1)} fusion(bf16[64,8,2048]{2,1,0:T(8,128)(2,1)S(1)} %copy-done.6, pred[512]{0:T(512)(128)(4,1)S(1)} %fusion.6, bf16[512,384]{0,1:T(8,128)(2,1)S(1)} %get-tuple-element.21, bf16[512,384]{0,1:T(8,128)(2,1)S(1)} %get-tuple-element.20), kind=kOutput, calls=%fused_computation.4 | convolution fusion | flops 1614807040 | bytes 6029824 | tf_op jit(solution)/shard_map/dot_general | solution.py:406
  179.4 0.0 copy-done.4
  179.4 3.2 %fusion.slot_ref = bf16[64,8,2048]{2,1,0:T(8,128)(2,1)} fusion(bf16[2048,768]{1,0:T(8,128)(2,1)S(1)} %copy-done.4, bf16[512,384]{0,1:T(8,128)(2,1)S(1)} %get-tuple-element.21, bf16[512,384]{0,1:T(8,128)(2,1)S(1)} %get-tuple-element.20), kind=kOutput, calls=%fused_computation.7 | convolution fusion | flops 1613234176 | bytes 6029312 | tf_op jit(solution)/shard_map/dot_general | solution.py:400
  182.5 2.3 convolution_convert_fusion.2.part_ref
  184.8 81.8 %shard_map.103 = (bf16[64,8,2048]{2,1,0:T(8,128)(2,1)}, bf16[384,2048]{1,0:T(8,128)(2,1)}, bf16[256,384]{1,0:T(8,128)(2,1)}, bf16[256,384]{1,0:T(8,128)(2,1)}) custom-call(bf16[64,8,2048]{2,1,0:T(8,128)(2,1)} %fusion.slot_ref, bf16[384,2048]{1,0:T(8,128)(2,1)} %convolution_convert_fusion.2.part_ref, bf16[2048,768]{1,0:T(8,128)(2,1)} %convolution_convert_fusion.joined_ref), custom_call_target="tpu_custom_call" | custom-call | tf_op jit(solution)/shard_map/pallas_call | solution.py:314
  266.7 0.0 copy-start.3
  266.7 0.0 copy-start.2
  266.7 0.0 copy-start
  266.7 4.2 %gather_fusion.2 = bf16[128,2048]{1,0:T(8,128)(2,1)} fusion(bf16[512,2048]{1,0:T(8,128)(2,1)} %bitcast.34, s32[1024]{0:T(1024)S(1)} %pad_clamp_fusion), kind=kCustom, calls=%fused_computation.2 | custom fusion | bytes 1049088 | tf_op jit(solution)/shard_map/gather | solution.py:417
  270.9 0.0 copy-done.3
  270.9 0.7 copy.17
  271.6 0.0 copy-done.2
  271.6 0.7 copy.18
  272.3 0.0 copy-done
  272.3 1.1 copy.19
  (7 shorter events, 0.1 us)
Async XLA Ops:
  5.3 3.3 %copy-start.1 = (bf16[128,2048]{1,0:T(8,128)(2,1)S(1)}, bf16[128,2048]{1,0:T(8,128)(2,1)}, u32[]{:S(2)}) copy-start(bf16[128,2048]{1,0:T(8,128)(2,1)} %param.7) | copy-start | bytes 1572868
  169.4 4.6 %copy-start.5 = (bf16[64,8,2048]{2,1,0:T(8,128)(2,1)S(1)}, bf16[64,8,2048]{2,1,0:T(8,128)(2,1)}, u32[]{:S(2)}) copy-start(bf16[64,8,2048]{2,1,0:T(8,128)(2,1)} %get-tuple-element.12) | copy-start | bytes 6291460
  169.4 4.6 %copy-start.7 = (bf16[384,2048]{1,0:T(8,128)(2,1)S(1)}, bf16[384,2048]{1,0:T(8,128)(2,1)}, u32[]{:S(2)}) copy-start(bf16[384,2048]{1,0:T(8,128)(2,1)} %get-tuple-element.13) | copy-start | bytes 4718596
  174.0 1.6 copy-start.6
  175.6 3.7 %copy-start.4 = (bf16[2048,768]{1,0:T(8,128)(2,1)S(1)}, bf16[2048,768]{1,0:T(8,128)(2,1)}, u32[]{:S(2)}) copy-start(bf16[2048,768]{1,0:T(8,128)(2,1)} %get-tuple-element.15) | copy-start | bytes 9437188
  266.7 4.3 %copy-start.3 = (bf16[256,384]{1,0:T(8,128)(2,1)S(1)}, bf16[256,384]{1,0:T(8,128)(2,1)}, u32[]{:S(2)}) copy-start(bf16[256,384]{1,0:T(8,128)(2,1)} %get-tuple-element.17) | copy-start | bytes 589828
  266.7 4.9 %copy-start.2 = (bf16[256,384]{1,0:T(8,128)(2,1)S(1)}, bf16[256,384]{1,0:T(8,128)(2,1)}, u32[]{:S(2)}) copy-start(bf16[256,384]{1,0:T(8,128)(2,1)} %get-tuple-element.18) | copy-start | bytes 589828
  266.7 5.6 %copy-start = (bf16[384,2048]{1,0:T(8,128)(2,1)S(1)}, bf16[384,2048]{1,0:T(8,128)(2,1)}, u32[]{:S(2)}) copy-start(bf16[384,2048]{1,0:T(8,128)(2,1)} %get-tuple-element.19) | copy-start | bytes 4718596

commit v8 on v7

--- a/solution.py
+++ b/solution.py
@@ -9,9 +9,8 @@
 MESH = pl.DeviceIdType.MESH
 
 
-def forward_kernel(n, groups, depth, inputs_ref, grads_ref, wg_ref, wu_ref, wd_ref, inputs_out,
-                   grads_out, joined_out, down_out, send_sem, recv_sem, local_sem, ag_send,
-                   ag_recv, own_sem):
+def forward_kernel(n, groups, depth, inputs_ref, wg_ref, wu_ref, wd_ref, inputs_out, joined_out,
+                   down_out, send_sem, recv_sem, local_sem, ag_send, ag_recv, own_sem):
     me = lax.axis_index("expert")
     row = lax.axis_index("dp")
     width = wg_ref.shape[1]
@@ -32,13 +31,13 @@
     lax.fori_loop(1, n, greet, 0)
     lax.fori_loop(1, groups, greet_group, 0)
     pl.semaphore_wait(barrier, n - 1 + groups - 1)
-    sources = (inputs_ref, grads_ref)
-    targets = (inputs_out, grads_out)
+    sources = (inputs_ref,)
+    targets = (inputs_out,)
     local = [
         pltpu.make_async_copy(
             sources[a].at[me, pl.ds(0, depth)], targets[a].at[me, pl.ds(0, depth)], local_sem.at[a]
         )
-        for a in range(2)
+        for a in range(len(sources))
     ]
     for copy in local:
         copy.start()
@@ -55,7 +54,7 @@
 
     def start(i, carry):
         peer = lax.rem(me + i, n)
-        for a in range(2):
+        for a in range(len(sources)):
             remote(a, peer, me).start()
         return carry
 
@@ -111,7 +110,7 @@
     def finish(i, carry):
         peer = lax.rem(me + i, n)
         source = lax.rem(me + n - i, n)
-        for a in range(2):
+        for a in range(len(sources)):
             remote(a, peer, me).wait_send()
             remote(a, source, source).wait_recv()
         return carry
@@ -121,23 +120,22 @@
         copy.wait()
 
 
-def forward_exchange(send_inputs, send_grads, wg, wu, wd, groups, depth, collective_id):
-    n = send_inputs.shape[0]
+def forward_exchange(send_rows, wg, wu, wd, groups, depth, collective_id):
+    n = send_rows.shape[0]
     any_spec = pl.BlockSpec(memory_space=pl.ANY)
     return pl.pallas_call(
         functools.partial(forward_kernel, n, groups, depth),
         out_shape=[
-            jax.ShapeDtypeStruct(send_inputs.shape, send_inputs.dtype),
-            jax.ShapeDtypeStruct(send_grads.shape, send_grads.dtype),
+            jax.ShapeDtypeStruct(send_rows.shape, send_rows.dtype),
             jax.ShapeDtypeStruct((groups * wg.shape[0], 2 * wg.shape[1]), wg.dtype),
             jax.ShapeDtypeStruct((wd.shape[0], groups * wd.shape[1]), wd.dtype),
         ],
-        in_specs=[any_spec] * 5,
-        out_specs=[any_spec] * 4,
+        in_specs=[any_spec] * 4,
+        out_specs=[any_spec] * 3,
         scratch_shapes=[
-            pltpu.SemaphoreType.DMA((2, n)),
-            pltpu.SemaphoreType.DMA((2, n)),
-            pltpu.SemaphoreType.DMA((2,)),
+            pltpu.SemaphoreType.DMA((1, n)),
+            pltpu.SemaphoreType.DMA((1, n)),
+            pltpu.SemaphoreType.DMA((1,)),
             pltpu.SemaphoreType.DMA((3, groups)),
             pltpu.SemaphoreType.DMA((3, groups)),
             pltpu.SemaphoreType.DMA((3,)),
@@ -145,7 +143,7 @@
         compiler_params=pltpu.CompilerParams(
             collective_id=collective_id, has_side_effects=True
         ),
-    )(send_inputs, send_grads, wg, wu, wd)
+    )(send_rows, wg, wu, wd)
 
 
 def return_kernel(n, groups, depth, slot_ref, part_ref, joined_ref, out_ref, down_ref, gate_ref, up_ref,
@@ -373,16 +371,18 @@
     )
     grad_table = jnp.concatenate([entry_scaled, jnp.zeros((1, model_width), jnp.bfloat16)], axis=0)
     input_table = jnp.concatenate([tokens, jnp.zeros((1, model_width), tokens.dtype)], axis=0)
-    send_grads = grad_table[source].reshape(expert_count, block, model_width)
-    send_inputs = input_table[source // per_token].reshape(expert_count, block, model_width)
-    rows_in, grads_in, full_joined, full_down = forward_exchange(
-        send_inputs, send_grads, w_gate[0], w_up[0], w_down[0], groups, slot_depth, 0
-    )
+    send_rows = jnp.concatenate(
+        [input_table[source // per_token], grad_table[source]], axis=1
+    ).reshape(expert_count, block, 2 * model_width)
+    received, full_joined, full_down = forward_exchange(
+        send_rows, w_gate[0], w_up[0], w_down[0], groups, slot_depth, 0
+    )
+    received = received.reshape(slot_count, 2 * model_width)
+    rows_in = received[:, :model_width]
+    grads_in = received[:, model_width:]
     filled = (jnp.arange(slot_count, dtype=jnp.int32) % block < slot_depth)[:, None]
-    rows_in = jnp.where(filled, rows_in.reshape(slot_count, model_width), 0).astype(tokens.dtype)
-    grads_in = jnp.where(filled, grads_in.reshape(slot_count, model_width), 0).astype(
-        jnp.bfloat16
-    )
+    rows_in = jnp.where(filled, rows_in, 0).astype(tokens.dtype)
+    grads_in = jnp.where(filled, grads_in, 0).astype(jnp.bfloat16)
     preact = jnp.dot(rows_in, full_joined, preferred_element_type=jnp.float32)
     hidden_grad = lax.dot_general(
         grads_in, full_down, (((1,), (1,)), ((), ())), preferred_element_type=jnp.float32

time: 274 us -> 274 us (level)
    reshape x0 -> x1, other arithmetic: none -> 3.92 us  [on_device(): send_rows = jnp.concatenate([input_table[source // per_token], grad_table...]
where the time goes in v8:
time: 274 us
  Pallas kernels  238 us (87%)
  matrix products  15.1 us (6%)
  local copies, waits for them, and re-layouts  14.2 us (5%)
  other arithmetic  5.58 us (2%)
    pallas_call x1, Pallas kernels, forward_exchange(): pl.pallas_call(functools.partial(forward_kernel, n, groups, depth), out_s...  156 us
    pallas_call x1, Pallas kernels, return_and_reduce(): pl.pallas_call(functools.partial(return_kernel, n, groups, depth), out_sh...  81.8 us

profile of v8, /device:TPU:1, one launch (start us, length us, event | category | flops | bytes accessed | tf_op | source)
XLA Modules:
  0.0 273.7 jit_solution(13403256631175419500)
XLA Ops:
  0.6 0.0 copy-start.4
  0.6 1.2 multiply_convert_fusion
  1.9 0.0 copy-done.4
  1.9 0.1 fusion.5
  2.0 0.2 reduce_window_sum.11
  2.2 0.2 select_reduce_fusion
  2.4 1.0 scatter_custom_fusion
  3.4 0.0 copy-start.1
  3.4 2.5 gather_fusion.1
  5.9 0.0 copy-done.1
  5.9 3.3 %gather_fusion = bf16[512,2048]{1,0:T(8,128)(2,1)} fusion(bf16[129,2048]{1,0:T(8,128)(2,1)S(1)} %concatenate.12, s32[1024]{0:T(1024)S(1)} %pad_clamp_fusion.1), kind=kCustom, calls=%fused_computation | custom fusion | bytes 4196352 | tf_op jit(solution)/shard_map/gather | solution.py:375
  9.2 3.9 %maximum_bitcast_fusion.inputs_ref = bf16[64,8,4096]{2,1,0:T(8,128)(2,1)} fusion(bf16[512,2048]{1,0:T(8,128)(2,1)S(1)} %gather_fusion.1, bf16[512,2048]{1,0:T(8,128)(2,1)} %gather_fusion), kind=kLoop, calls=%fused_computation.4 | loop fusion | flops 8388608 | bytes 8388608 | tf_op jit(solution)/shard_map/reshape | solution.py:376
  13.2 156.3 %shard_map.102 = (bf16[64,8,4096]{2,1,0:T(8,128)(2,1)}, bf16[2048,768]{1,0:T(8,128)(2,1)}, bf16[384,2048]{1,0:T(8,128)(2,1)}) custom-call(bf16[64,8,4096]{2,1,0:T(8,128)(2,1)} %maximum_bitcast_fusion.inputs_ref, bf16[256,384]{1,0:T(8,128)(2,1)} %bitcast.25, bf16[256,384]{1,0:T(8,128)(2,1)} %bitcast.26, bf16[384,256]{1,0:T(8,128)(2,1)} %bitcast.27), custom_call_target="tpu_custom_call" | custom-call | tf_op jit(solution)/shard_map/pallas_call | solution.py:126
  169.4 0.0 copy-start.5
  169.4 0.0 copy-start.7
  169.5 4.6 %fusion.2 = f32[512,768]{0,1:T(8,128)S(1)} fusion(bf16[2048,768]{1,0:T(8,128)(2,1)} %get-tuple-element.13, bf16[512,4096]{1,0:T(8,128)(2,1)} %bitcast.33, pred[512]{0:T(512)(128)(4,1)S(1)} %fusion.6), kind=kOutput, calls=%fused_computation.18 | convolution fusion | flops 1611661312 | bytes 6816256 | tf_op jit(solution)/shard_map/dot_general | solution.py:386
  174.0 0.0 copy-done.5
  174.1 0.0 copy-done.7
  174.1 0.0 copy-start.6
  174.1 1.3 multiply_convert_fusion.3
  175.4 0.6 copy-done.6
  176.0 3.2 %fusion.slot_ref = bf16[64,8,2048]{2,1,0:T(8,128)(2,1)} fusion(bf16[2048,768]{1,0:T(8,128)(2,1)S(1)} %copy-done.6, bf16[512,384]{0,1:T(8,128)(2,1)S(1)} %get-tuple-element.19, bf16[512,384]{0,1:T(8,128)(2,1)S(1)} %get-tuple-element.18), kind=kOutput, calls=%fused_computation.8 | convolution fusion | flops 1613234176 | bytes 6029312 | tf_op jit(solution)/shard_map/dot_general | solution.py:400
  179.2 2.3 convolution_convert_fusion.2.part_ref
  181.4 3.7 %convolution_convert_fusion.joined_ref = bf16[2048,768]{1,0:T(8,128)(2,1)} fusion(bf16[512,4096]{1,0:T(8,128)(2,1)S(1)} %bitcast.36, pred[512]{0:T(512)(128)(4,1)S(1)} %fusion.6, bf16[512,384]{0,1:T(8,128)(2,1)S(1)} %get-tuple-element.19, bf16[512,384]{0,1:T(8,128)(2,1)S(1)} %get-tuple-element.18), kind=kOutput, calls=%fused_computation.5 | convolution fusion | flops 1614807040 | bytes 6029824 | tf_op jit(solution)/shard_map/dot_general | solution.py:406
  185.1 81.8 %shard_map.103 = (bf16[64,8,2048]{2,1,0:T(8,128)(2,1)}, bf16[384,2048]{1,0:T(8,128)(2,1)}, bf16[256,384]{1,0:T(8,128)(2,1)}, bf16[256,384]{1,0:T(8,128)(2,1)}) custom-call(bf16[64,8,2048]{2,1,0:T(8,128)(2,1)} %fusion.slot_ref, bf16[384,2048]{1,0:T(8,128)(2,1)} %convolution_convert_fusion.2.part_ref, bf16[2048,768]{1,0:T(8,128)(2,1)} %convolution_convert_fusion.joined_ref), custom_call_target="tpu_custom_call" | custom-call | tf_op jit(solution)/shard_map/pallas_call | solution.py:312
  267.0 0.0 copy-start.3
  267.0 0.0 copy-start.2
  267.0 0.0 copy-start
  267.0 4.2 %gather_fusion.2 = bf16[128,2048]{1,0:T(8,128)(2,1)} fusion(bf16[512,2048]{1,0:T(8,128)(2,1)} %bitcast.23, s32[1024]{0:T(1024)S(1)} %pad_clamp_fusion), kind=kCustom, calls=%fused_computation.2 | custom fusion | bytes 1049088 | tf_op jit(solution)/shard_map/gather | solution.py:417
  271.2 0.0 copy-done.3
  271.2 0.7 copy.17
  271.9 0.0 copy-done.2
  271.9 0.7 copy.18
  272.6 0.0 copy-done
  272.6 1.1 copy.19
  (8 shorter events, 0.1 us)
Async XLA Ops:
  0.6 1.3 copy-start.4
  3.4 2.5 copy-start.1
  169.4 4.6 %copy-start.5 = (bf16[64,8,4096]{2,1,0:T(8,128)(2,1)S(1)}, bf16[64,8,4096]{2,1,0:T(8,128)(2,1)}, u32[]{:S(2)}) copy-start(bf16[64,8,4096]{2,1,0:T(8,128)(2,1)} %get-tuple-element.11) | copy-start | bytes 12582916
  169.4 4.6 %copy-start.7 = (bf16[384,2048]{1,0:T(8,128)(2,1)S(1)}, bf16[384,2048]{1,0:T(8,128)(2,1)}, u32[]{:S(2)}) copy-start(bf16[384,2048]{1,0:T(8,128)(2,1)} %get-tuple-element.12) | copy-start | bytes 4718596
  174.1 1.9 copy-start.6
  267.0 4.3 %copy-start.3 = (bf16[256,384]{1,0:T(8,128)(2,1)S(1)}, bf16[256,384]{1,0:T(8,128)(2,1)}, u32[]{:S(2)}) copy-start(bf16[256,384]{1,0:T(8,128)(2,1)} %get-tuple-element.15) | copy-start | bytes 589828
  267.0 4.9 %copy-start.2 = (bf16[256,384]{1,0:T(8,128)(2,1)S(1)}, bf16[256,384]{1,0:T(8,128)(2,1)}, u32[]{:S(2)}) copy-start(bf16[256,384]{1,0:T(8,128)(2,1)} %get-tuple-element.16) | copy-start | bytes 589828
  267.0 5.6 %copy-start = (bf16[384,2048]{1,0:T(8,128)(2,1)S(1)}, bf16[384,2048]{1,0:T(8,128)(2,1)}, u32[]{:S(2)}) copy-start(bf16[384,2048]{1,0:T(8,128)(2,1)} %get-tuple-element.17) | copy-start | bytes 4718596

commit v9 on v8

--- a/solution.py
+++ b/solution.py
@@ -146,9 +146,10 @@
     )(send_rows, wg, wu, wd)
 
 
-def return_kernel(n, groups, depth, slot_ref, part_ref, joined_ref, out_ref, down_ref, gate_ref, up_ref,
-                  send_sem, recv_sem, local_sem, rs_send, rs_recv, ag_send, ag_recv, js_send,
-                  js_recv, own_sem, parts, reduced, joined_parts, joined_sum):
+def return_kernel(n, groups, depth, slot_ref, act_ref, grads_ref, rows_ref, sides_ref, out_ref,
+                  down_ref, gate_ref, up_ref, send_sem, recv_sem, local_sem, rs_send, rs_recv,
+                  ag_send, ag_recv, js_send, js_recv, own_sem, parts, reduced, joined_parts,
+                  joined_sum, part_ref, joined_ref):
     me = lax.axis_index("expert")
     row = lax.axis_index("dp")
     rows = reduced.shape[0]
@@ -189,6 +190,12 @@
         return carry
 
     lax.fori_loop(1, n, start, 0)
+    part_ref[...] = lax.dot_general(
+        act_ref[...], grads_ref[...], (((0,), (0,)), ((), ())), preferred_element_type=jnp.float32
+    ).astype(part_ref.dtype)
+    joined_ref[...] = lax.dot_general(
+        rows_ref[...], sides_ref[...], (((0,), (0,)), ((), ())), preferred_element_type=jnp.float32
+    ).astype(joined_ref.dtype)
 
     def scatter_copy(other, slot):
         return pltpu.make_async_remote_copy(
@@ -303,21 +310,25 @@
     local.wait()
 
 
-def return_and_reduce(slot_grad, down_part, joined_part, groups, depth, collective_id):
+def return_and_reduce(slot_grad, activated, grads_in, rows_in, both_sides, groups, depth,
+                      collective_id):
     n = slot_grad.shape[0]
-    rows = down_part.shape[0] // groups
-    joined_rows = joined_part.shape[0] // groups
-    width = joined_part.shape[1] // 2
+    hidden = activated.shape[1]
+    width = grads_in.shape[1]
+    joined_width = both_sides.shape[1]
+    rows = hidden // groups
+    joined_rows = width // groups
     any_spec = pl.BlockSpec(memory_space=pl.ANY)
+    vmem_spec = pl.BlockSpec(memory_space=pltpu.VMEM)
     return pl.pallas_call(
         functools.partial(return_kernel, n, groups, depth),
         out_shape=[
             jax.ShapeDtypeStruct(slot_grad.shape, slot_grad.dtype),
-            jax.ShapeDtypeStruct(down_part.shape, down_part.dtype),
-            jax.ShapeDtypeStruct((joined_rows, width), joined_part.dtype),
-            jax.ShapeDtypeStruct((joined_rows, width), joined_part.dtype),
+            jax.ShapeDtypeStruct((hidden, width), grads_in.dtype),
+            jax.ShapeDtypeStruct((joined_rows, joined_width // 2), rows_in.dtype),
+            jax.ShapeDtypeStruct((joined_rows, joined_width // 2), rows_in.dtype),
         ],
-        in_specs=[any_spec] * 3,
+        in_specs=[any_spec] + [vmem_spec] * 4,
         out_specs=[any_spec] * 4,
         scratch_shapes=[
             pltpu.SemaphoreType.DMA((n,)),
@@ -330,15 +341,17 @@
             pltpu.SemaphoreType.DMA((groups,)),
             pltpu.SemaphoreType.DMA((groups,)),
             pltpu.SemaphoreType.DMA((5,)),
-            pltpu.VMEM((groups, rows, down_part.shape[1]), down_part.dtype),
-            pltpu.VMEM((rows, down_part.shape[1]), down_part.dtype),
-            pltpu.VMEM((groups, joined_rows, joined_part.shape[1]), joined_part.dtype),
-            pltpu.VMEM((joined_rows, joined_part.shape[1]), joined_part.dtype),
+            pltpu.VMEM((groups, rows, width), grads_in.dtype),
+            pltpu.VMEM((rows, width), grads_in.dtype),
+            pltpu.VMEM((groups, joined_rows, joined_width), rows_in.dtype),
+            pltpu.VMEM((joined_rows, joined_width), rows_in.dtype),
+            pltpu.VMEM((hidden, width), grads_in.dtype),
+            pltpu.VMEM((width, joined_width), rows_in.dtype),
         ],
         compiler_params=pltpu.CompilerParams(
-            collective_id=collective_id, has_side_effects=True
+            collective_id=collective_id, has_side_effects=True, vmem_limit_bytes=60 * 1024 * 1024
         ),
-    )(slot_grad, down_part, joined_part)
+    )(slot_grad, activated, grads_in, rows_in, both_sides)
 
 
 def on_device(tokens, out_grad, expert_ids, gates, w_gate, w_up, w_down):
@@ -400,16 +413,12 @@
     slot_grad = lax.dot_general(
         both_sides, full_joined, (((1,), (1,)), ((), ())), preferred_element_type=jnp.float32
     ).astype(jnp.bfloat16)
-    down_part = lax.dot_general(
-        activated, grads_in, (((0,), (0,)), ((), ())), preferred_element_type=jnp.float32
-    ).astype(jnp.bfloat16)
-    joined_part = lax.dot_general(
-        rows_in, both_sides, (((0,), (0,)), ((), ())), preferred_element_type=jnp.float32
-    ).astype(jnp.bfloat16)
     returned, down_grad, gate_grad, up_grad = return_and_reduce(
         slot_grad.reshape(expert_count, block, model_width),
-        down_part,
-        joined_part,
+        activated,
+        grads_in,
+        rows_in,
+        both_sides,
         groups,
         slot_depth,
         1,

time: 274 us -> 277 us (1.011)
  matrix products: 15.1 us -> 7.2 us
  other arithmetic: 5.58 us -> 11.2 us
  Pallas kernels: 238 us -> 243 us
    dot_general x2 -> x0, matrix products: 5.97 us -> none  [the longest x1 3.7 us: on_device(): lax.dot_general(rows_in, both_sides, (((0,), (0,)), ((), ())), preferred_...]
    pallas_call x1, Pallas kernels: 81.8 us -> 86.7 us  [return_and_reduce(): pl.pallas_call(functools.partial(return_kernel, n, groups, depth), out_sh...]
    dot_general x1, matrix products: 4.58 us -> 1.79 us  [on_device(): preact = jnp.dot(rows_in, full_joined, preferred_element_type=jnp.float32)]
where the time goes in v9:
time: 277 us
  Pallas kernels  243 us (88%)
  local copies, waits for them, and re-layouts  14.7 us (5%)
  other arithmetic  11.2 us (4%)
  matrix products  7.2 us (3%)
    pallas_call x1, Pallas kernels, forward_exchange(): pl.pallas_call(functools.partial(forward_kernel, n, groups, depth), out_s...  156 us
    pallas_call x1, Pallas kernels, return_and_reduce(): pl.pallas_call(functools.partial(return_kernel, n, groups, depth), out_sh...  86.7 us

profile of v9, /device:TPU:1, one launch (start us, length us, event | category | flops | bytes accessed | tf_op | source)
XLA Modules:
  0.0 276.9 jit_solution(5080584772047704345)
XLA Ops:
  0.6 0.7 fusion.2
  1.4 0.2 reduce_window_sum.11
  1.5 0.8 select_reduce_fusion
  2.4 0.7 fusion.9
  3.0 1.0 scatter_custom_fusion
  4.1 1.2 multiply_convert_fusion
  5.3 0.0 copy-start.3
  5.3 2.5 gather_fusion.1
  7.8 0.0 copy-done.3
  7.9 3.3 %gather_fusion = bf16[512,2048]{1,0:T(8,128)(2,1)} fusion(bf16[129,2048]{1,0:T(8,128)(2,1)S(1)} %concatenate.12, s32[1024]{0:T(1024)S(1)} %pad_clamp_fusion.1), kind=kCustom, calls=%fused_computation | custom fusion | bytes 4196352 | tf_op jit(solution)/shard_map/gather | solution.py:388
  11.2 3.9 %maximum_bitcast_fusion.inputs_ref = bf16[64,8,4096]{2,1,0:T(8,128)(2,1)} fusion(bf16[512,2048]{1,0:T(8,128)(2,1)S(1)} %gather_fusion.1, bf16[512,2048]{1,0:T(8,128)(2,1)} %gather_fusion), kind=kLoop, calls=%fused_computation.4 | loop fusion | flops 8388608 | bytes 8388608 | tf_op jit(solution)/shard_map/reshape | solution.py:389
  15.1 156.3 %shard_map.102 = (bf16[64,8,4096]{2,1,0:T(8,128)(2,1)}, bf16[2048,768]{1,0:T(8,128)(2,1)}, bf16[384,2048]{1,0:T(8,128)(2,1)}) custom-call(bf16[64,8,4096]{2,1,0:T(8,128)(2,1)} %maximum_bitcast_fusion.inputs_ref, bf16[256,384]{1,0:T(8,128)(2,1)} %bitcast.28, bf16[256,384]{1,0:T(8,128)(2,1)} %bitcast.29, bf16[384,256]{1,0:T(8,128)(2,1)} %bitcast.30), custom_call_target="tpu_custom_call" | custom-call | tf_op jit(solution)/shard_map/pallas_call | solution.py:126
  171.4 0.0 copy-start.6
  171.4 2.7 slice_select_fusion
  174.1 0.0 copy-start
  174.1 0.0 copy-start.1
  174.1 0.4 copy-done.6
  174.5 0.0 copy-start.7
  174.5 1.8 fusion.10
  176.3 0.0 copy-done
  176.3 0.0 copy-done.1
  176.3 0.7 copy-done.7
  177.0 2.3 multiply_convert_fusion.3
  179.3 0.9 pad_maximum_fusion.sides_ref
  180.2 3.2 %fusion.slot_ref = bf16[64,8,2048]{2,1,0:T(8,128)(2,1)} fusion(bf16[2048,768]{1,0:T(8,128)(2,1)S(1)} %copy-done.6, bf16[512,384]{1,0:T(8,128)(2,1)S(1)} %get-tuple-element.21, bf16[512,384]{1,0:T(8,128)(2,1)S(1)} %get-tuple-element.20), kind=kOutput, calls=%fused_computation.6 | convolution fusion | flops 1613234176 | bytes 6029312 | tf_op jit(solution)/shard_map/dot_general | solution.py:413
  183.4 86.7 %shard_map.103 = (bf16[64,8,2048]{2,1,0:T(8,128)(2,1)}, bf16[384,2048]{1,0:T(8,128)(2,1)}, bf16[256,384]{1,0:T(8,128)(2,1)}, bf16[256,384]{1,0:T(8,128)(2,1)}) custom-call(bf16[64,8,2048]{2,1,0:T(8,128)(2,1)} %fusion.slot_ref, bf16[512,384]{1,0:T(8,128)(2,1)} %get-tuple-element.22.act_ref, bf16[512,2048]{1,0:T(8,128)(2,1)} %copy-done.1, ...), custom_call_target="tpu_custom_call" | custom-call | tf_op jit(solution)/shard_map/pallas_call | solution.py:323
  270.1 0.0 copy-start.5
  270.1 0.0 copy-start.4
  270.1 0.0 copy-start.2
  270.1 4.2 %gather_fusion.2 = bf16[128,2048]{1,0:T(8,128)(2,1)} fusion(bf16[512,2048]{1,0:T(8,128)(2,1)} %bitcast.25, s32[1024]{0:T(1024)S(1)} %pad_clamp_fusion), kind=kCustom, calls=%fused_computation.2 | custom fusion | bytes 1049088 | tf_op jit(solution)/shard_map/gather | solution.py:426
  274.4 0.0 copy-done.5
  274.4 0.7 copy.17
  275.0 0.0 copy-done.4
  275.0 0.7 copy.18
  275.7 0.0 copy-done.2
  275.7 1.1 copy.19
  (7 shorter events, 0.1 us)
Async XLA Ops:
  5.3 2.5 copy-start.3
  171.4 3.2 %copy-start.6 = (bf16[2048,768]{1,0:T(8,128)(2,1)S(1)}, bf16[2048,768]{1,0:T(8,128)(2,1)}, u32[]{:S(2)}) copy-start(bf16[2048,768]{1,0:T(8,128)(2,1)} %get-tuple-element.13) | copy-start | bytes 9437188
  174.1 2.2 copy-start
  174.1 2.2 copy-start.1
  174.5 2.5 copy-start.7
  270.1 4.3 %copy-start.5 = (bf16[256,384]{1,0:T(8,128)(2,1)S(1)}, bf16[256,384]{1,0:T(8,128)(2,1)}, u32[]{:S(2)}) copy-start(bf16[256,384]{1,0:T(8,128)(2,1)} %get-tuple-element.15) | copy-start | bytes 589828
  270.1 4.9 %copy-start.4 = (bf16[256,384]{1,0:T(8,128)(2,1)S(1)}, bf16[256,384]{1,0:T(8,128)(2,1)}, u32[]{:S(2)}) copy-start(bf16[256,384]{1,0:T(8,128)(2,1)} %get-tuple-element.16) | copy-start | bytes 589828
  270.1 5.6 %copy-start.2 = (bf16[384,2048]{1,0:T(8,128)(2,1)S(1)}, bf16[384,2048]{1,0:T(8,128)(2,1)}, u32[]{:S(2)}) copy-start(bf16[384,2048]{1,0:T(8,128)(2,1)} %get-tuple-element.17) | copy-start | bytes 4718596

commit v10 on v7

--- a/solution.py
+++ b/solution.py
@@ -414,9 +414,14 @@
         slot_depth,
         1,
     )
-    picked = returned.reshape(slot_count, model_width)[slot_of_entry]
-    picked = picked.astype(jnp.float32).reshape(tok_rows, per_token, model_width)
-    input_grad = jnp.sum(picked, axis=1).astype(jnp.bfloat16)
+    owner = (slot_of_entry[:, None] == jnp.arange(slot_count, dtype=jnp.int32)[None, :]).astype(
+        jnp.bfloat16
+    )
+    input_grad = jnp.dot(
+        owner.reshape(tok_rows, per_token, slot_count).sum(axis=1),
+        jnp.where(filled, returned.reshape(slot_count, model_width), 0).astype(jnp.bfloat16),
+        preferred_element_type=jnp.float32,
+    ).astype(jnp.bfloat16)
     return (input_grad, gate_grad[None], up_grad[None], down_grad[None])
 
 

time: 274 us -> 273 us (level)
  local copies, waits for them, and re-layouts: 14.7 us -> 10.5 us
  matrix products: 15 us -> 18.1 us
    gather x1 -> x0, local copies, waits for them, and re-layouts: 4.23 us -> none  [on_device(): picked = returned.reshape(slot_count, model_width)[slot_of_entry]]
    dot_general x0 -> x1, matrix products: none -> 3.06 us  [on_device(): jnp.dot(owner.reshape(tok_rows, per_token, slot_count).sum(axis=1), jnp.w...]
where the time goes in v10:
time: 273 us; the launch traced here: 272 us
  Pallas kernels  239 us (88%)
  matrix products  18.1 us (7%)
  local copies, waits for them, and re-layouts  10.5 us (4%)
  other arithmetic  3.64 us (1%)
    pallas_call x1, Pallas kernels, forward_exchange(): pl.pallas_call(functools.partial(forward_kernel, n, groups, depth), out_s...  157 us
    pallas_call x1, Pallas kernels, return_and_reduce(): pl.pallas_call(functools.partial(return_kernel, n, groups, depth), out_sh...  81.8 us

profile of v10, /device:TPU:1, one launch (start us, length us, event | category | flops | bytes accessed | tf_op | source)
XLA Modules:
  0.0 272.3 jit_solution(18076869279565739176)
XLA Ops:
  0.6 0.7 fusion.12
  1.4 0.2 reduce_window_sum.11
  1.5 0.8 select_reduce_fusion
  2.4 0.7 fusion.32
  3.0 1.0 scatter_custom_fusion
  4.1 1.2 multiply_convert_fusion
  5.3 0.0 copy-start.1
  5.3 3.3 %gather_fusion.1 = bf16[512,2048]{1,0:T(8,128)(2,1)} fusion(bf16[129,2048]{1,0:T(8,128)(2,1)S(1)} %concatenate.10, s32[1024]{0:T(1024)S(1)} %pad_clamp_fusion), kind=kCustom, calls=%fused_computation.1 | custom fusion | bytes 4196352 | tf_op jit(solution)/shard_map/gather | solution.py:376
  8.6 0.0 copy-done.1
  8.7 3.3 %gather_fusion = bf16[512,2048]{1,0:T(8,128)(2,1)} fusion(bf16[129,2048]{1,0:T(8,128)(2,1)S(1)} %concatenate.9, s32[1024]{0:T(1024)S(1)} %pad_clamp_fusion), kind=kCustom, calls=%fused_computation | custom fusion | bytes 4196352 | tf_op jit(solution)/shard_map/gather | solution.py:377
  12.0 157.4 %shard_map.102 = (bf16[64,8,2048]{2,1,0:T(8,128)(2,1)}, bf16[64,8,2048]{2,1,0:T(8,128)(2,1)}, bf16[2048,768]{1,0:T(8,128)(2,1)}, bf16[384,2048]{1,0:T(8,128)(2,1)}) custom-call(bf16[64,8,2048]{2,1,0:T(8,128)(2,1)} %bitcast.42, bf16[64,8,2048]{2,1,0:T(8,128)(2,1)} %bitcast.41, bf16[256,384]{1,0:T(8,128)(2,1)} %bitcast.44, bf16[256,384]{1,0:T(8,128)(2,1)} %bitcast.45, ...), custom_call_target="tpu_custom_call" | custom-call | tf_op jit(solution)/shard_map/pallas_call | solution.py:127
  169.4 0.0 copy-start.5
  169.4 0.0 copy-start.7
  169.4 4.6 %fusion.6 = f32[512,768]{0,1:T(8,128)S(1)} fusion(bf16[2048,768]{1,0:T(8,128)(2,1)} %get-tuple-element.15, bf16[64,8,2048]{2,1,0:T(8,128)(2,1)} %get-tuple-element.14, pred[512]{0:T(512)(128)(4,1)S(1)} %fusion.17), kind=kOutput, calls=%fused_computation.16 | convolution fusion | flops 1611661312 | bytes 6816256 | tf_op jit(solution)/shard_map/dot_general | solution.py:386
  174.0 0.0 copy-done.5
  174.0 0.0 copy-done.7
  174.1 0.0 copy-start.6
  174.1 1.3 multiply_convert_fusion.3
  175.4 0.3 copy-done.6
  175.6 0.0 copy-start.4
  175.6 3.7 %convolution_convert_fusion.joined_ref = bf16[2048,768]{1,0:T(8,128)(2,1)} fusion(bf16[64,8,2048]{2,1,0:T(8,128)(2,1)S(1)} %copy-done.6, pred[512]{0:T(512)(128)(4,1)S(1)} %fusion.17, bf16[512,384]{0,1:T(8,128)(2,1)S(1)} %get-tuple-element.21, bf16[512,384]{0,1:T(8,128)(2,1)S(1)} %get-tuple-element.20), kind=kOutput, calls=%fused_computation.3 | convolution fusion | flops 1614807040 | bytes 6029824 | tf_op jit(solution)/shard_map/dot_general | solution.py:406
  179.4 0.0 copy-done.4
  179.4 3.2 %fusion.slot_ref = bf16[64,8,2048]{2,1,0:T(8,128)(2,1)} fusion(bf16[2048,768]{1,0:T(8,128)(2,1)S(1)} %copy-done.4, bf16[512,384]{0,1:T(8,128)(2,1)S(1)} %get-tuple-element.21, bf16[512,384]{0,1:T(8,128)(2,1)S(1)} %get-tuple-element.20), kind=kOutput, calls=%fused_computation.6 | convolution fusion | flops 1613234176 | bytes 6029312 | tf_op jit(solution)/shard_map/dot_general | solution.py:400
  182.6 2.3 convolution_convert_fusion.2.part_ref
  184.8 81.8 %shard_map.103 = (bf16[64,8,2048]{2,1,0:T(8,128)(2,1)}, bf16[384,2048]{1,0:T(8,128)(2,1)}, bf16[256,384]{1,0:T(8,128)(2,1)}, bf16[256,384]{1,0:T(8,128)(2,1)}) custom-call(bf16[64,8,2048]{2,1,0:T(8,128)(2,1)} %fusion.slot_ref, bf16[384,2048]{1,0:T(8,128)(2,1)} %convolution_convert_fusion.2.part_ref, bf16[2048,768]{1,0:T(8,128)(2,1)} %convolution_convert_fusion.joined_ref), custom_call_target="tpu_custom_call" | custom-call | tf_op jit(solution)/shard_map/pallas_call | solution.py:314
  266.7 0.0 copy-start.3
  266.7 0.0 copy-start.2
  266.7 0.0 copy-start
  266.7 3.1 %convolution_convert_fusion.3 = bf16[128,2048]{1,0:T(8,128)(2,1)} fusion(bf16[64,8,2048]{2,1,0:T(8,128)(2,1)} %get-tuple-element.16, pred[64,8]{1,0:T(8,128)(4,1)S(1)} %fusion.13, s32[128]{0:T(128)S(1)} %get-tuple-element.22), kind=kOutput, calls=%fused_computation.7 | convolution fusion | flops 269811712 | bytes 2622464 | tf_op jit(solution)/shard_map/dot_general | solution.py:420
  269.8 0.0 copy-done.3
  269.8 0.7 copy.19
  270.5 0.0 copy-done.2
  270.5 0.7 copy.20
  271.1 0.0 copy-done
  271.1 1.1 copy.21
  (7 shorter events, 0.1 us)
Async XLA Ops:
  5.3 3.3 %copy-start.1 = (bf16[128,2048]{1,0:T(8,128)(2,1)S(1)}, bf16[128,2048]{1,0:T(8,128)(2,1)}, u32[]{:S(2)}) copy-start(bf16[128,2048]{1,0:T(8,128)(2,1)} %param.7) | copy-start | bytes 1572868
  169.4 4.6 %copy-start.5 = (bf16[64,8,2048]{2,1,0:T(8,128)(2,1)S(1)}, bf16[64,8,2048]{2,1,0:T(8,128)(2,1)}, u32[]{:S(2)}) copy-start(bf16[64,8,2048]{2,1,0:T(8,128)(2,1)} %get-tuple-element.12) | copy-start | bytes 6291460
  169.4 4.6 %copy-start.7 = (bf16[384,2048]{1,0:T(8,128)(2,1)S(1)}, bf16[384,2048]{1,0:T(8,128)(2,1)}, u32[]{:S(2)}) copy-start(bf16[384,2048]{1,0:T(8,128)(2,1)} %get-tuple-element.13) | copy-start | bytes 4718596
  174.1 1.6 copy-start.6
  175.6 3.7 %copy-start.4 = (bf16[2048,768]{1,0:T(8,128)(2,1)S(1)}, bf16[2048,768]{1,0:T(8,128)(2,1)}, u32[]{:S(2)}) copy-start(bf16[2048,768]{1,0:T(8,128)(2,1)} %get-tuple-element.15) | copy-start | bytes 9437188
  266.7 3.1 %copy-start.3 = (bf16[256,384]{1,0:T(8,128)(2,1)S(1)}, bf16[256,384]{1,0:T(8,128)(2,1)}, u32[]{:S(2)}) copy-start(bf16[256,384]{1,0:T(8,128)(2,1)} %get-tuple-element.17) | copy-start | bytes 589828
  266.7 3.8 %copy-start.2 = (bf16[256,384]{1,0:T(8,128)(2,1)S(1)}, bf16[256,384]{1,0:T(8,128)(2,1)}, u32[]{:S(2)}) copy-start(bf16[256,384]{1,0:T(8,128)(2,1)} %get-tuple-element.18) | copy-start | bytes 589828
  266.7 4.4 %copy-start = (bf16[384,2048]{1,0:T(8,128)(2,1)S(1)}, bf16[384,2048]{1,0:T(8,128)(2,1)}, u32[]{:S(2)}) copy-start(bf16[384,2048]{1,0:T(8,128)(2,1)} %get-tuple-element.19) | copy-start | bytes 4718596

commit v11 on v10

--- a/solution.py
+++ b/solution.py
@@ -371,10 +371,16 @@
         .astype(jnp.bfloat16)
         .reshape(entries, model_width)
     )
-    grad_table = jnp.concatenate([entry_scaled, jnp.zeros((1, model_width), jnp.bfloat16)], axis=0)
-    input_table = jnp.concatenate([tokens, jnp.zeros((1, model_width), tokens.dtype)], axis=0)
-    send_grads = grad_table[source].reshape(expert_count, block, model_width)
-    send_inputs = input_table[source // per_token].reshape(expert_count, block, model_width)
+    choose = (source[:, None] == jnp.arange(entries, dtype=jnp.int32)[None, :]).astype(jnp.bfloat16)
+    choose_token = (
+        source[:, None] // per_token == jnp.arange(tok_rows, dtype=jnp.int32)[None, :]
+    ).astype(tokens.dtype)
+    send_grads = jnp.dot(choose, entry_scaled, preferred_element_type=jnp.float32).astype(
+        jnp.bfloat16
+    ).reshape(expert_count, block, model_width)
+    send_inputs = jnp.dot(choose_token, tokens, preferred_element_type=jnp.float32).astype(
+        tokens.dtype
+    ).reshape(expert_count, block, model_width)
     rows_in, grads_in, full_joined, full_down = forward_exchange(
         send_inputs, send_grads, w_gate[0], w_up[0], w_down[0], groups, slot_depth, 0
     )

time: 273 us -> 269 us (0.985)
  local copies, waits for them, and re-layouts: 10.5 us -> 3.78 us
  matrix products: 18.1 us -> 22.4 us
    gather x2 -> x0, local copies, waits for them, and re-layouts: 6.6 us -> none  [the longest x1 3.31 us: on_device(): send_grads = grad_table[source].reshape(expert_count, block, model_width)]
    dot_general x0 -> x2, matrix products: none -> 4.24 us  [the longest x1 2.15 us: on_device(): jnp.dot(choose, entry_scaled, preferred_element_type=jnp.float32)]
where the time goes in v11:
time: 269 us
  Pallas kernels  239 us (89%)
  matrix products  22.4 us (8%)
  local copies, waits for them, and re-layouts  3.78 us (1%)
    pallas_call x1, Pallas kernels, forward_exchange(): pl.pallas_call(functools.partial(forward_kernel, n, groups, depth), out_s...  157 us
    pallas_call x1, Pallas kernels, return_and_reduce(): pl.pallas_call(functools.partial(return_kernel, n, groups, depth), out_sh...  81.9 us

profile of v11, /device:TPU:1, one launch (start us, length us, event | category | flops | bytes accessed | tf_op | source)
XLA Modules:
  0.0 268.7 jit_solution(10703743339568332365)
XLA Ops:
  0.6 0.0 copy-start
  0.6 0.0 copy-start.5
  0.7 0.0 copy-start.2
  0.7 0.8 fusion.17
  1.5 0.2 reduce_window_sum.11
  1.7 0.8 select_reduce_fusion
  2.5 0.7 fusion.37
  3.2 1.0 scatter_custom_fusion
  4.2 0.0 copy-done
  4.2 2.1 fusion.inputs_ref
  6.3 0.0 copy-done.5
  6.3 0.0 copy-done.2
  6.3 2.1 fusion.1.grads_ref
  8.4 157.4 %shard_map.102 = (bf16[64,8,2048]{2,1,0:T(8,128)(2,1)}, bf16[64,8,2048]{2,1,0:T(8,128)(2,1)}, bf16[2048,768]{1,0:T(8,128)(2,1)}, bf16[384,2048]{1,0:T(8,128)(2,1)}) custom-call(bf16[64,8,2048]{2,1,0:T(8,128)(2,1)} %fusion.inputs_ref, bf16[64,8,2048]{2,1,0:T(8,128)(2,1)} %fusion.1.grads_ref, bf16[256,384]{1,0:T(8,128)(2,1)} %bitcast.45, ...), custom_call_target="tpu_custom_call" | custom-call | tf_op jit(solution)/shard_map/pallas_call | solution.py:127
  165.8 0.0 copy-start.7
  165.8 0.0 copy-start.9
  165.9 4.6 %fusion.8 = f32[512,768]{0,1:T(8,128)S(1)} fusion(bf16[2048,768]{1,0:T(8,128)(2,1)} %get-tuple-element.15, bf16[64,8,2048]{2,1,0:T(8,128)(2,1)} %get-tuple-element.14, pred[512]{0:T(512)(128)(4,1)S(1)} %fusion.22), kind=kOutput, calls=%fused_computation.18 | convolution fusion | flops 1611661312 | bytes 6816256 | tf_op jit(solution)/shard_map/dot_general | solution.py:392
  170.4 0.0 copy-done.7
  170.5 0.0 copy-done.9
  170.5 0.0 copy-start.8
  170.5 1.3 multiply_convert_fusion.3
  171.8 0.3 copy-done.8
  172.1 0.0 copy-start.6
  172.1 3.7 %convolution_convert_fusion.joined_ref = bf16[2048,768]{1,0:T(8,128)(2,1)} fusion(bf16[64,8,2048]{2,1,0:T(8,128)(2,1)S(1)} %copy-done.8, pred[512]{0:T(512)(128)(4,1)S(1)} %fusion.22, bf16[512,384]{0,1:T(8,128)(2,1)S(1)} %get-tuple-element.21, bf16[512,384]{0,1:T(8,128)(2,1)S(1)} %get-tuple-element.20), kind=kOutput, calls=%fused_computation.1 | convolution fusion | flops 1614807040 | bytes 6029824 | tf_op jit(solution)/shard_map/dot_general | solution.py:412
  175.8 0.0 copy-done.6
  175.8 3.2 %fusion.2.slot_ref = bf16[64,8,2048]{2,1,0:T(8,128)(2,1)} fusion(bf16[2048,768]{1,0:T(8,128)(2,1)S(1)} %copy-done.6, bf16[512,384]{0,1:T(8,128)(2,1)S(1)} %get-tuple-element.21, bf16[512,384]{0,1:T(8,128)(2,1)S(1)} %get-tuple-element.20), kind=kOutput, calls=%fused_computation.8 | convolution fusion | flops 1613234176 | bytes 6029312 | tf_op jit(solution)/shard_map/dot_general | solution.py:406
  179.0 2.3 convolution_convert_fusion.4.part_ref
  181.3 81.9 %shard_map.103 = (bf16[64,8,2048]{2,1,0:T(8,128)(2,1)}, bf16[384,2048]{1,0:T(8,128)(2,1)}, bf16[256,384]{1,0:T(8,128)(2,1)}, bf16[256,384]{1,0:T(8,128)(2,1)}) custom-call(bf16[64,8,2048]{2,1,0:T(8,128)(2,1)} %fusion.2.slot_ref, bf16[384,2048]{1,0:T(8,128)(2,1)} %convolution_convert_fusion.4.part_ref, bf16[2048,768]{1,0:T(8,128)(2,1)} %convolution_convert_fusion.joined_ref), custom_call_target="tpu_custom_call" | custom-call | tf_op jit(solution)/shard_map/pallas_call | solution.py:314
  263.1 0.0 copy-start.4
  263.2 0.0 copy-start.3
  263.2 0.0 copy-start.1
  263.2 3.1 %convolution_convert_fusion.5 = bf16[128,2048]{1,0:T(8,128)(2,1)} fusion(bf16[64,8,2048]{2,1,0:T(8,128)(2,1)} %get-tuple-element.16, pred[64,8]{1,0:T(8,128)(4,1)S(1)} %fusion.18, s32[128]{0:T(128)S(1)} %get-tuple-element.22), kind=kOutput, calls=%fused_computation.9 | convolution fusion | flops 269811712 | bytes 2622464 | tf_op jit(solution)/shard_map/dot_general | solution.py:426
  266.2 0.0 copy-done.4
  266.2 0.7 copy.19
  266.9 0.0 copy-done.3
  266.9 0.7 copy.20
  267.6 0.0 copy-done.1
  267.6 1.1 copy.21
  (3 shorter events, 0.0 us)
Async XLA Ops:
  0.6 3.5 %copy-start = (bf16[128,2048]{1,0:T(8,128)(2,1)S(1)}, bf16[128,2048]{1,0:T(8,128)(2,1)}, u32[]{:S(2)}) copy-start(bf16[128,2048]{1,0:T(8,128)(2,1)} %param.7) | copy-start | bytes 1572868
  0.6 5.6 %copy-start.5 = (f32[128,1]{0,1:T(1,128)S(1)}, f32[128,1]{0,1:T(1,128)}, u32[]{:S(2)}) copy-start(f32[128,1]{0,1:T(1,128)} %param.10) | copy-start | bytes 1540
  0.7 5.6 %copy-start.2 = (bf16[128,2048]{1,0:T(8,128)(2,1)S(1)}, bf16[128,2048]{1,0:T(8,128)(2,1)}, u32[]{:S(2)}) copy-start(bf16[128,2048]{1,0:T(8,128)(2,1)} %param.8) | copy-start | bytes 1572868
  165.8 4.6 %copy-start.7 = (bf16[64,8,2048]{2,1,0:T(8,128)(2,1)S(1)}, bf16[64,8,2048]{2,1,0:T(8,128)(2,1)}, u32[]{:S(2)}) copy-start(bf16[64,8,2048]{2,1,0:T(8,128)(2,1)} %get-tuple-element.12) | copy-start | bytes 6291460
  165.8 4.6 %copy-start.9 = (bf16[384,2048]{1,0:T(8,128)(2,1)S(1)}, bf16[384,2048]{1,0:T(8,128)(2,1)}, u32[]{:S(2)}) copy-start(bf16[384,2048]{1,0:T(8,128)(2,1)} %get-tuple-element.13) | copy-start | bytes 4718596
  170.5 1.6 copy-start.8
  172.1 3.7 %copy-start.6 = (bf16[2048,768]{1,0:T(8,128)(2,1)S(1)}, bf16[2048,768]{1,0:T(8,128)(2,1)}, u32[]{:S(2)}) copy-start(bf16[2048,768]{1,0:T(8,128)(2,1)} %get-tuple-element.15) | copy-start | bytes 9437188
  263.1 3.1 %copy-start.4 = (bf16[256,384]{1,0:T(8,128)(2,1)S(1)}, bf16[256,384]{1,0:T(8,128)(2,1)}, u32[]{:S(2)}) copy-start(bf16[256,384]{1,0:T(8,128)(2,1)} %get-tuple-element.17) | copy-start | bytes 589828
  263.2 3.8 %copy-start.3 = (bf16[256,384]{1,0:T(8,128)(2,1)S(1)}, bf16[256,384]{1,0:T(8,128)(2,1)}, u32[]{:S(2)}) copy-start(bf16[256,384]{1,0:T(8,128)(2,1)} %get-tuple-element.18) | copy-start | bytes 589828
  263.2 4.4 %copy-start.1 = (bf16[384,2048]{1,0:T(8,128)(2,1)S(1)}, bf16[384,2048]{1,0:T(8,128)(2,1)}, u32[]{:S(2)}) copy-start(bf16[384,2048]{1,0:T(8,128)(2,1)} %get-tuple-element.19) | copy-start | bytes 4718596

commit v12 on v11

--- a/solution.py
+++ b/solution.py
@@ -361,20 +361,15 @@
     before = jnp.cumsum(onehot, axis=0) - onehot
     ranking = jnp.sum(before * onehot, axis=1)
     slot_of_entry = flat_ids * block + ranking
-    source = (
-        jnp.full((slot_count,), entries, jnp.int32)
-        .at[slot_of_entry]
-        .set(jnp.arange(entries, dtype=jnp.int32))
-    )
     entry_scaled = (
         (gates[:, :, None] * out_grad.astype(jnp.float32)[:, None, :])
         .astype(jnp.bfloat16)
         .reshape(entries, model_width)
     )
-    choose = (source[:, None] == jnp.arange(entries, dtype=jnp.int32)[None, :]).astype(jnp.bfloat16)
-    choose_token = (
-        source[:, None] // per_token == jnp.arange(tok_rows, dtype=jnp.int32)[None, :]
-    ).astype(tokens.dtype)
+    choose = (
+        jnp.arange(slot_count, dtype=jnp.int32)[:, None] == slot_of_entry[None, :]
+    ).astype(jnp.bfloat16)
+    choose_token = choose.reshape(slot_count, tok_rows, per_token).sum(axis=2).astype(tokens.dtype)
     send_grads = jnp.dot(choose, entry_scaled, preferred_element_type=jnp.float32).astype(
         jnp.bfloat16
     ).reshape(expert_count, block, model_width)

time: 269 us -> 268 us (level)
  no operation moved by 1% of the time
where the time goes in v12:
time: 268 us
  Pallas kernels  239 us (89%)
  matrix products  22.4 us (8%)
  local copies, waits for them, and re-layouts  2.8 us (1%)
    pallas_call x1, Pallas kernels, forward_exchange(): pl.pallas_call(functools.partial(forward_kernel, n, groups, depth), out_s...  157 us
    pallas_call x1, Pallas kernels, return_and_reduce(): pl.pallas_call(functools.partial(return_kernel, n, groups, depth), out_sh...  82 us

profile of v12, /device:TPU:1, one launch (start us, length us, event | category | flops | bytes accessed | tf_op | source)
XLA Modules:
  0.0 267.9 jit_solution(15809688984325818040)
XLA Ops:
  0.6 0.0 copy-start
  0.6 0.0 copy-start.6
  0.7 0.0 copy-start.2
  0.7 0.8 fusion.17
  1.5 0.2 reduce_window_sum.11
  1.7 0.8 select_reduce_fusion
  2.5 0.7 multiply_add_fusion
  3.2 0.0 copy-done
  3.2 2.0 fusion.inputs_ref
  5.2 0.0 copy-done.6
  5.2 0.0 copy-done.2
  5.2 2.1 fusion.1.grads_ref
  7.4 157.4 %shard_map.102 = (bf16[64,8,2048]{2,1,0:T(8,128)(2,1)}, bf16[64,8,2048]{2,1,0:T(8,128)(2,1)}, bf16[2048,768]{1,0:T(8,128)(2,1)}, bf16[384,2048]{1,0:T(8,128)(2,1)}) custom-call(bf16[64,8,2048]{2,1,0:T(8,128)(2,1)} %fusion.inputs_ref, bf16[64,8,2048]{2,1,0:T(8,128)(2,1)} %fusion.1.grads_ref, bf16[256,384]{1,0:T(8,128)(2,1)} %bitcast.42, ...), custom_call_target="tpu_custom_call" | custom-call | tf_op jit(solution)/shard_map/pallas_call | solution.py:127
  164.8 0.0 copy-start.8
  164.8 0.0 copy-start.10
  164.8 4.6 %fusion.8 = f32[512,768]{0,1:T(8,128)S(1)} fusion(bf16[2048,768]{1,0:T(8,128)(2,1)} %get-tuple-element.15, bf16[64,8,2048]{2,1,0:T(8,128)(2,1)} %get-tuple-element.14, pred[512]{0:T(512)(128)(4,1)S(1)} %fusion.22), kind=kOutput, calls=%fused_computation.17 | convolution fusion | flops 1611661312 | bytes 6816256 | tf_op jit(solution)/shard_map/dot_general | solution.py:387
  169.4 0.0 copy-done.8
  169.4 0.0 copy-done.10
  169.4 0.0 copy-start.9
  169.4 1.3 multiply_convert_fusion.3
  170.8 0.3 copy-done.9
  171.0 0.0 copy-start.7
  171.0 3.8 %convolution_convert_fusion.joined_ref = bf16[2048,768]{1,0:T(8,128)(2,1)} fusion(bf16[64,8,2048]{2,1,0:T(8,128)(2,1)S(1)} %copy-done.9, pred[512]{0:T(512)(128)(4,1)S(1)} %fusion.22, bf16[512,384]{0,1:T(8,128)(2,1)S(1)} %get-tuple-element.21, bf16[512,384]{0,1:T(8,128)(2,1)S(1)} %get-tuple-element.20), kind=kOutput, calls=%fused_computation | convolution fusion | flops 1614807040 | bytes 6029824 | tf_op jit(solution)/shard_map/dot_general | solution.py:407
  174.8 0.0 copy-done.7
  174.8 3.2 %fusion.2.slot_ref = bf16[64,8,2048]{2,1,0:T(8,128)(2,1)} fusion(bf16[2048,768]{1,0:T(8,128)(2,1)S(1)} %copy-done.7, bf16[512,384]{0,1:T(8,128)(2,1)S(1)} %get-tuple-element.21, bf16[512,384]{0,1:T(8,128)(2,1)S(1)} %get-tuple-element.20), kind=kOutput, calls=%fused_computation.7 | convolution fusion | flops 1613234176 | bytes 6029312 | tf_op jit(solution)/shard_map/dot_general | solution.py:401
  178.0 2.3 convolution_convert_fusion.4.part_ref
  180.3 0.0 copy-start.5
  180.3 82.0 %shard_map.103 = (bf16[64,8,2048]{2,1,0:T(8,128)(2,1)}, bf16[384,2048]{1,0:T(8,128)(2,1)}, bf16[256,384]{1,0:T(8,128)(2,1)}, bf16[256,384]{1,0:T(8,128)(2,1)}) custom-call(bf16[64,8,2048]{2,1,0:T(8,128)(2,1)} %fusion.2.slot_ref, bf16[384,2048]{1,0:T(8,128)(2,1)} %convolution_convert_fusion.4.part_ref, bf16[2048,768]{1,0:T(8,128)(2,1)} %convolution_convert_fusion.joined_ref), custom_call_target="tpu_custom_call" | custom-call | tf_op jit(solution)/shard_map/pallas_call | solution.py:314
  262.2 0.0 copy-start.4
  262.3 0.0 copy-done.5
  262.3 0.0 copy-start.3
  262.3 0.0 copy-start.1
  262.3 3.1 %convolution_convert_fusion.5 = bf16[128,2048]{1,0:T(8,128)(2,1)} fusion(bf16[64,8,2048]{2,1,0:T(8,128)(2,1)} %get-tuple-element.16, pred[64,8]{1,0:T(8,128)(4,1)S(1)} %fusion.18, s32[128]{0:T(128)S(1)} %fusion.26), kind=kOutput, calls=%fused_computation.8 | convolution fusion | flops 269811712 | bytes 2622464 | tf_op jit(solution)/shard_map/dot_general | solution.py:421
  265.4 0.0 copy-done.4
  265.4 0.7 copy.19
  266.1 0.0 copy-done.3
  266.1 0.7 copy.20
  266.7 0.0 copy-done.1
  266.7 1.1 copy.21
  (3 shorter events, 0.0 us)
Async XLA Ops:
  0.6 2.5 copy-start
  0.6 4.6 %copy-start.6 = (f32[128,1]{0,1:T(1,128)S(1)}, f32[128,1]{0,1:T(1,128)}, u32[]{:S(2)}) copy-start(f32[128,1]{0,1:T(1,128)} %param.10) | copy-start | bytes 1540
  0.7 4.6 %copy-start.2 = (bf16[128,2048]{1,0:T(8,128)(2,1)S(1)}, bf16[128,2048]{1,0:T(8,128)(2,1)}, u32[]{:S(2)}) copy-start(bf16[128,2048]{1,0:T(8,128)(2,1)} %param.8) | copy-start | bytes 1572868
  164.8 4.6 %copy-start.8 = (bf16[64,8,2048]{2,1,0:T(8,128)(2,1)S(1)}, bf16[64,8,2048]{2,1,0:T(8,128)(2,1)}, u32[]{:S(2)}) copy-start(bf16[64,8,2048]{2,1,0:T(8,128)(2,1)} %get-tuple-element.12) | copy-start | bytes 6291460
  164.8 4.6 %copy-start.10 = (bf16[384,2048]{1,0:T(8,128)(2,1)S(1)}, bf16[384,2048]{1,0:T(8,128)(2,1)}, u32[]{:S(2)}) copy-start(bf16[384,2048]{1,0:T(8,128)(2,1)} %get-tuple-element.13) | copy-start | bytes 4718596
  169.4 1.6 copy-start.9
  171.0 3.8 %copy-start.7 = (bf16[2048,768]{1,0:T(8,128)(2,1)S(1)}, bf16[2048,768]{1,0:T(8,128)(2,1)}, u32[]{:S(2)}) copy-start(bf16[2048,768]{1,0:T(8,128)(2,1)} %get-tuple-element.15) | copy-start | bytes 9437188
  180.3 82.0 %copy-start.5 = (s32[128,1]{0,1:T(1,128)S(1)}, s32[128,1]{0,1:T(1,128)}, u32[]{:S(2)}) copy-start(s32[128,1]{0,1:T(1,128)} %param.9) | copy-start | bytes 1540
  262.2 3.1 %copy-start.4 = (bf16[256,384]{1,0:T(8,128)(2,1)S(1)}, bf16[256,384]{1,0:T(8,128)(2,1)}, u32[]{:S(2)}) copy-start(bf16[256,384]{1,0:T(8,128)(2,1)} %get-tuple-element.17) | copy-start | bytes 589828
  262.3 3.8 %copy-start.3 = (bf16[256,384]{1,0:T(8,128)(2,1)S(1)}, bf16[256,384]{1,0:T(8,128)(2,1)}, u32[]{:S(2)}) copy-start(bf16[256,384]{1,0:T(8,128)(2,1)} %get-tuple-element.18) | copy-start | bytes 589828
  262.3 4.4 %copy-start.1 = (bf16[384,2048]{1,0:T(8,128)(2,1)S(1)}, bf16[384,2048]{1,0:T(8,128)(2,1)}, u32[]{:S(2)}) copy-start(bf16[384,2048]{1,0:T(8,128)(2,1)} %get-tuple-element.19) | copy-start | bytes 4718596

commit v13 on v12

--- a/solution.py
+++ b/solution.py
@@ -355,11 +355,9 @@
     block = 8 * pl.cdiv(slot_depth, 8)
     slot_count = expert_count * block
     flat_ids = expert_ids.reshape(entries)
-    onehot = (flat_ids[:, None] == jnp.arange(expert_count, dtype=jnp.int32)[None, :]).astype(
-        jnp.int32
-    )
-    before = jnp.cumsum(onehot, axis=0) - onehot
-    ranking = jnp.sum(before * onehot, axis=1)
+    order = jnp.arange(entries, dtype=jnp.int32)
+    earlier = (flat_ids[:, None] == flat_ids[None, :]) & (order[:, None] > order[None, :])
+    ranking = jnp.sum(earlier.astype(jnp.int32), axis=1)
     slot_of_entry = flat_ids * block + ranking
     entry_scaled = (
         (gates[:, :, None] * out_grad.astype(jnp.float32)[:, None, :])

time: 268 us -> 267 us (level)
  no operation moved by 1% of the time
where the time goes in v13:
time: 267 us
  Pallas kernels  239 us (90%)
  matrix products  22.2 us (8%)
  local copies, waits for them, and re-layouts  2.82 us (1%)
    pallas_call x1, Pallas kernels, forward_exchange(): pl.pallas_call(functools.partial(forward_kernel, n, groups, depth), out_s...  157 us
    pallas_call x1, Pallas kernels, return_and_reduce(): pl.pallas_call(functools.partial(return_kernel, n, groups, depth), out_sh...  82 us

profile of v13, /device:TPU:1, one launch (start us, length us, event | category | flops | bytes accessed | tf_op | source)
XLA Modules:
  0.0 266.9 jit_solution(11790886568528547988)
XLA Ops:
  0.6 0.0 copy-start
  0.6 0.0 copy-start.5
  0.7 0.0 copy-start.2
  0.7 0.9 convert_reduce_fusion
  1.6 0.7 multiply_add_fusion
  2.3 0.0 copy-done
  2.3 2.0 fusion.inputs_ref
  4.3 0.0 copy-done.5
  4.3 0.0 copy-done.2
  4.3 2.1 fusion.1.grads_ref
  6.5 157.4 %shard_map.102 = (bf16[64,8,2048]{2,1,0:T(8,128)(2,1)}, bf16[64,8,2048]{2,1,0:T(8,128)(2,1)}, bf16[2048,768]{1,0:T(8,128)(2,1)}, bf16[384,2048]{1,0:T(8,128)(2,1)}) custom-call(bf16[64,8,2048]{2,1,0:T(8,128)(2,1)} %fusion.inputs_ref, bf16[64,8,2048]{2,1,0:T(8,128)(2,1)} %fusion.1.grads_ref, bf16[256,384]{1,0:T(8,128)(2,1)} %bitcast.42, ...), custom_call_target="tpu_custom_call" | custom-call | tf_op jit(solution)/shard_map/pallas_call | solution.py:127
  163.9 0.0 copy-start.7
  163.9 0.0 copy-start.9
  163.9 4.6 %fusion.8 = f32[512,768]{0,1:T(8,128)S(1)} fusion(bf16[2048,768]{1,0:T(8,128)(2,1)} %get-tuple-element.15, bf16[64,8,2048]{2,1,0:T(8,128)(2,1)} %get-tuple-element.14, pred[512]{0:T(512)(128)(4,1)S(1)} %fusion.22), kind=kOutput, calls=%fused_computation.17 | convolution fusion | flops 1611661312 | bytes 6816256 | tf_op jit(solution)/shard_map/dot_general | solution.py:385
  168.5 0.0 copy-done.7
  168.5 0.0 copy-done.9
  168.5 0.0 copy-start.8
  168.5 1.3 multiply_convert_fusion.3
  169.8 0.3 copy-done.8
  170.1 0.0 copy-start.6
  170.1 3.7 %convolution_convert_fusion.joined_ref = bf16[2048,768]{1,0:T(8,128)(2,1)} fusion(bf16[64,8,2048]{2,1,0:T(8,128)(2,1)S(1)} %copy-done.8, pred[512]{0:T(512)(128)(4,1)S(1)} %fusion.22, bf16[512,384]{0,1:T(8,128)(2,1)S(1)} %get-tuple-element.21, bf16[512,384]{0,1:T(8,128)(2,1)S(1)} %get-tuple-element.20), kind=kOutput, calls=%fused_computation | convolution fusion | flops 1614807040 | bytes 6029824 | tf_op jit(solution)/shard_map/dot_general | solution.py:405
  173.8 0.0 copy-done.6
  173.8 3.2 %fusion.2.slot_ref = bf16[64,8,2048]{2,1,0:T(8,128)(2,1)} fusion(bf16[2048,768]{1,0:T(8,128)(2,1)S(1)} %copy-done.6, bf16[512,384]{0,1:T(8,128)(2,1)S(1)} %get-tuple-element.21, bf16[512,384]{0,1:T(8,128)(2,1)S(1)} %get-tuple-element.20), kind=kOutput, calls=%fused_computation.7 | convolution fusion | flops 1613234176 | bytes 6029312 | tf_op jit(solution)/shard_map/dot_general | solution.py:399
  177.0 2.2 convolution_convert_fusion.4.part_ref
  179.2 0.0 copy-start.10
  179.2 82.0 %shard_map.103 = (bf16[64,8,2048]{2,1,0:T(8,128)(2,1)}, bf16[384,2048]{1,0:T(8,128)(2,1)}, bf16[256,384]{1,0:T(8,128)(2,1)}, bf16[256,384]{1,0:T(8,128)(2,1)}) custom-call(bf16[64,8,2048]{2,1,0:T(8,128)(2,1)} %fusion.2.slot_ref, bf16[384,2048]{1,0:T(8,128)(2,1)} %convolution_convert_fusion.4.part_ref, bf16[2048,768]{1,0:T(8,128)(2,1)} %convolution_convert_fusion.joined_ref), custom_call_target="tpu_custom_call" | custom-call | tf_op jit(solution)/shard_map/pallas_call | solution.py:314
  261.2 0.0 copy-start.4
  261.2 0.0 copy-done.10
  261.3 0.0 copy-start.3
  261.3 0.0 copy-start.1
  261.3 3.1 %convolution_convert_fusion.5 = bf16[128,2048]{1,0:T(8,128)(2,1)} fusion(bf16[64,8,2048]{2,1,0:T(8,128)(2,1)} %get-tuple-element.16, pred[64,8]{1,0:T(8,128)(4,1)S(1)} %fusion.18, s32[128]{0:T(128)S(1)} %fusion.26), kind=kOutput, calls=%fused_computation.8 | convolution fusion | flops 269811712 | bytes 2622464 | tf_op jit(solution)/shard_map/dot_general | solution.py:419
  264.4 0.0 copy-done.4
  264.4 0.7 copy.21
  265.0 0.0 copy-done.3
  265.0 0.7 copy.22
  265.7 0.0 copy-done.1
  265.7 1.1 copy.23
  (3 shorter events, 0.0 us)
Async XLA Ops:
  0.6 1.6 copy-start
  0.6 3.7 %copy-start.5 = (f32[128,1]{0,1:T(1,128)S(1)}, f32[128,1]{0,1:T(1,128)}, u32[]{:S(2)}) copy-start(f32[128,1]{0,1:T(1,128)} %param.10) | copy-start | bytes 1540
  0.7 3.7 %copy-start.2 = (bf16[128,2048]{1,0:T(8,128)(2,1)S(1)}, bf16[128,2048]{1,0:T(8,128)(2,1)}, u32[]{:S(2)}) copy-start(bf16[128,2048]{1,0:T(8,128)(2,1)} %param.8) | copy-start | bytes 1572868
  163.9 4.6 %copy-start.7 = (bf16[64,8,2048]{2,1,0:T(8,128)(2,1)S(1)}, bf16[64,8,2048]{2,1,0:T(8,128)(2,1)}, u32[]{:S(2)}) copy-start(bf16[64,8,2048]{2,1,0:T(8,128)(2,1)} %get-tuple-element.12) | copy-start | bytes 6291460
  163.9 4.6 %copy-start.9 = (bf16[384,2048]{1,0:T(8,128)(2,1)S(1)}, bf16[384,2048]{1,0:T(8,128)(2,1)}, u32[]{:S(2)}) copy-start(bf16[384,2048]{1,0:T(8,128)(2,1)} %get-tuple-element.13) | copy-start | bytes 4718596
  168.5 1.6 copy-start.8
  170.1 3.7 %copy-start.6 = (bf16[2048,768]{1,0:T(8,128)(2,1)S(1)}, bf16[2048,768]{1,0:T(8,128)(2,1)}, u32[]{:S(2)}) copy-start(bf16[2048,768]{1,0:T(8,128)(2,1)} %get-tuple-element.15) | copy-start | bytes 9437188
  179.2 82.0 %copy-start.10 = (s32[128,1]{0,1:T(1,128)S(1)}, s32[128,1]{0,1:T(1,128)}, u32[]{:S(2)}) copy-start(s32[128,1]{0,1:T(1,128)} %param.9) | copy-start | bytes 1540
  261.2 3.1 %copy-start.4 = (bf16[256,384]{1,0:T(8,128)(2,1)S(1)}, bf16[256,384]{1,0:T(8,128)(2,1)}, u32[]{:S(2)}) copy-start(bf16[256,384]{1,0:T(8,128)(2,1)} %get-tuple-element.17) | copy-start | bytes 589828
  261.3 3.8 %copy-start.3 = (bf16[256,384]{1,0:T(8,128)(2,1)S(1)}, bf16[256,384]{1,0:T(8,128)(2,1)}, u32[]{:S(2)}) copy-start(bf16[256,384]{1,0:T(8,128)(2,1)} %get-tuple-element.18) | copy-start | bytes 589828
  261.3 4.4 %copy-start.1 = (bf16[384,2048]{1,0:T(8,128)(2,1)S(1)}, bf16[384,2048]{1,0:T(8,128)(2,1)}, u32[]{:S(2)}) copy-start(bf16[384,2048]{1,0:T(8,128)(2,1)} %get-tuple-element.19) | copy-start | bytes 4718596

commit v14 on v13

--- a/solution.py
+++ b/solution.py
@@ -413,12 +413,10 @@
         slot_depth,
         1,
     )
-    owner = (slot_of_entry[:, None] == jnp.arange(slot_count, dtype=jnp.int32)[None, :]).astype(
-        jnp.bfloat16
-    )
-    input_grad = jnp.dot(
-        owner.reshape(tok_rows, per_token, slot_count).sum(axis=1),
+    input_grad = lax.dot_general(
+        choose_token,
         jnp.where(filled, returned.reshape(slot_count, model_width), 0).astype(jnp.bfloat16),
+        (((0,), (0,)), ((), ())),
         preferred_element_type=jnp.float32,
     ).astype(jnp.bfloat16)
     return (input_grad, gate_grad[None], up_grad[None], down_grad[None])

time: 267 us -> 267 us (level)
  no operation moved by 1% of the time
where the time goes in v14:
time: 267 us
  Pallas kernels  239 us (90%)
  matrix products  22.3 us (8%)
  local copies, waits for them, and re-layouts  2.8 us (1%)
    pallas_call x1, Pallas kernels, forward_exchange(): pl.pallas_call(functools.partial(forward_kernel, n, groups, depth), out_s...  157 us
    pallas_call x1, Pallas kernels, return_and_reduce(): pl.pallas_call(functools.partial(return_kernel, n, groups, depth), out_sh...  81.8 us

profile of v14, /device:TPU:1, one launch (start us, length us, event | category | flops | bytes accessed | tf_op | source)
XLA Modules:
  0.0 266.7 jit_solution(10248377988176822956)
XLA Ops:
  0.6 0.0 copy-start
  0.6 0.0 copy-start.5
  0.7 0.0 copy-start.2
  0.7 0.9 convert_reduce_fusion
  1.6 0.7 multiply_add_fusion
  2.3 0.0 copy-done
  2.3 2.0 fusion.inputs_ref
  4.3 0.0 copy-done.5
  4.3 0.0 copy-done.2
  4.3 2.1 fusion.1.grads_ref
  6.4 157.4 %shard_map.102 = (bf16[64,8,2048]{2,1,0:T(8,128)(2,1)}, bf16[64,8,2048]{2,1,0:T(8,128)(2,1)}, bf16[2048,768]{1,0:T(8,128)(2,1)}, bf16[384,2048]{1,0:T(8,128)(2,1)}) custom-call(bf16[64,8,2048]{2,1,0:T(8,128)(2,1)} %fusion.inputs_ref, bf16[64,8,2048]{2,1,0:T(8,128)(2,1)} %fusion.1.grads_ref, bf16[256,384]{1,0:T(8,128)(2,1)} %bitcast.33, ...), custom_call_target="tpu_custom_call" | custom-call | tf_op jit(solution)/shard_map/pallas_call | solution.py:127
  163.9 0.0 copy-start.7
  163.9 0.0 copy-start.9
  163.9 4.6 %fusion.8 = f32[512,768]{0,1:T(8,128)S(1)} fusion(bf16[2048,768]{1,0:T(8,128)(2,1)} %get-tuple-element.15, bf16[64,8,2048]{2,1,0:T(8,128)(2,1)} %get-tuple-element.14, pred[512]{0:T(512)(128)(4,1)S(1)} %fusion.20), kind=kOutput, calls=%fused_computation.17 | convolution fusion | flops 1611661312 | bytes 6816256 | tf_op jit(solution)/shard_map/dot_general | solution.py:385
  168.5 0.0 copy-done.7
  168.5 0.0 copy-done.9
  168.5 0.0 copy-start.8
  168.5 1.3 multiply_convert_fusion.3
  169.8 0.3 copy-done.8
  170.1 0.0 copy-start.6
  170.1 3.7 %convolution_convert_fusion.joined_ref = bf16[2048,768]{1,0:T(8,128)(2,1)} fusion(bf16[64,8,2048]{2,1,0:T(8,128)(2,1)S(1)} %copy-done.8, pred[512]{0:T(512)(128)(4,1)S(1)} %fusion.20, bf16[512,384]{0,1:T(8,128)(2,1)S(1)} %get-tuple-element.21, bf16[512,384]{0,1:T(8,128)(2,1)S(1)} %get-tuple-element.20), kind=kOutput, calls=%fused_computation | convolution fusion | flops 1614807040 | bytes 6029824 | tf_op jit(solution)/shard_map/dot_general | solution.py:405
  173.8 0.0 copy-done.6
  173.8 3.2 %fusion.2.slot_ref = bf16[64,8,2048]{2,1,0:T(8,128)(2,1)} fusion(bf16[2048,768]{1,0:T(8,128)(2,1)S(1)} %copy-done.6, bf16[512,384]{0,1:T(8,128)(2,1)S(1)} %get-tuple-element.21, bf16[512,384]{0,1:T(8,128)(2,1)S(1)} %get-tuple-element.20), kind=kOutput, calls=%fused_computation.7 | convolution fusion | flops 1613234176 | bytes 6029312 | tf_op jit(solution)/shard_map/dot_general | solution.py:399
  177.0 2.3 convolution_convert_fusion.4.part_ref
  179.3 81.8 %shard_map.103 = (bf16[64,8,2048]{2,1,0:T(8,128)(2,1)}, bf16[384,2048]{1,0:T(8,128)(2,1)}, bf16[256,384]{1,0:T(8,128)(2,1)}, bf16[256,384]{1,0:T(8,128)(2,1)}) custom-call(bf16[64,8,2048]{2,1,0:T(8,128)(2,1)} %fusion.2.slot_ref, bf16[384,2048]{1,0:T(8,128)(2,1)} %convolution_convert_fusion.4.part_ref, bf16[2048,768]{1,0:T(8,128)(2,1)} %convolution_convert_fusion.joined_ref), custom_call_target="tpu_custom_call" | custom-call | tf_op jit(solution)/shard_map/pallas_call | solution.py:314
  261.1 0.0 copy-start.4
  261.1 0.0 copy-start.3
  261.2 0.0 copy-start.1
  261.2 3.1 %convolution_convert_fusion.5 = bf16[128,2048]{1,0:T(8,128)(2,1)} fusion(bf16[64,8,2048]{2,1,0:T(8,128)(2,1)} %get-tuple-element.16, pred[64,8]{1,0:T(8,128)(4,1)S(1)} %fusion.16, s32[128]{0:T(128)S(1)} %multiply_add_fusion), kind=kOutput, calls=%fused_computation.8 | convolution fusion | flops 269811712 | bytes 2622464 | tf_op jit(solution)/shard_map/dot_general | solution.py:416
  264.2 0.0 copy-done.4
  264.2 0.7 copy.19
  264.9 0.0 copy-done.3
  264.9 0.7 copy.20
  265.6 0.0 copy-done.1
  265.6 1.1 copy.21
  (2 shorter events, 0.0 us)
Async XLA Ops:
  0.6 1.6 copy-start
  0.6 3.7 %copy-start.5 = (f32[128,1]{0,1:T(1,128)S(1)}, f32[128,1]{0,1:T(1,128)}, u32[]{:S(2)}) copy-start(f32[128,1]{0,1:T(1,128)} %param.10) | copy-start | bytes 1540
  0.7 3.6 %copy-start.2 = (bf16[128,2048]{1,0:T(8,128)(2,1)S(1)}, bf16[128,2048]{1,0:T(8,128)(2,1)}, u32[]{:S(2)}) copy-start(bf16[128,2048]{1,0:T(8,128)(2,1)} %param.8) | copy-start | bytes 1572868
  163.9 4.6 %copy-start.7 = (bf16[64,8,2048]{2,1,0:T(8,128)(2,1)S(1)}, bf16[64,8,2048]{2,1,0:T(8,128)(2,1)}, u32[]{:S(2)}) copy-start(bf16[64,8,2048]{2,1,0:T(8,128)(2,1)} %get-tuple-element.12) | copy-start | bytes 6291460
  163.9 4.6 %copy-start.9 = (bf16[384,2048]{1,0:T(8,128)(2,1)S(1)}, bf16[384,2048]{1,0:T(8,128)(2,1)}, u32[]{:S(2)}) copy-start(bf16[384,2048]{1,0:T(8,128)(2,1)} %get-tuple-element.13) | copy-start | bytes 4718596
  168.5 1.6 copy-start.8
  170.1 3.7 %copy-start.6 = (bf16[2048,768]{1,0:T(8,128)(2,1)S(1)}, bf16[2048,768]{1,0:T(8,128)(2,1)}, u32[]{:S(2)}) copy-start(bf16[2048,768]{1,0:T(8,128)(2,1)} %get-tuple-element.15) | copy-start | bytes 9437188
  261.1 3.1 %copy-start.4 = (bf16[256,384]{1,0:T(8,128)(2,1)S(1)}, bf16[256,384]{1,0:T(8,128)(2,1)}, u32[]{:S(2)}) copy-start(bf16[256,384]{1,0:T(8,128)(2,1)} %get-tuple-element.17) | copy-start | bytes 589828
  261.1 3.8 %copy-start.3 = (bf16[256,384]{1,0:T(8,128)(2,1)S(1)}, bf16[256,384]{1,0:T(8,128)(2,1)}, u32[]{:S(2)}) copy-start(bf16[256,384]{1,0:T(8,128)(2,1)} %get-tuple-element.18) | copy-start | bytes 589828
  261.2 4.4 %copy-start.1 = (bf16[384,2048]{1,0:T(8,128)(2,1)S(1)}, bf16[384,2048]{1,0:T(8,128)(2,1)}, u32[]{:S(2)}) copy-start(bf16[384,2048]{1,0:T(8,128)(2,1)} %get-tuple-element.19) | copy-start | bytes 4718596
